TPU v7x, 32 devices: a whole 2x2x4 slice. The times are simulated.
32 devices in a mesh: rows: 8 (over y, x, core), agg: 4 (over z).
Axes of the slice: x: 2, y: 2, z: 4, core: 2. Of those that a mesh axis runs over, the one named last changes fastest.
Arguments:
- load_rhs: bfloat16 [2048, 128, 128], P(('rows', 'agg')), may hold values from -6 to 6
- blocks: bfloat16 [2048, 8, 128, 128], P(('rows', 'agg'))
- columns: int32 [2048, 8], P(('rows', 'agg')), may hold values from 0 to 2047, as said below
- counts: int32 [2048], P(('rows', 'agg')), may hold values from 3 to 8, as said below
- smoother: bfloat16 [2048, 128, 128], P(('rows', 'agg'))
- agg_sizes: int32 [8, 32], P('rows'), may hold values from 1 to 24, 256 in all within a row
- coarse_inv: bfloat16 [256, 128, 128], P(('rows', 'agg'))
Outputs:
- corrected: float32 [2048, 128, 128], P(('rows', 'agg'))
Inputs may be any that keep to these rules, and one draw needn't show every extreme that they name: columns[i, k] lies within 16 of i; slot 0 is i, slot 1 is min(i + 16, 2047), slot 2 is max(i - 16, 0). `counts`: slots 0 to 2 are always live; the first block row of each device has all 8 live. `agg_sizes`: each row sums to 256.
All inputs are finite; a program needn't handle non-finite values.
Results may differ from a plain program's by a relative error of at most 0.0044.
Values may be sent and summed in bfloat16 or wider, within the bound.
No kernel may reach another device: no remote copies, remote signals or barrier semaphores. Data moves between devices by JAX's collectives and lax.ppermute only.
A program may use at most 192 MiB of HBM per device.

v0:
```python
import jax
import jax.numpy as jnp
from jax import lax
from jax.experimental import pallas as pl
from jax.experimental.pallas import tpu as pltpu
from jax.sharding import PartitionSpec as P

HALO = 16

relax_fine = 0.8
relax_coarse = 1.0

AXES = ("rows", "agg")
F32 = jnp.float32
BF16 = jnp.bfloat16
I32 = jnp.int32
MIB = 1024 * 1024
WEIGHT = 32

SMEM = pl.BlockSpec(memory_space=pltpu.SMEM)
VM = pl.BlockSpec(memory_space=pltpu.VMEM)
ANY = pl.BlockSpec(memory_space=pl.ANY)
HBM = pl.BlockSpec(memory_space=pltpu.HBM)


def mm(a, b):
    return jnp.dot(a, b, preferred_element_type=F32)


def cost(flops, nbytes):
    return pl.CostEstimate(flops=WEIGHT * flops, bytes_accessed=nbytes, transcendentals=0)


def params(mib):
    return pltpu.CompilerParams(vmem_limit_bytes=mib * MIB)


def near(x):
    return pltpu.with_memory_space_constraint(x, pltpu.VMEM)


def far(x):
    return pltpu.with_memory_space_constraint(x, pltpu.HBM)


class Sizes:
    def __init__(self, rows, slots, bs, n, aggs, group):
        self.R, self.K, self.BS, self.N, self.A, self.G = rows, slots, bs, n, aggs, group
        self.H = HALO


def edge_smooth(p, rhs, smoother):
    step = 8
    starts = [0, step, p.R - p.H, p.R - p.H + step]

    def kernel(b_hbm, s_hbm, lo_ref, hi_ref, b, s, sems):
        copies = []
        for c, at in enumerate(starts):
            copies.append(pltpu.make_async_copy(b_hbm.at[pl.ds(at, step)], b.at[c], sems.at[0, c]))
            copies.append(pltpu.make_async_copy(s_hbm.at[pl.ds(at, step)], s.at[c], sems.at[1, c]))
        for c in copies:
            c.start()
        for c in range(len(starts)):
            copies[2 * c].wait()
            copies[2 * c + 1].wait()
            out = lo_ref if c < 2 else hi_ref
            for r in range(step):
                out[(c % 2) * step + r] = (relax_fine * mm(s[c, r], b[c, r])).astype(BF16)

    out = jax.ShapeDtypeStruct((p.H, p.BS, p.N), BF16)
    return pl.pallas_call(
        kernel,
        in_specs=[HBM, HBM],
        out_specs=[VM, VM],
        out_shape=[out, out],
        scratch_shapes=[
            pltpu.VMEM((4, step, p.BS, p.N), BF16),
            pltpu.VMEM((4, step, p.BS, p.BS), BF16),
            pltpu.SemaphoreType.DMA((2, 4)),
        ],
        compiler_params=params(8),
        cost_estimate=cost(4 * p.H * p.BS * p.BS * p.N, 6 * p.H * p.BS * p.N),
        name="edge_smooth",
    )(far(rhs), far(smoother))


def row_product(p, blk, i, ext, lcol):
    lhs = jnp.concatenate([blk[i, k] for k in range(p.K)], axis=1)
    rhs = jnp.concatenate([ext[lcol[k, i]] for k in range(p.K)], axis=0)
    return mm(lhs, rhs)


def inner_first(p, pos, cols, counts, sizes, rhs, smoother, blocks, next_inverse):
    piece = 8
    pieces = p.R // piece

    def kernel(
        pos_ref, col_ref, cnt_ref, size_ref, b_hbm, sm_hbm, blk_hbm, inv_hbm,
        b, sm, blk, s2, ext2, acc, lcol, hslot, hcol, hn, bounds, trims, ext, lists, sems, list_sems,
    ):
        start, here = pos_ref[0], pos_ref[1]
        small = [
            pltpu.make_async_copy(src.at[pl.ds(c * piece, piece)], dst.at[pl.ds(c * piece, piece)], sems.at[j, c])
            for c in range(pieces)
            for j, (src, dst) in enumerate(((b_hbm, b), (sm_hbm, sm)))
        ]

        def block_copy(c):
            at = pl.ds(c * piece, piece)
            return pltpu.make_async_copy(blk_hbm.at[at], blk.at[at], sems.at[2, c])

        for c in small:
            c.start()
        inner_pieces = range(p.H // piece, pieces - p.H // piece)
        end_pieces = [c for c in range(pieces) if c not in inner_pieces]
        for c in [*inner_pieces, *end_pieces]:
            block_copy(c).start()
        ext[p.R] = jnp.zeros((p.BS, p.N), BF16)
        ext2[p.R] = jnp.zeros((p.BS, p.N), BF16)

        cols = col_ref[...] - start
        ks = lax.broadcasted_iota(I32, (p.K, p.R), 0)
        live = ks < cnt_ref[...]
        inside = jnp.logical_and(cols >= 0, cols < p.R)
        lists[0] = jnp.where(jnp.logical_and(live, inside), cols, p.R)
        outside = jnp.where(jnp.logical_and(live, jnp.logical_not(inside)), 1, 0)
        place = jnp.where(cols < 0, cols + p.H, cols - p.R + p.H)
        count = jnp.zeros((1, p.R), I32)
        slot_rows = [jnp.zeros((1, p.R), I32)] * p.K
        col_rows = [jnp.full((1, p.R), 2 * p.H, I32)] * p.K
        for k in range(p.K):
            out = outside[k:k + 1]
            for j in range(k + 1):
                mine = jnp.logical_and(out > 0, count == j)
                slot_rows[j] = jnp.where(mine, k, slot_rows[j])
                col_rows[j] = jnp.where(mine, place[k:k + 1], col_rows[j])
            count = count + out
        lists[1] = jnp.concatenate(slot_rows, axis=0)
        lists[2] = jnp.concatenate(col_rows, axis=0)
        lists[3] = jnp.broadcast_to(count, (p.K, p.R))
        list_copies = [
            pltpu.make_async_copy(lists.at[j], dst, list_sems.at[j]) for j, dst in enumerate((lcol, hslot, hcol, hn))
        ]
        for c in list_copies:
            c.start()

        def smooth_row(r, c):
            v = relax_fine * mm(sm[r], b[r])
            s2[r] = v
            ext[r] = v.astype(BF16)
            return c

        for c in range(pieces):
            small[2 * c].wait()
            small[2 * c + 1].wait()
            lax.fori_loop(c * piece, (c + 1) * piece, smooth_row, 0, unroll=8)

        def inner_row(i, c):
            res = b[i].astype(F32) - row_product(p, blk, i, ext, lcol)
            v = s2[i] + relax_fine * mm(sm[i], res.astype(BF16))
            s2[i] = v
            ext2[i] = v.astype(BF16)
            return c

        for c in list_copies:
            c.wait()
        for c in inner_pieces:
            block_copy(c).wait()
            lax.fori_loop(c * piece, (c + 1) * piece, inner_row, 0, unroll=4)

        def edge_row(r, c):
            i = jnp.where(r < p.H, r, r + p.R - 2 * p.H)
            acc[r] = b[i].astype(F32) - row_product(p, blk, i, ext, lcol)
            return c

        for j, c in enumerate(end_pieces):
            block_copy(c).wait()
            lax.fori_loop(j * piece, (j + 1) * piece, edge_row, 0, unroll=4)

        bounds[0] = 0

        def agg(a, t):
            end, first, last, before, after, lowest, highest = t
            begin = end
            end = end + size_ref[0, a]
            bounds[a + 1] = jnp.clip(end, 0, p.R)
            leads = jnp.logical_and(begin <= 0, end > 0)
            ends = jnp.logical_and(begin < p.R, end >= p.R)
            first = jnp.where(leads, end, first)
            last = jnp.where(ends, begin, last)
            lowest = jnp.where(leads, a, lowest)
            highest = jnp.where(ends, a, highest)
            before = jnp.where(jnp.logical_and(begin < 0, end > 0), 1, before)
            after = jnp.where(jnp.logical_and(begin < p.R, end > p.R), 1, after)
            return end, first, last, before, after, lowest, highest

        zero = jnp.int32(0)
        _, first, last, before, after, lowest, highest = lax.fori_loop(0, p.A, agg, (-here * p.R,) + (zero,) * 6)
        trims[0] = jnp.clip(first, 0, p.R)
        trims[1] = jnp.clip(last, 0, p.R)
        trims[2] = before
        trims[3] = after
        trims[4] = lowest
        trims[5] = highest

    ints = lambda n: jax.ShapeDtypeStruct((n,), I32)
    return pl.pallas_call(
        kernel,
        in_specs=[SMEM, VM, VM, SMEM] + [HBM] * 3 + [ANY],
        out_specs=[VM] * 6 + [SMEM] * 6,
        out_shape=[
            pltpu.VMEM(rhs.shape, BF16),
            pltpu.VMEM(smoother.shape, BF16),
            pltpu.VMEM(blocks.shape, BF16),
            pltpu.VMEM((p.R, p.BS, p.N), F32),
            pltpu.VMEM((p.R + 1, p.BS, p.N), BF16),
            pltpu.VMEM((2 * p.H, p.BS, p.N), F32),
            *[jax.ShapeDtypeStruct((p.K, p.R), I32)] * 4,
            ints(p.A + 1),
            ints(6),
        ],
        scratch_shapes=[
            pltpu.VMEM((p.R + 1, p.BS, p.N), BF16),
            pltpu.VMEM((4, p.K, p.R), I32),
            pltpu.SemaphoreType.DMA((3, pieces)),
            pltpu.SemaphoreType.DMA((4,)),
        ],
        compiler_params=params(8),
        cost_estimate=cost(2 * p.R * p.K * p.BS * p.BS * p.N, 2 * p.R * p.K * p.BS * p.BS),
        name="inner_first",
    )(pos, cols, counts, sizes, far(rhs), far(smoother), far(blocks), next_inverse)


GROUP = 4
WIDE = 4


def end_row(p, r):
    return jnp.where(r < p.H, r, r + p.R - 2 * p.H)


def halo_product(hslot, hcol, blk, i, slots, halo):
    lhs = jnp.concatenate([blk[i, hslot[j, i]] for j in slots], axis=1)
    rhs = jnp.concatenate([halo[hcol[j, i]] for j in slots], axis=0)
    return mm(lhs, rhs)


def take_rest(p, hslot, hcol, hn, blk, halo, acc):
    def row(r, c):
        i = end_row(p, r)

        @pl.when(hn[0, i] > WIDE)
        def _():
            acc[r] = acc[r] - halo_product(hslot, hcol, blk, i, range(WIDE, p.K), halo)

        return c

    lax.fori_loop(0, 2 * p.H, row, 0)


def fill_halo(p, before, after, halo):
    halo[:p.H] = before[...]
    halo[p.H:2 * p.H] = after[...]
    halo[2 * p.H] = jnp.zeros((p.BS, p.N), BF16)


def edge_second(p, hslot, hcol, hn, before, after, acc, smoother, blocks, s2, ext2):
    def kernel(hs, hc, hn_ref, bef, aft, acc_in, sm, blk, s2_in, ext_in, s2_out, ext_out, acc_ref, lo, hi, halo, res):
        fill_halo(p, bef, aft, halo)
        take_rest(p, hs, hc, hn_ref, blk, halo, acc_ref)

        def residual(r, c):
            i = end_row(p, r)
            res[r] = (acc_ref[r] - halo_product(hs, hc, blk, i, range(WIDE), halo)).astype(BF16)
            return c

        lax.fori_loop(0, 2 * p.H, residual, 0, unroll=8)

        def sweep(out, r0, i0):
            for g in range(0, p.H, GROUP):
                rows = range(g, g + GROUP)
                new = [s2_in[i0 + r] + relax_fine * mm(sm[i0 + r], res[r0 + r]) for r in rows]
                for r, v in zip(rows, new):
                    s2_out[i0 + r] = v
                    out[r] = v.astype(BF16)
                    ext_out[i0 + r] = v.astype(BF16)

        sweep(lo, 0, 0)
        sweep(hi, p.H, p.R - p.H)

    out = jax.ShapeDtypeStruct((p.H, p.BS, p.N), BF16)
    return pl.pallas_call(
        kernel,
        in_specs=[SMEM] * 3 + [VM] * 7,
        out_specs=[VM] * 5,
        out_shape=[
            pltpu.VMEM((p.R, p.BS, p.N), F32),
            pltpu.VMEM((p.R + 1, p.BS, p.N), BF16),
            pltpu.VMEM((2 * p.H, p.BS, p.N), F32),
            out,
            out,
        ],
        input_output_aliases={8: 0, 9: 1, 5: 2},
        scratch_shapes=[
            pltpu.VMEM((2 * p.H + 1, p.BS, p.N), BF16),
            pltpu.VMEM((2 * p.H, p.BS, p.N), BF16),
        ],
        compiler_params=params(8),
        cost_estimate=cost(8 * p.H * p.BS * p.BS * p.N, 4 * p.H * p.K * p.BS * p.BS),
        name="edge_second",
    )(hslot, hcol, hn, near(before), near(after), near(acc), near(smoother), near(blocks), near(s2), near(ext2))


def aggregate_sum(p, resid, first, last):
    return lax.fori_loop(
        first, last, lambda r, t: t + resid[r].astype(F32), jnp.zeros((p.BS, p.N), F32)
    )


class Rows:
    def __init__(self, fixed, out, sems):
        self.fixed, self.out, self.sems = fixed, out, sems

    def copy(self, r):
        return pltpu.make_async_copy(self.fixed.at[r], self.out.at[r], self.sems.at[r])

    def add(self, p, inverse, res, s2, first, last):
        fix = (relax_coarse * mm(inverse, res)).astype(BF16).astype(F32)

        def row(r, c):
            self.fixed[r] = s2[r] + fix
            self.copy(r).start()
            return c

        lax.fori_loop(first, last, row, 0)

    def wait(self, first, last):
        def row(r, c):
            self.copy(r).wait()
            return c

        lax.fori_loop(first, last, row, 0)


def inner_aggregate(p, first, last):
    return jnp.logical_and(first >= p.H, last <= p.R - p.H)


def fix_aggregates(p, bounds, rows, inv, r2, s2, wanted):
    def chosen(a):
        return jnp.logical_and(bounds[a] < bounds[a + 1], wanted(bounds[a], bounds[a + 1]))

    def one(a, c):
        @pl.when(chosen(a))
        def _():
            res = aggregate_sum(p, r2, bounds[a], bounds[a + 1]).astype(BF16)
            rows.add(p, inv[a], res, s2, bounds[a], bounds[a + 1])

        return c

    lax.fori_loop(0, p.A, one, 0)

    def wait():
        def done(a, c):
            pl.when(chosen(a))(lambda: rows.wait(bounds[a], bounds[a + 1]))
            return c

        lax.fori_loop(0, p.A, done, 0)

    return wait


def rows_scratch(p):
    return [pltpu.VMEM((p.R, p.BS, p.N), F32), pltpu.SemaphoreType.DMA((p.R,))]


def inner_residual(p, pos, lcol, bounds, rhs, blocks, ext2, s2, inverses):
    share = p.A // p.G

    def kernel(pos_ref, lcol_ref, bd, ext, b, blk, s2_ref, *rest):
        inv_refs, (r2, acc, inv, out, fixed, row_sems, sems) = rest[:p.G], rest[p.G:]
        copies = []
        for t in range(p.G):
            place = lax.rem(pos_ref[1] - t + p.G, p.G) * share
            copies.append(pltpu.make_async_copy(inv_refs[t], inv.at[pl.ds(place, share)], sems.at[t]))
        for c in copies:
            c.start()

        def inner_row(i, c):
            r2[i] = (b[i].astype(F32) - row_product(p, blk, i, ext, lcol_ref)).astype(BF16)
            return c

        lax.fori_loop(p.H, p.R - p.H, inner_row, 0, unroll=4)
        for c in copies:
            c.wait()
        rows = Rows(fixed, out, row_sems)
        wait = fix_aggregates(p, bd, rows, inv, r2, s2_ref, lambda first, last: inner_aggregate(p, first, last))

        def edge_row(r, c):
            i = end_row(p, r)
            acc[r] = b[i].astype(F32) - row_product(p, blk, i, ext, lcol_ref)
            return c

        lax.fori_loop(0, 2 * p.H, edge_row, 0, unroll=4)
        wait()

    return pl.pallas_call(
        kernel,
        in_specs=[SMEM] * 3 + [VM] * 4 + [ANY] * p.G,
        out_specs=[VM] * 3 + [HBM],
        out_shape=[
            pltpu.VMEM((p.R, p.BS, p.N), BF16),
            pltpu.VMEM((2 * p.H, p.BS, p.N), F32),
            pltpu.VMEM((p.A, p.BS, p.BS), BF16),
            jax.ShapeDtypeStruct((p.R, p.BS, p.N), F32),
        ],
        scratch_shapes=rows_scratch(p) + [pltpu.SemaphoreType.DMA((p.G,))],
        compiler_params=params(8),
        cost_estimate=cost(2 * p.R * p.K * p.BS * p.BS * p.N, 2 * p.R * p.K * p.BS * p.BS),
        name="inner_residual",
    )(pos, lcol, bounds, near(ext2), near(rhs), near(blocks), near(s2), *inverses)


def edge_final(p, hslot, hcol, hn, trims, before, after, acc, blocks, r2):
    def kernel(hs, hc, hn_ref, trim, bef, aft, acc_in, blk, r2_in, r2_out, acc_ref, part_first, part_last, halo):
        fill_halo(p, bef, aft, halo)
        take_rest(p, hs, hc, hn_ref, blk, halo, acc_ref)

        def row(r, c):
            i = end_row(p, r)
            r2_out[i] = (acc_ref[r] - halo_product(hs, hc, blk, i, range(WIDE), halo)).astype(BF16)
            return c

        lax.fori_loop(0, 2 * p.H, row, 0, unroll=8)
        part_first[...] = aggregate_sum(p, r2_out, 0, trim[0]).astype(BF16)
        part_last[...] = aggregate_sum(p, r2_out, trim[1], p.R).astype(BF16)

    one = jax.ShapeDtypeStruct((p.BS, p.N), BF16)
    return pl.pallas_call(
        kernel,
        in_specs=[SMEM] * 4 + [VM] * 5,
        out_specs=[VM] * 4,
        out_shape=[
            pltpu.VMEM((p.R, p.BS, p.N), BF16),
            pltpu.VMEM((2 * p.H, p.BS, p.N), F32),
            one,
            one,
        ],
        input_output_aliases={8: 0, 6: 1},
        scratch_shapes=[pltpu.VMEM((2 * p.H + 1, p.BS, p.N), BF16)],
        compiler_params=params(8),
        cost_estimate=cost(4 * p.H * p.BS * p.BS * p.N, 4 * p.H * p.K * p.BS * p.BS),
        name="edge_final",
    )(hslot, hcol, hn, trims, near(before), near(after), near(acc), near(blocks), near(r2))


def coarse_own(p, bounds, trims, r2, s2, inv, out):
    def kernel(bd, trim, r2_ref, s2_ref, inv_ref, out_in, out_ref, fixed, row_sems):
        rows = Rows(fixed, out_ref, row_sems)

        def wanted(first, last):
            split = jnp.logical_or(
                jnp.logical_and(first == 0, trim[2] > 0), jnp.logical_and(last == p.R, trim[3] > 0)
            )
            return jnp.logical_not(jnp.logical_or(split, inner_aggregate(p, first, last)))

        fix_aggregates(p, bd, rows, inv_ref, r2_ref, s2_ref, wanted)()

    return pl.pallas_call(
        kernel,
        in_specs=[SMEM] * 2 + [VM] * 3 + [HBM],
        out_specs=HBM,
        out_shape=jax.ShapeDtypeStruct((p.R, p.BS, p.N), F32),
        input_output_aliases={5: 0},
        scratch_shapes=rows_scratch(p),
        compiler_params=params(8),
        cost_estimate=cost(p.A * p.BS * p.BS * p.N, 5 * p.R * p.BS * p.N),
        name="coarse_own",
    )(bounds, trims, near(r2), near(s2), near(inv), out)


def coarse_split(p, bounds, trims, part_first, part_last, from_before, from_after, s2, inv, out):
    def kernel(bd, trim, first_ref, last_ref, bef, aft, s2_ref, inv_ref, out_in, out_ref, fixed, row_sems):
        rows = Rows(fixed, out_ref, row_sems)

        @pl.when(trim[2] > 0)
        def _():
            res = (bef[...].astype(F32) + first_ref[...].astype(F32)).astype(BF16)
            rows.add(p, inv_ref[trim[4]], res, s2_ref, 0, trim[0])

        @pl.when(trim[3] > 0)
        def _():
            res = (last_ref[...].astype(F32) + aft[...].astype(F32)).astype(BF16)
            rows.add(p, inv_ref[trim[5]], res, s2_ref, trim[1], p.R)

        pl.when(trim[2] > 0)(lambda: rows.wait(0, trim[0]))
        pl.when(trim[3] > 0)(lambda: rows.wait(trim[1], p.R))

    return pl.pallas_call(
        kernel,
        in_specs=[SMEM] * 2 + [VM] * 6 + [HBM],
        out_specs=HBM,
        out_shape=jax.ShapeDtypeStruct((p.R, p.BS, p.N), F32),
        input_output_aliases={8: 0},
        scratch_shapes=rows_scratch(p),
        compiler_params=params(8),
        cost_estimate=cost(4 * p.BS * p.BS * p.N, p.R * p.BS * p.N),
        name="coarse_split",
    )(
        bounds, trims, near(part_first), near(part_last), near(from_before), near(from_after), near(s2), near(inv), out
    )


def shift(value, axis, up):
    size = lax.axis_size(axis)
    pairs = [(i, i + 1) for i in range(size - 1)]
    return lax.ppermute(value, axis, pairs if up else [(j, i) for i, j in pairs])


def body(load_rhs, blocks, columns, counts, smoother, agg_sizes, coarse_inv):
    rows, bs, n = load_rhs.shape
    group = lax.axis_size("agg")
    p = Sizes(rows, blocks.shape[1], bs, n, agg_sizes.shape[1], group)
    here = lax.axis_index("agg")
    pos = jnp.stack([lax.axis_index(AXES) * rows, here]).astype(I32)

    lo1, hi1 = edge_smooth(p, load_rhs, smoother)
    before1, after1 = shift(hi1, AXES, True), shift(lo1, AXES, False)
    turn = lambda v, t: lax.ppermute(v, "agg", [(i, (i + t) % group) for i in range(group)])
    inverses = [coarse_inv, turn(coarse_inv, 1)]
    rhs, smoother, blocks, s2, ext2, acc1, lcol, hslot, hcol, hn, bounds, trims = inner_first(
        p, pos, columns.T, counts[None, :], agg_sizes, load_rhs, smoother, blocks, inverses[1]
    )
    late, hn = lax.optimization_barrier((coarse_inv, hn))
    inverses += [turn(late, t) for t in range(2, group)]

    s2, ext2, _, lo2, hi2 = edge_second(p, hslot, hcol, hn, before1, after1, acc1, smoother, blocks, s2, ext2)
    before2, after2 = shift(hi2, AXES, True), shift(lo2, AXES, False)
    r2, acc2, inv, out = inner_residual(p, pos, lcol, bounds, rhs, blocks, ext2, s2, inverses)
    r2, _, part_first, part_last = edge_final(p, hslot, hcol, hn, trims, before2, after2, acc2, blocks, r2)
    from_before, from_after = shift(part_last, "agg", True), shift(part_first, "agg", False)
    out = coarse_own(p, bounds, trims, r2, s2, inv, out)
    return coarse_split(p, bounds, trims, part_first, part_last, from_before, from_after, s2, inv, out)


def solution(mesh):
    placed = (
        P(AXES, None, None),
        P(AXES, None, None, None),
        P(AXES, None),
        P(AXES),
        P(AXES, None, None),
        P("rows", None),
        P(AXES, None, None),
    )
    return jax.shard_map(
        body, mesh=mesh, in_specs=placed, out_specs=P(AXES, None, None), check_vma=False
    )
```

profile of v0, /device:TPU:0, one launch (start us, length us, event | category | flops | bytes accessed | tf_op | source)
XLA Modules:
  0.0 87.9 jit_solution(8427553932162115917)
XLA Ops:
  0.0 0.0 copy-start.3
  0.0 0.0 copy-start.2
  0.0 0.0 copy-start.1
  0.0 3.1 %collective-permute-start = (bf16[8,128,128]{2,1,0:T(8,128)(2,1)}, bf16[8,128,128]{2,1,0:T(8,128)(2,1)S(1)}, u32[]{:S(2)}, u32[]{:S(2)}) collective-permute-start(bf16[8,128,128]{2,1,0:T(8,128)(2,1)} %rest_0_.1), channel_id=1, source_target_pairs={{0,1},{1,2},{2,3},{3,0},{4,5},{5,6},{6,7},{7,4},{8,9},{9,10},{10,1... | collective-permute-start | bytes 786440 | tf_op jit(solution)/shard_map/ppermute | solution.py:529
  3.1 2.0 %edge_smooth.1 = (bf16[16,128,128]{2,1,0:T(8,128)(2,1)S(1)}, bf16[16,128,128]{2,1,0:T(8,128)(2,1)S(1)}) custom-call(bf16[64,128,128]{2,1,0:T(8,128)(2,1)} %b_hbm.3, bf16[64,128,128]{2,1,0:T(8,128)(2,1)} %s_hbm.1), custom_call_target="tpu_custom_call" | custom-call | flops 4294967296 | bytes 1572864 | tf_op jit(solution)/shard_map/edge_smooth/pallas_call | solution.py:71
  5.1 3.5 %collective-permute-start.1 = (bf16[16,128,128]{2,1,0:T(8,128)(2,1)S(1)}, bf16[16,128,128]{2,1,0:T(8,128)(2,1)S(1)}, u32[]{:S(2)}, u32[]{:S(2)}) collective-permute-start(bf16[16,128,128]{2,1,0:T(8,128)(2,1)S(1)} %get-tuple-element.38), channel_id=1, source_target_pairs={{0,1},{1,2},{2,3},{3,4},{4,5},{5,6},{6,7},{7,8},{8,9},{9,10},{10,1... | collective-permute-start | bytes 1572872 | tf_op jit(solution)/shard_map/ppermute | solution.py:517
  8.6 1.3 %collective-permute-start.2 = (bf16[16,128,128]{2,1,0:T(8,128)(2,1)S(1)}, bf16[16,128,128]{2,1,0:T(8,128)(2,1)S(1)}, u32[]{:S(2)}, u32[]{:S(2)}) collective-permute-start(bf16[16,128,128]{2,1,0:T(8,128)(2,1)S(1)} %get-tuple-element.39), channel_id=1, source_target_pairs={{1,0},{2,1},{3,2},{4,3},{5,4},{6,5},{7,6},{8,7},{9,8},{10,9},{11,1... | collective-permute-start | bytes 1572872 | tf_op jit(solution)/shard_map/ppermute | solution.py:517
  9.9 0.1 pad_add_fusion.pos_ref
  10.0 1.6 %collective-permute-done.inv_hbm.rest_1_ = bf16[8,128,128]{2,1,0:T(8,128)(2,1)S(1)} collective-permute-done((bf16[8,128,128]{2,1,0:T(8,128)(2,1)}, bf16[8,128,128]{2,1,0:T(8,128)(2,1)S(1)}, u32[]{:S(2)}, u32[]{:S(2)}) %collective-permute-start) | collective-permute-done | bytes 262176 | tf_op jit(solution)/shard_map/ppermute | solution.py:529
  11.6 0.0 copy-done.3
  11.6 0.0 copy-done.2
  11.6 0.0 copy-done.1
  11.6 0.0 copy-start
  11.7 16.6 %inner_first.1 = (bf16[64,128,128]{2,1,0:T(8,128)(2,1)S(1)}, bf16[64,128,128]{2,1,0:T(8,128)(2,1)S(1)}, bf16[64,8,128,128]{3,2,1,0:T(8,128)(2,1)S(1)}, f32[64,12...) custom-call(s32[2]{0:T(128)S(1)} %pad_add_fusion.pos_ref, ...), custom_call_target="tpu_custom_call" | custom-call | flops 68719476736 | bytes 16777216 | tf_op jit(solution)/shard_map/inner_first/pallas_call | solution.py:207
  28.2 0.0 copy-done
  28.2 2.9 %collective-permute-start.6 = (bf16[8,128,128]{2,1,0:T(8,128)(2,1)S(1)}, bf16[8,128,128]{2,1,0:T(8,128)(2,1)S(1)}, u32[]{:S(2)}, u32[]{:S(2)}) collective-permute-start(bf16[8,128,128]{2,1,0:T(8,128)(2,1)S(1)} %copy-done), channel_id=1, source_target_pairs={{0,3},{1,0},{2,1},{3,2},{4,7},{5,4},{6,5},{7,6},{8,11},{9,8},{10,9... | collective-permute-start | bytes 786440 | tf_op jit(solution)/shard_map/ppermute | solution.py:529
  31.2 0.0 collective-permute-start.5
  31.2 0.0 collective-permute-done.1.bef
  31.2 3.0 %collective-permute-done.2.aft = bf16[16,128,128]{2,1,0:T(8,128)(2,1)S(1)} collective-permute-done((bf16[16,128,128]{2,1,0:T(8,128)(2,1)S(1)}, bf16[16,128,128]{2,1,0:T(8,128)(2,1)S(1)}, u32[]{:S(2)}, u32[]{:S(2)}) %collective-permute-start.2) | collective-permute-done | bytes 524320 | tf_op jit(solution)/shard_map/ppermute | solution.py:517
  34.2 3.9 %edge_second.1 = (f32[64,128,128]{2,1,0:T(8,128)S(1)}, bf16[65,128,128]{2,1,0:T(8,128)(2,1)S(1)}, f32[32,128,128]{2,1,0:T(8,128)S(1)}, bf16[16,128,128]{2,1,0:T(8,128)(2,1)S(1)}, bf16[16,128,128]{2,1,0:T(8,128)(2,1)S(1)}) custom-call(s32[8,64]{1,0:T(8,128)S(1)} %get-tuple-element.34.hs, ...), custom_call_target="tpu_custom_call", output_to_operand_aliasing={{0}: (8, {}), {1}: (9, {}), {2}: (5, {})} | custom-call | flops 8589934592 | bytes 8388608 | tf_op jit(solution)/shard_map/edge_second/pallas_call | solution.py:292
  38.1 2.7 %collective-permute-start.3 = (bf16[16,128,128]{2,1,0:T(8,128)(2,1)S(1)}, bf16[16,128,128]{2,1,0:T(8,128)(2,1)S(1)}, u32[]{:S(2)}, u32[]{:S(2)}) collective-permute-start(bf16[16,128,128]{2,1,0:T(8,128)(2,1)S(1)} %get-tuple-element.45), channel_id=1, source_target_pairs={{0,1},{1,2},{2,3},{3,4},{4,5},{5,6},{6,7},{7,8},{8,9},{9,10},{10,1... | collective-permute-start | bytes 1572872 | tf_op jit(solution)/shard_map/ppermute | solution.py:517
  40.8 1.3 %collective-permute-start.4 = (bf16[16,128,128]{2,1,0:T(8,128)(2,1)S(1)}, bf16[16,128,128]{2,1,0:T(8,128)(2,1)S(1)}, u32[]{:S(2)}, u32[]{:S(2)}) collective-permute-start(bf16[16,128,128]{2,1,0:T(8,128)(2,1)S(1)} %get-tuple-element.46), channel_id=1, source_target_pairs={{1,0},{2,1},{3,2},{4,3},{5,4},{6,5},{7,6},{8,7},{9,8},{10,9},{11,1... | collective-permute-start | bytes 1572872 | tf_op jit(solution)/shard_map/ppermute | solution.py:517
  42.1 0.0 collective-permute-done.6.rest_3_
  42.1 20.2 %collective-permute-done.5.rest_2_ = bf16[8,128,128]{2,1,0:T(8,128)(2,1)S(1)} collective-permute-done((bf16[8,128,128]{2,1,0:T(8,128)(2,1)S(1)}, bf16[8,128,128]{2,1,0:T(8,128)(2,1)S(1)}, u32[]{:S(2)}, u32[]{:S(2)}) %collective-permute-start.5) | collective-permute-done | bytes 262176 | tf_op jit(solution)/shard_map/ppermute | solution.py:529
  62.3 10.4 %inner_residual.1 = (bf16[64,128,128]{2,1,0:T(8,128)(2,1)S(1)}, f32[32,128,128]{2,1,0:T(8,128)S(1)}, bf16[32,128,128]{2,1,0:T(8,128)(2,1)S(1)}, f32[64,128,128]{2,1,0:T(8,128)}) custom-call(s32[2]{0:T(128)S(1)} %pad_add_fusion.pos_ref, s32[8,64]{1,0:T(8,128)S(1)} %get-tuple-element.47.lcol_ref, s32[33]{0:T(128)S(1)} %get-tuple-element.32.bd, ...), custom_call_target="tpu_custom_call" | custom-call | flops 68719476736 | bytes 16777216 | tf_op jit(solution)/shard_map/inner_residual/pallas_call | solution.py:407
  72.8 0.0 collective-permute-done.3.bef
  72.8 0.1 collective-permute-done.4.aft
  72.8 3.3 %edge_final.1 = (bf16[64,128,128]{2,1,0:T(8,128)(2,1)S(1)}, f32[32,128,128]{2,1,0:T(8,128)S(1)}, bf16[128,128]{1,0:T(8,128)(2,1)S(1)}, bf16[128,128]{1,0:T(8,128)(2,1)S(1)}) custom-call(s32[8,64]{1,0:T(8,128)S(1)} %get-tuple-element.34.hs, s32[8,64]{1,0:T(8,128)S(1)} %get-tuple-element.35.hc, ...), custom_call_target="tpu_custom_call", output_to_operand_aliasing={{0}: (8, {}), {1}: (6, {})} | custom-call | flops 4294967296 | bytes 8388608 | tf_op jit(solution)/shard_map/edge_final/pallas_call | solution.py:439
  76.1 1.3 %collective-permute-start.8 = (bf16[128,128]{1,0:T(8,128)(2,1)S(1)}, bf16[128,128]{1,0:T(8,128)(2,1)S(1)}, u32[]{:S(2)}, u32[]{:S(2)}) collective-permute-start(bf16[128,128]{1,0:T(8,128)(2,1)S(1)} %get-tuple-element.54.first_ref), channel_id=1, source_target_pairs={{1,0},{2,1},{3,2},{5,4},{6,5},{7,6},{9,8},{10,9},{11,10},{13,12},{... | collective-permute-start | bytes 98312 | tf_op jit(solution)/shard_map/ppermute | solution.py:517
  77.4 4.5 %collective-permute-start.7 = (bf16[128,128]{1,0:T(8,128)(2,1)S(1)}, bf16[128,128]{1,0:T(8,128)(2,1)S(1)}, u32[]{:S(2)}, u32[]{:S(2)}) collective-permute-start(bf16[128,128]{1,0:T(8,128)(2,1)S(1)} %get-tuple-element.55.last_ref), channel_id=1, source_target_pairs={{0,1},{1,2},{2,3},{4,5},{5,6},{6,7},{8,9},{9,10},{10,11},{12,13},{... | collective-permute-start | bytes 98312 | tf_op jit(solution)/shard_map/ppermute | solution.py:517
  82.0 3.8 %coarse_own.1.out_in = f32[64,128,128]{2,1,0:T(8,128)} custom-call(s32[33]{0:T(128)S(1)} %get-tuple-element.32.bd, s32[6]{0:T(128)S(1)} %get-tuple-element.33.trim, bf16[64,128,128]{2,1,0:T(8,128)(2,1)S(1)} %get-tuple-element.57.r2_ref, f32[64,128,128]{2,1,0:T(8,128)S(1)} %get-tuple-element.50.s2_ref, ...), custom_call_target="tpu_custom_call", output_to_operand_aliasing={{}: (5, {})} | custom-call | flops 2147483648 | bytes 5242880 | tf_op jit(solution)/shard_map/coarse_own/pallas_call | solution.py:469
  85.8 0.0 collective-permute-done.8.aft
  85.8 0.0 collective-permute-done.7.bef
  85.8 2.1 %coarse_split.1 = f32[64,128,128]{2,1,0:T(8,128)} custom-call(s32[33]{0:T(128)S(1)} %get-tuple-element.32.bd, s32[6]{0:T(128)S(1)} %get-tuple-element.33.trim, bf16[128,128]{1,0:T(8,128)(2,1)S(1)} %get-tuple-element.54.first_ref, bf16[128,128]{1,0:T(8,128)(2,1)S(1)} %get-tuple-element.55.last_ref, ...), custom_call_target="tpu_custom_call", output_to_operand_aliasing={{}: (8, {})} | custom-call | flops 268435456 | bytes 1048576 | tf_op jit(solution)/shard_map/coarse_split/pallas_call | solution.py:499
Async XLA Ops:
  0.0 11.6 %copy-start.3 = (s32[1,32]{1,0:T(1,128)S(1)}, s32[1,32]{1,0:T(1,128)}, u32[]{:S(2)}) copy-start(s32[1,32]{1,0:T(1,128)} %size_ref.1) | copy-start | bytes 388
  0.0 11.6 %copy-start.2 = (s32[64]{0:T(128)S(1)}, s32[64]{0:T(128)}, u32[]{:S(2)}) copy-start(s32[64]{0:T(128)} %param.10) | copy-start | bytes 772
  0.0 11.6 %copy-start.1 = (s32[64,8]{0,1:T(8,128)S(1)}, s32[64,8]{0,1:T(8,128)}, u32[]{:S(2)}) copy-start(s32[64,8]{0,1:T(8,128)} %param.9) | copy-start | bytes 6148
  0.0 11.6 %collective-permute-start = (bf16[8,128,128]{2,1,0:T(8,128)(2,1)}, bf16[8,128,128]{2,1,0:T(8,128)(2,1)S(1)}, u32[]{:S(2)}, u32[]{:S(2)}) collective-permute-start(bf16[8,128,128]{2,1,0:T(8,128)(2,1)} %rest_0_.1), channel_id=1, source_target_pairs={{0,1},{1,2},{2,3},{3,0},{4,5},{5,6},{6,7},{7,4},{8,9},{9,10},{10,1... | collective-permute-start | bytes 786440 | tf_op jit(solution)/shard_map/ppermute | solution.py:529
  5.1 26.1 %collective-permute-start.1 = (bf16[16,128,128]{2,1,0:T(8,128)(2,1)S(1)}, bf16[16,128,128]{2,1,0:T(8,128)(2,1)S(1)}, u32[]{:S(2)}, u32[]{:S(2)}) collective-permute-start(bf16[16,128,128]{2,1,0:T(8,128)(2,1)S(1)} %get-tuple-element.38), channel_id=1, source_target_pairs={{0,1},{1,2},{2,3},{3,4},{4,5},{5,6},{6,7},{7,8},{8,9},{9,10},{10,1... | collective-permute-start | bytes 1572872 | tf_op jit(solution)/shard_map/ppermute | solution.py:517
  8.6 25.6 %collective-permute-start.2 = (bf16[16,128,128]{2,1,0:T(8,128)(2,1)S(1)}, bf16[16,128,128]{2,1,0:T(8,128)(2,1)S(1)}, u32[]{:S(2)}, u32[]{:S(2)}) collective-permute-start(bf16[16,128,128]{2,1,0:T(8,128)(2,1)S(1)} %get-tuple-element.39), channel_id=1, source_target_pairs={{1,0},{2,1},{3,2},{4,3},{5,4},{6,5},{7,6},{8,7},{9,8},{10,9},{11,1... | collective-permute-start | bytes 1572872 | tf_op jit(solution)/shard_map/ppermute | solution.py:517
  11.6 16.6 %copy-start = (bf16[8,128,128]{2,1,0:T(8,128)(2,1)S(1)}, bf16[8,128,128]{2,1,0:T(8,128)(2,1)}, u32[]{:S(2)}) copy-start(bf16[8,128,128]{2,1,0:T(8,128)(2,1)} %rest_0_.1) | copy-start | bytes 786436
  28.2 13.9 %collective-permute-start.6 = (bf16[8,128,128]{2,1,0:T(8,128)(2,1)S(1)}, bf16[8,128,128]{2,1,0:T(8,128)(2,1)S(1)}, u32[]{:S(2)}, u32[]{:S(2)}) collective-permute-start(bf16[8,128,128]{2,1,0:T(8,128)(2,1)S(1)} %copy-done), channel_id=1, source_target_pairs={{0,3},{1,0},{2,1},{3,2},{4,7},{5,4},{6,5},{7,6},{8,11},{9,8},{10,9... | collective-permute-start | bytes 786440 | tf_op jit(solution)/shard_map/ppermute | solution.py:529
  31.2 31.2 %collective-permute-start.5 = (bf16[8,128,128]{2,1,0:T(8,128)(2,1)S(1)}, bf16[8,128,128]{2,1,0:T(8,128)(2,1)S(1)}, u32[]{:S(2)}, u32[]{:S(2)}) collective-permute-start(bf16[8,128,128]{2,1,0:T(8,128)(2,1)S(1)} %copy-done), channel_id=1, source_target_pairs={{0,2},{1,3},{2,0},{3,1},{4,6},{5,7},{6,4},{7,5},{8,10},{9,11},{10,... | collective-permute-start | bytes 786440 | tf_op jit(solution)/shard_map/ppermute | solution.py:529
  38.1 34.6 %collective-permute-start.3 = (bf16[16,128,128]{2,1,0:T(8,128)(2,1)S(1)}, bf16[16,128,128]{2,1,0:T(8,128)(2,1)S(1)}, u32[]{:S(2)}, u32[]{:S(2)}) collective-permute-start(bf16[16,128,128]{2,1,0:T(8,128)(2,1)S(1)} %get-tuple-element.45), channel_id=1, source_target_pairs={{0,1},{1,2},{2,3},{3,4},{4,5},{5,6},{6,7},{7,8},{8,9},{9,10},{10,1... | collective-permute-start | bytes 1572872 | tf_op jit(solution)/shard_map/ppermute | solution.py:517
  40.8 32.1 %collective-permute-start.4 = (bf16[16,128,128]{2,1,0:T(8,128)(2,1)S(1)}, bf16[16,128,128]{2,1,0:T(8,128)(2,1)S(1)}, u32[]{:S(2)}, u32[]{:S(2)}) collective-permute-start(bf16[16,128,128]{2,1,0:T(8,128)(2,1)S(1)} %get-tuple-element.46), channel_id=1, source_target_pairs={{1,0},{2,1},{3,2},{4,3},{5,4},{6,5},{7,6},{8,7},{9,8},{10,9},{11,1... | collective-permute-start | bytes 1572872 | tf_op jit(solution)/shard_map/ppermute | solution.py:517
  76.1 9.7 %collective-permute-start.8 = (bf16[128,128]{1,0:T(8,128)(2,1)S(1)}, bf16[128,128]{1,0:T(8,128)(2,1)S(1)}, u32[]{:S(2)}, u32[]{:S(2)}) collective-permute-start(bf16[128,128]{1,0:T(8,128)(2,1)S(1)} %get-tuple-element.54.first_ref), channel_id=1, source_target_pairs={{1,0},{2,1},{3,2},{5,4},{6,5},{7,6},{9,8},{10,9},{11,10},{13,12},{... | collective-permute-start | bytes 98312 | tf_op jit(solution)/shard_map/ppermute | solution.py:517
  77.4 8.4 %collective-permute-start.7 = (bf16[128,128]{1,0:T(8,128)(2,1)S(1)}, bf16[128,128]{1,0:T(8,128)(2,1)S(1)}, u32[]{:S(2)}, u32[]{:S(2)}) collective-permute-start(bf16[128,128]{1,0:T(8,128)(2,1)S(1)} %get-tuple-element.55.last_ref), channel_id=1, source_target_pairs={{0,1},{1,2},{2,3},{4,5},{5,6},{6,7},{8,9},{9,10},{10,11},{12,13},{... | collective-permute-start | bytes 98312 | tf_op jit(solution)/shard_map/ppermute | solution.py:517
where the time goes:
time: 88 us; the launch traced here: 87.9 us
  Pallas kernels  42 us (48%)
  waiting for transfers between devices  25 us (28%)
  starting transfers between devices  20.6 us (23%)
    ppermute x3, waiting for transfers between devices, body(): lax.ppermute(v, 'agg', [(i, (i + t) % group) for i in range(group)])  21.9 us
    pallas_call x1, Pallas kernels, inner_first(): pl.pallas_call(kernel, in_specs=[SMEM, VM, VM, SMEM] + [HBM] * 3 + [ANY],...  16.6 us
    ppermute x6, starting transfers between devices, shift(): lax.ppermute(value, axis, pairs if up else [(j, i) for i, j in pairs])  14.6 us
    pallas_call x1, Pallas kernels, inner_residual(): pl.pallas_call(kernel, in_specs=[SMEM] * 3 + [VM] * 4 + [ANY] * p.G, out_...  10.4 us
    ppermute x3, starting transfers between devices, body(): lax.ppermute(v, 'agg', [(i, (i + t) % group) for i in range(group)])  6.02 us
    pallas_call x1, Pallas kernels, edge_second(): pl.pallas_call(kernel, in_specs=[SMEM] * 3 + [VM] * 7, out_specs=[VM] * 5...  3.9 us
    pallas_call x1, Pallas kernels, coarse_own(): pl.pallas_call(kernel, in_specs=[SMEM] * 2 + [VM] * 3 + [HBM], out_specs=...  3.81 us
    pallas_call x1, Pallas kernels, edge_final(): pl.pallas_call(kernel, in_specs=[SMEM] * 4 + [VM] * 5, out_specs=[VM] * 4...  3.26 us
  transfers between devices with their start and end apart: 9, of which 4 were waited for; matrix products, arithmetic and copies ran while one was open for 0% of the time, Pallas kernels for 42%

commit v1 on v0

v1 whole, which is shorter than its diff:
```python
import jax
import jax.numpy as jnp
from jax import lax
from jax.experimental import pallas as pl
from jax.experimental.pallas import tpu as pltpu
from jax.sharding import PartitionSpec as P

HALO = 16

relax_fine = 0.8
relax_coarse = 1.0

AXES = ("rows", "agg")
F32 = jnp.float32
BF16 = jnp.bfloat16
I32 = jnp.int32
MIB = 1024 * 1024
WEIGHT = 32

SMEM = pl.BlockSpec(memory_space=pltpu.SMEM)
VM = pl.BlockSpec(memory_space=pltpu.VMEM)
ANY = pl.BlockSpec(memory_space=pl.ANY)
HBM = pl.BlockSpec(memory_space=pltpu.HBM)


def mm(a, b):
    return jnp.dot(a, b, preferred_element_type=F32)


def cost(flops, nbytes):
    return pl.CostEstimate(flops=WEIGHT * flops, bytes_accessed=nbytes, transcendentals=0)


def params(mib):
    return pltpu.CompilerParams(vmem_limit_bytes=mib * MIB)


def near(x):
    return pltpu.with_memory_space_constraint(x, pltpu.VMEM)


def far(x):
    return pltpu.with_memory_space_constraint(x, pltpu.HBM)


class Sizes:
    def __init__(self, rows, slots, bs, n, aggs, group):
        self.R, self.K, self.BS, self.N, self.A, self.G = rows, slots, bs, n, aggs, group
        self.H = HALO


def edge_smooth(p, rhs, smoother):
    step = 8
    starts = [0, step, p.R - p.H, p.R - p.H + step]

    def kernel(b_hbm, s_hbm, lo_ref, hi_ref, b, s, sems):
        copies = []
        for c, at in enumerate(starts):
            copies.append(pltpu.make_async_copy(b_hbm.at[pl.ds(at, step)], b.at[c], sems.at[0, c]))
            copies.append(pltpu.make_async_copy(s_hbm.at[pl.ds(at, step)], s.at[c], sems.at[1, c]))
        for c in copies:
            c.start()
        for c in range(len(starts)):
            copies[2 * c].wait()
            copies[2 * c + 1].wait()
            out = lo_ref if c < 2 else hi_ref
            for r in range(step):
                out[(c % 2) * step + r] = (relax_fine * mm(s[c, r], b[c, r])).astype(BF16)

    out = jax.ShapeDtypeStruct((p.H, p.BS, p.N), BF16)
    return pl.pallas_call(
        kernel,
        in_specs=[HBM, HBM],
        out_specs=[VM, VM],
        out_shape=[out, out],
        scratch_shapes=[
            pltpu.VMEM((4, step, p.BS, p.N), BF16),
            pltpu.VMEM((4, step, p.BS, p.BS), BF16),
            pltpu.SemaphoreType.DMA((2, 4)),
        ],
        compiler_params=params(8),
        cost_estimate=cost(4 * p.H * p.BS * p.BS * p.N, 6 * p.H * p.BS * p.N),
        name="edge_smooth",
    )(far(rhs), far(smoother))


def end_row(p, r):
    return jnp.where(r < p.H, r, r + p.R - 2 * p.H)


def row_product(p, blk, at, i, ext, lcol):
    lhs = jnp.concatenate([blk[at, k] for k in range(p.K)], axis=1)
    rhs = jnp.concatenate([ext[lcol[k, i]] for k in range(p.K)], axis=0)
    return mm(lhs, rhs)


def first_sweep(p, pos, cols, counts, sizes, rhs, smoother, blocks, distant):
    piece = 8
    pieces = p.R // piece
    end_pieces = 2 * p.H // piece

    def kernel(
        pos_ref, col_ref, cnt_ref, size_ref, b_hbm, sm_hbm, blk_hbm, _,
        b, sm, blk, s2, ext, acc, lcol, hslot, hcol, hn, bounds, trims, lists, sems, list_sems,
    ):
        start, here = pos_ref[0], pos_ref[1]
        small = [
            pltpu.make_async_copy(src.at[pl.ds(c * piece, piece)], dst.at[pl.ds(c * piece, piece)], sems.at[j, c])
            for c in range(pieces)
            for j, (src, dst) in enumerate(((b_hbm, b), (sm_hbm, sm)))
        ]

        def block_copy(c):
            src = pl.ds(c * piece if c < end_pieces // 2 else p.R - 2 * p.H + c * piece, piece)
            return pltpu.make_async_copy(blk_hbm.at[src], blk.at[pl.ds(c * piece, piece)], sems.at[2, c])

        for c in small:
            c.start()
        for c in range(end_pieces):
            block_copy(c).start()
        ext[p.R] = jnp.zeros((p.BS, p.N), BF16)

        cols = col_ref[...] - start
        ks = lax.broadcasted_iota(I32, (p.K, p.R), 0)
        live = ks < cnt_ref[...]
        inside = jnp.logical_and(cols >= 0, cols < p.R)
        lists[0] = jnp.where(jnp.logical_and(live, inside), cols, p.R)
        outside = jnp.where(jnp.logical_and(live, jnp.logical_not(inside)), 1, 0)
        place = jnp.where(cols < 0, cols + p.H, cols - p.R + p.H)
        count = jnp.zeros((1, p.R), I32)
        slot_rows = [jnp.zeros((1, p.R), I32)] * p.K
        col_rows = [jnp.full((1, p.R), 2 * p.H, I32)] * p.K
        for k in range(p.K):
            out = outside[k:k + 1]
            for j in range(k + 1):
                mine = jnp.logical_and(out > 0, count == j)
                slot_rows[j] = jnp.where(mine, k, slot_rows[j])
                col_rows[j] = jnp.where(mine, place[k:k + 1], col_rows[j])
            count = count + out
        lists[1] = jnp.concatenate(slot_rows, axis=0)
        lists[2] = jnp.concatenate(col_rows, axis=0)
        lists[3] = jnp.broadcast_to(count, (p.K, p.R))
        list_copies = [
            pltpu.make_async_copy(lists.at[j], dst, list_sems.at[j]) for j, dst in enumerate((lcol, hslot, hcol, hn))
        ]
        for c in list_copies:
            c.start()

        def smooth_row(r, c):
            v = relax_fine * mm(sm[r], b[r])
            s2[r] = v
            ext[r] = v.astype(BF16)
            return c

        for c in range(pieces):
            small[2 * c].wait()
            small[2 * c + 1].wait()
            lax.fori_loop(c * piece, (c + 1) * piece, smooth_row, 0, unroll=8)

        for c in list_copies:
            c.wait()

        def edge_row(r, c):
            i = end_row(p, r)
            acc[r] = b[i].astype(F32) - row_product(p, blk, r, i, ext, lcol)
            return c

        for c in range(end_pieces):
            block_copy(c).wait()
            lax.fori_loop(c * piece, (c + 1) * piece, edge_row, 0, unroll=4)

        bounds[0] = 0

        def agg(a, t):
            end, first, last, before, after, lowest, highest = t
            begin = end
            end = end + size_ref[0, a]
            bounds[a + 1] = jnp.clip(end, 0, p.R)
            leads = jnp.logical_and(begin <= 0, end > 0)
            ends = jnp.logical_and(begin < p.R, end >= p.R)
            first = jnp.where(leads, end, first)
            last = jnp.where(ends, begin, last)
            lowest = jnp.where(leads, a, lowest)
            highest = jnp.where(ends, a, highest)
            before = jnp.where(jnp.logical_and(begin < 0, end > 0), 1, before)
            after = jnp.where(jnp.logical_and(begin < p.R, end > p.R), 1, after)
            return end, first, last, before, after, lowest, highest

        zero = jnp.int32(0)
        _, first, last, before, after, lowest, highest = lax.fori_loop(0, p.A, agg, (-here * p.R,) + (zero,) * 6)
        trims[0] = jnp.clip(first, 0, p.R)
        trims[1] = jnp.clip(last, 0, p.R)
        trims[2] = before
        trims[3] = after
        trims[4] = lowest
        trims[5] = highest

    ints = lambda n: jax.ShapeDtypeStruct((n,), I32)
    return pl.pallas_call(
        kernel,
        in_specs=[SMEM, VM, VM, SMEM] + [HBM] * 4,
        out_specs=[VM] * 6 + [SMEM] * 6,
        out_shape=[
            pltpu.VMEM(rhs.shape, BF16),
            pltpu.VMEM(smoother.shape, BF16),
            pltpu.VMEM((2 * p.H,) + blocks.shape[1:], BF16),
            pltpu.VMEM((p.R, p.BS, p.N), F32),
            pltpu.VMEM((p.R + 1, p.BS, p.N), BF16),
            pltpu.VMEM((2 * p.H, p.BS, p.N), F32),
            *[jax.ShapeDtypeStruct((p.K, p.R), I32)] * 4,
            ints(p.A + 1),
            ints(6),
        ],
        scratch_shapes=[
            pltpu.VMEM((4, p.K, p.R), I32),
            pltpu.SemaphoreType.DMA((3, pieces)),
            pltpu.SemaphoreType.DMA((4,)),
        ],
        compiler_params=params(8),
        cost_estimate=cost(2 * p.R * p.K * p.BS * p.BS * p.N, 2 * p.R * p.K * p.BS * p.BS),
        name="first_sweep",
    )(pos, cols, counts, sizes, far(rhs), far(smoother), far(blocks), far(distant))


GROUP = 4
WIDE = 4


def halo_product(hslot, hcol, blk, r, i, slots, halo):
    lhs = jnp.concatenate([blk[r, hslot[j, i]] for j in slots], axis=1)
    rhs = jnp.concatenate([halo[hcol[j, i]] for j in slots], axis=0)
    return mm(lhs, rhs)


def take_rest(p, hslot, hcol, hn, blk, halo, acc):
    def row(r, c):
        i = end_row(p, r)

        @pl.when(hn[0, i] > WIDE)
        def _():
            acc[r] = acc[r] - halo_product(hslot, hcol, blk, r, i, range(WIDE, p.K), halo)

        return c

    lax.fori_loop(0, 2 * p.H, row, 0)


def fill_halo(p, before, after, halo):
    halo[:p.H] = before[...]
    halo[p.H:2 * p.H] = after[...]
    halo[2 * p.H] = jnp.zeros((p.BS, p.N), BF16)


def edge_second(p, hslot, hcol, hn, before, after, acc, smoother, blocks, s2):
    def kernel(hs, hc, hn_ref, bef, aft, acc_in, sm, blk, s2_in, s2_out, ext_out, acc_ref, lo, hi, halo, res):
        fill_halo(p, bef, aft, halo)
        take_rest(p, hs, hc, hn_ref, blk, halo, acc_ref)

        def residual(r, c):
            i = end_row(p, r)
            res[r] = (acc_ref[r] - halo_product(hs, hc, blk, r, i, range(WIDE), halo)).astype(BF16)
            return c

        lax.fori_loop(0, 2 * p.H, residual, 0, unroll=8)

        def sweep(out, r0, i0):
            for g in range(0, p.H, GROUP):
                rows = range(g, g + GROUP)
                new = [s2_in[i0 + r] + relax_fine * mm(sm[i0 + r], res[r0 + r]) for r in rows]
                for r, v in zip(rows, new):
                    s2_out[i0 + r] = v
                    out[r] = v.astype(BF16)
                    ext_out[i0 + r] = v.astype(BF16)

        sweep(lo, 0, 0)
        sweep(hi, p.H, p.R - p.H)
        ext_out[p.R] = jnp.zeros((p.BS, p.N), BF16)

    out = jax.ShapeDtypeStruct((p.H, p.BS, p.N), BF16)
    return pl.pallas_call(
        kernel,
        in_specs=[SMEM] * 3 + [VM] * 6,
        out_specs=[VM] * 5,
        out_shape=[
            pltpu.VMEM((p.R, p.BS, p.N), F32),
            pltpu.VMEM((p.R + 1, p.BS, p.N), BF16),
            pltpu.VMEM((2 * p.H, p.BS, p.N), F32),
            out,
            out,
        ],
        input_output_aliases={8: 0, 5: 2},
        scratch_shapes=[
            pltpu.VMEM((2 * p.H + 1, p.BS, p.N), BF16),
            pltpu.VMEM((2 * p.H, p.BS, p.N), BF16),
        ],
        compiler_params=params(8),
        cost_estimate=cost(8 * p.H * p.BS * p.BS * p.N, 4 * p.H * p.K * p.BS * p.BS),
        name="edge_second",
    )(hslot, hcol, hn, near(before), near(after), near(acc), near(smoother), near(blocks), near(s2))


def aggregate_sum(p, resid, first, last):
    return lax.fori_loop(
        first, last, lambda r, t: t + resid[r].astype(F32), jnp.zeros((p.BS, p.N), F32)
    )


def add_fix(inverse, res, s2, first, last):
    fix = (relax_coarse * mm(inverse, res)).astype(BF16).astype(F32)

    def row(r, c):
        s2[r] = s2[r] + fix
        return c

    lax.fori_loop(first, last, row, 0)


def inner_aggregate(p, first, last):
    return jnp.logical_and(first >= p.H, last <= p.R - p.H)


def inner_rows(p, pos, lcol, bounds, rhs, smoother, end_blocks, blocks, ext1, ext2, s2, inverses):
    piece = 4
    inner = p.R - 2 * p.H
    share = p.A // p.G

    def kernel(pos_ref, lcol_ref, bd, b, sm, end_blk, ext1_ref, ext_in, s2_ref, blk_hbm, *rest):
        inv_refs, (r2, acc, inv, ext, s2_out, out, blk, row_sems, sems, blk_sems) = rest[:4], rest[4:]

        def block_copy(c):
            src = blk_hbm.at[pl.ds(p.H + c * piece, piece)]
            return pltpu.make_async_copy(src, blk.at[pl.ds(c * piece, piece)], blk_sems.at[c])

        for c in range(inner // piece):
            block_copy(c).start()

        own, before, after, distant = inv_refs

        def place(src, t):
            at = pl.ds(lax.rem(pos_ref[1] - t + p.G, p.G) * share, share)
            return pltpu.make_async_copy(src, inv.at[at], sems.at[t])

        def place_all(act):
            act(place(own, 0))

            @pl.when(pos_ref[2] == 0)
            def _():
                act(place(before, 1))
                act(place(after, p.G - 1))

            @pl.when(pos_ref[2] > 0)
            def _():
                for t in range(1, p.G):
                    act(place(distant.at[t - 1], t))

        place_all(lambda c: c.start())

        for c in range(inner // piece):
            block_copy(c).wait()
            rows = range(c * piece, (c + 1) * piece)
            res = [
                (b[p.H + r].astype(F32) - row_product(p, blk, r, p.H + r, ext1_ref, lcol_ref)).astype(BF16) for r in rows
            ]
            new = [s2_ref[p.H + r] + relax_fine * mm(sm[p.H + r], v) for r, v in zip(rows, res)]
            for r, v in zip(rows, new):
                s2_out[p.H + r] = v
                ext[p.H + r] = v.astype(BF16)

        def inner_row(r, c):
            i = p.H + r
            r2[i] = (b[i].astype(F32) - row_product(p, blk, r, i, ext, lcol_ref)).astype(BF16)
            return c

        lax.fori_loop(0, inner, inner_row, 0, unroll=4)
        place_all(lambda c: c.wait())

        def copy(r):
            return pltpu.make_async_copy(s2_out.at[r], out.at[r], row_sems.at[r])

        def send(r, c):
            copy(r).start()
            return c

        def wait(r, c):
            copy(r).wait()
            return c

        def aggregates(act):
            def one(a, c):
                first, last = bd[a], bd[a + 1]
                pl.when(jnp.logical_and(first < last, inner_aggregate(p, first, last)))(lambda: act(a, first, last))
                return c

            lax.fori_loop(0, p.A, one, 0)

        def fix(a, first, last):
            res = aggregate_sum(p, r2, first, last).astype(BF16)
            add_fix(inv[a], res, s2_out, first, last)
            lax.fori_loop(first, last, send, 0)

        aggregates(fix)

        def edge_row(r, c):
            i = end_row(p, r)
            acc[r] = b[i].astype(F32) - row_product(p, end_blk, r, i, ext, lcol_ref)
            return c

        lax.fori_loop(0, 2 * p.H, edge_row, 0, unroll=4)

        def settle(a, first, last):
            lax.fori_loop(first, last, wait, 0)

        aggregates(settle)

    return pl.pallas_call(
        kernel,
        in_specs=[SMEM] * 3 + [VM] * 6 + [HBM] + [ANY] * 3 + [HBM],
        out_specs=[VM] * 5 + [HBM],
        out_shape=[
            pltpu.VMEM((p.R, p.BS, p.N), BF16),
            pltpu.VMEM((2 * p.H, p.BS, p.N), F32),
            pltpu.VMEM((p.A, p.BS, p.BS), BF16),
            pltpu.VMEM((p.R + 1, p.BS, p.N), BF16),
            pltpu.VMEM((p.R, p.BS, p.N), F32),
            jax.ShapeDtypeStruct((p.R, p.BS, p.N), F32),
        ],
        input_output_aliases={7: 3, 8: 4},
        scratch_shapes=[
            pltpu.VMEM((inner,) + blocks.shape[1:], BF16),
            pltpu.SemaphoreType.DMA((p.R,)),
            pltpu.SemaphoreType.DMA((p.G,)),
            pltpu.SemaphoreType.DMA((inner // piece,)),
        ],
        compiler_params=params(16),
        cost_estimate=cost(2 * p.R * p.K * p.BS * p.BS * p.N, 2 * p.R * p.K * p.BS * p.BS),
        name="inner_rows",
    )(
        pos, lcol, bounds, near(rhs), near(smoother), near(end_blocks), near(ext1), near(ext2), near(s2), far(blocks),
        *inverses[:3], far(inverses[3]),
    )


def edge_final(p, hslot, hcol, hn, trims, before, after, acc, blocks, r2):
    def kernel(hs, hc, hn_ref, trim, bef, aft, acc_in, blk, r2_in, r2_out, acc_ref, part_first, part_last, halo):
        fill_halo(p, bef, aft, halo)
        take_rest(p, hs, hc, hn_ref, blk, halo, acc_ref)

        def row(r, c):
            i = end_row(p, r)
            r2_out[i] = (acc_ref[r] - halo_product(hs, hc, blk, r, i, range(WIDE), halo)).astype(BF16)
            return c

        lax.fori_loop(0, 2 * p.H, row, 0, unroll=8)
        part_first[...] = aggregate_sum(p, r2_out, 0, trim[0]).astype(BF16)
        part_last[...] = aggregate_sum(p, r2_out, trim[1], p.R).astype(BF16)

    one = jax.ShapeDtypeStruct((p.BS, p.N), BF16)
    return pl.pallas_call(
        kernel,
        in_specs=[SMEM] * 4 + [VM] * 5,
        out_specs=[VM] * 4,
        out_shape=[
            pltpu.VMEM((p.R, p.BS, p.N), BF16),
            pltpu.VMEM((2 * p.H, p.BS, p.N), F32),
            one,
            one,
        ],
        input_output_aliases={8: 0, 6: 1},
        scratch_shapes=[pltpu.VMEM((2 * p.H + 1, p.BS, p.N), BF16)],
        compiler_params=params(8),
        cost_estimate=cost(4 * p.H * p.BS * p.BS * p.N, 4 * p.H * p.K * p.BS * p.BS),
        name="edge_final",
    )(hslot, hcol, hn, trims, near(before), near(after), near(acc), near(blocks), near(r2))


def coarse_own(p, bounds, trims, r2, s2, inv):
    def kernel(bd, trim, r2_ref, s2_in, inv_ref, s2_ref):
        def one(a, c):
            first, last = bd[a], bd[a + 1]
            split = jnp.logical_or(
                jnp.logical_and(first == 0, trim[2] > 0), jnp.logical_and(last == p.R, trim[3] > 0)
            )
            done = jnp.logical_or(split, inner_aggregate(p, first, last))

            @pl.when(jnp.logical_and(first < last, jnp.logical_not(done)))
            def _():
                res = aggregate_sum(p, r2_ref, first, last).astype(BF16)
                add_fix(inv_ref[a], res, s2_ref, first, last)

            return c

        lax.fori_loop(0, p.A, one, 0)

    return pl.pallas_call(
        kernel,
        in_specs=[SMEM] * 2 + [VM] * 3,
        out_specs=VM,
        out_shape=pltpu.VMEM((p.R, p.BS, p.N), F32),
        input_output_aliases={3: 0},
        compiler_params=params(8),
        cost_estimate=cost(p.A * p.BS * p.BS * p.N, 5 * p.R * p.BS * p.N),
        name="coarse_own",
    )(bounds, trims, near(r2), near(s2), near(inv))


def coarse_split(p, bounds, trims, part_first, part_last, from_before, from_after, s2, inv, out):
    def kernel(bd, trim, first_ref, last_ref, bef, aft, s2_in, inv_ref, out_in, s2_ref, out_ref, row_sems):
        @pl.when(trim[2] > 0)
        def _():
            res = (bef[...].astype(F32) + first_ref[...].astype(F32)).astype(BF16)
            add_fix(inv_ref[trim[4]], res, s2_ref, 0, trim[0])

        @pl.when(trim[3] > 0)
        def _():
            res = (last_ref[...].astype(F32) + aft[...].astype(F32)).astype(BF16)
            add_fix(inv_ref[trim[5]], res, s2_ref, trim[1], p.R)

        def inner(a, t):
            begin, end = t
            first, last = bd[a], bd[a + 1]
            sent = jnp.logical_and(first < last, inner_aggregate(p, first, last))
            return jnp.where(sent, jnp.minimum(begin, first), begin), jnp.where(sent, last, end)

        begin, end = lax.fori_loop(0, p.A, inner, (jnp.int32(p.R), jnp.int32(p.R)))

        def copy(r):
            return pltpu.make_async_copy(s2_ref.at[r], out_ref.at[r], row_sems.at[r])

        def send(r, c):
            copy(r).start()
            return c

        def wait(r, c):
            copy(r).wait()
            return c

        for step in (send, wait):
            lax.fori_loop(0, begin, step, 0)
            lax.fori_loop(end, p.R, step, 0)

    return pl.pallas_call(
        kernel,
        in_specs=[SMEM] * 2 + [VM] * 6 + [HBM],
        out_specs=[VM, HBM],
        out_shape=[
            pltpu.VMEM((p.R, p.BS, p.N), F32),
            jax.ShapeDtypeStruct((p.R, p.BS, p.N), F32),
        ],
        input_output_aliases={6: 0, 8: 1},
        scratch_shapes=[pltpu.SemaphoreType.DMA((p.R,))],
        compiler_params=params(8),
        cost_estimate=cost(4 * p.BS * p.BS * p.N, p.R * p.BS * p.N),
        name="coarse_split",
    )(
        bounds, trims, near(part_first), near(part_last), near(from_before), near(from_after), near(s2), near(inv), out
    )[1]


def shift(value, axis, up):
    size = lax.axis_size(axis)
    pairs = [(i, i + 1) for i in range(size - 1)]
    return lax.ppermute(value, axis, pairs if up else [(j, i) for i, j in pairs])


def body(load_rhs, blocks, columns, counts, smoother, agg_sizes, coarse_inv):
    rows, bs, n = load_rhs.shape
    group = lax.axis_size("agg")
    p = Sizes(rows, blocks.shape[1], bs, n, agg_sizes.shape[1], group)
    here = lax.axis_index("agg")

    lo1, hi1 = edge_smooth(p, load_rhs, smoother)
    before1, after1 = shift(hi1, AXES, True), shift(lo1, AXES, False)

    sizes, own_inv, lo1 = lax.optimization_barrier((agg_sizes, coarse_inv, lo1))
    ids = jnp.arange(p.A, dtype=I32)
    ends = jnp.sum(jnp.where(ids[None, :] <= ids[:, None], sizes, 0), axis=1)
    owner = ids // (p.A // group)
    reach = jnp.maximum((ends - 1) // rows - owner, owner - (ends - sizes[0]) // rows)
    apart = jnp.max(reach) > 1

    def every(own):
        turn = lambda t: lax.ppermute(own, "agg", [(i, (i + t) % group) for i in range(group)])
        return jnp.stack([turn(t) for t in range(1, group)])

    def none(own):
        return jnp.zeros((group - 1,) + own.shape, own.dtype)

    distant = lax.cond(apart, every, none, own_inv)
    pos = jnp.stack([lax.axis_index(AXES) * rows, here, apart.astype(I32)]).astype(I32)
    rhs, smoother, end_blocks, s2, ext1, acc1, lcol, hslot, hcol, hn, bounds, trims = first_sweep(
        p, pos, columns.T, counts[None, :], agg_sizes, load_rhs, smoother, blocks, distant
    )
    late, hn = lax.optimization_barrier((coarse_inv, hn))
    inverses = coarse_inv, shift(late, "agg", True), shift(late, "agg", False), distant

    s2, ext2, _, lo2, hi2 = edge_second(p, hslot, hcol, hn, before1, after1, acc1, smoother, end_blocks, s2)
    before2, after2 = shift(hi2, AXES, True), shift(lo2, AXES, False)
    r2, acc2, inv, _, s2, out = inner_rows(
        p, pos, lcol, bounds, rhs, smoother, end_blocks, blocks, ext1, ext2, s2, inverses
    )
    r2, _, part_first, part_last = edge_final(p, hslot, hcol, hn, trims, before2, after2, acc2, end_blocks, r2)
    from_before, from_after = shift(part_last, "agg", True), shift(part_first, "agg", False)
    s2 = coarse_own(p, bounds, trims, r2, s2, inv)
    return coarse_split(p, bounds, trims, part_first, part_last, from_before, from_after, s2, inv, out)


def solution(mesh):
    placed = (
        P(AXES, None, None),
        P(AXES, None, None, None),
        P(AXES, None),
        P(AXES),
        P(AXES, None, None),
        P("rows", None),
        P(AXES, None, None),
    )
    return jax.shard_map(
        body, mesh=mesh, in_specs=placed, out_specs=P(AXES, None, None), check_vma=False
    )
```

time: 88 us -> 81.7 us (0.928)
  waiting for transfers between devices: 25 us -> 15.8 us
  Pallas kernels: 42 us -> 39.5 us
  starting transfers between devices: 20.6 us -> 22.7 us
  local copies, waits for them, and re-layouts: 0.02 us -> 0.99 us
    ppermute x3 -> x0, waiting for transfers between devices: 21.9 us -> none  [body(): lax.ppermute(v, 'agg', [(i, (i + t) % group) for i in range(group)])]
    ppermute x6 -> x8, waiting for transfers between devices: 3.12 us -> 15.8 us  [shift(): lax.ppermute(value, axis, pairs if up else [(j, i) for i, j in pairs])]
    ppermute x6 -> x8, starting transfers between devices: 14.6 us -> 22.7 us  [shift(): lax.ppermute(value, axis, pairs if up else [(j, i) for i, j in pairs])]
    ppermute x3 -> x0, starting transfers between devices: 6.02 us -> none  [body(): lax.ppermute(v, 'agg', [(i, (i + t) % group) for i in range(group)])]
    pallas_call x4, Pallas kernels: 34.7 us -> 31.2 us  [the longest x1 16.3 us: inner_rows(): pl.pallas_call(kernel, in_specs=[SMEM] * 3 + [VM] * 6 + [HBM] + [ANY] * 3...]
    pallas_call x1, Pallas kernels: 2.1 us -> 2.99 us  [coarse_split(): pl.pallas_call(kernel, in_specs=[SMEM] * 2 + [VM] * 6 + [HBM], out_specs=...]
  transfers between devices with their start and end apart: 9 -> 8, of which waited for: 4 -> 2; matrix products, arithmetic and copies ran while one was open for 0% -> 1% of each run, Pallas kernels for 42% -> 39%
where the time goes in v1:
time: 81.7 us; the launch traced here: 80.8 us
  Pallas kernels  39.5 us (48%)
  starting transfers between devices  22.7 us (28%)
  waiting for transfers between devices  15.8 us (19%)
  local copies, waits for them, and re-layouts  0.99 us (1%)
  between operations  0.88 us (1%)
  other arithmetic  0.84 us (1%)
    ppermute x8, starting transfers between devices, shift(): lax.ppermute(value, axis, pairs if up else [(j, i) for i, j in pairs])  22.7 us
    pallas_call x1, Pallas kernels, inner_rows(): pl.pallas_call(kernel, in_specs=[SMEM] * 3 + [VM] * 6 + [HBM] + [ANY] * 3...  16.3 us
    ppermute x8, waiting for transfers between devices, shift(): lax.ppermute(value, axis, pairs if up else [(j, i) for i, j in pairs])  15.8 us
    pallas_call x1, Pallas kernels, first_sweep(): pl.pallas_call(kernel, in_specs=[SMEM, VM, VM, SMEM] + [HBM] * 4, out_spe...  8.62 us
    pallas_call x1, Pallas kernels, edge_second(): pl.pallas_call(kernel, in_specs=[SMEM] * 3 + [VM] * 6, out_specs=[VM] * 5...  3.92 us
    pallas_call x1, Pallas kernels, edge_final(): pl.pallas_call(kernel, in_specs=[SMEM] * 4 + [VM] * 5, out_specs=[VM] * 4...  3.25 us
    pallas_call x1, Pallas kernels, coarse_split(): pl.pallas_call(kernel, in_specs=[SMEM] * 2 + [VM] * 6 + [HBM], out_specs=...  2.99 us
    pallas_call x1, Pallas kernels, coarse_own(): pl.pallas_call(kernel, in_specs=[SMEM] * 2 + [VM] * 3, out_specs=VM, out_...  2.34 us
  transfers between devices with their start and end apart: 8, of which 2 were waited for; matrix products, arithmetic and copies ran while one was open for 1% of the time, Pallas kernels for 39%

profile of v1, /device:TPU:0, one launch (start us, length us, event | category | flops | bytes accessed | tf_op | source)
XLA Modules:
  0.0 80.8 jit_solution(673950664762612134)
XLA Ops:
  0.0 0.0 copy-start.4
  0.0 0.0 copy-start.1
  0.0 2.0 %edge_smooth.1 = (bf16[16,128,128]{2,1,0:T(8,128)(2,1)S(1)}, bf16[16,128,128]{2,1,0:T(8,128)(2,1)S(1)}) custom-call(bf16[64,128,128]{2,1,0:T(8,128)(2,1)} %b_hbm.3, bf16[64,128,128]{2,1,0:T(8,128)(2,1)} %sm_hbm.1), custom_call_target="tpu_custom_call" | custom-call | flops 4294967296 | bytes 1572864 | tf_op jit(solution)/shard_map/edge_smooth/pallas_call | solution.py:71
  2.1 0.0 copy-start
  2.1 0.0 copy-start.2
  2.1 5.0 %collective-permute-start.3 = (bf16[16,128,128]{2,1,0:T(8,128)(2,1)S(1)}, bf16[16,128,128]{2,1,0:T(8,128)(2,1)S(1)}, u32[]{:S(2)}, u32[]{:S(2)}) collective-permute-start(bf16[16,128,128]{2,1,0:T(8,128)(2,1)S(1)} %get-tuple-element.49), channel_id=1, source_target_pairs={{0,1},{1,2},{2,3},{3,4},{4,5},{5,6},{6,7},{7,8},{8,9},{9,10},{10,1... | collective-permute-start | bytes 1572872 | tf_op jit(solution)/shard_map/ppermute | solution.py:562
  7.1 1.3 %collective-permute-start.4 = (bf16[16,128,128]{2,1,0:T(8,128)(2,1)S(1)}, bf16[16,128,128]{2,1,0:T(8,128)(2,1)S(1)}, u32[]{:S(2)}, u32[]{:S(2)}) collective-permute-start(bf16[16,128,128]{2,1,0:T(8,128)(2,1)S(1)} %get-tuple-element.40), channel_id=1, source_target_pairs={{1,0},{2,1},{3,2},{4,3},{5,4},{6,5},{7,6},{8,7},{9,8},{10,9},{11,1... | collective-permute-start | bytes 1572872 | tf_op jit(solution)/shard_map/ppermute | solution.py:562
  8.4 0.0 copy-done.1
  8.4 0.1 select_reduce_fusion
  8.5 0.7 maximum_reduce_fusion
  9.8 0.0 copy-done.4
  9.8 0.2 conditional.1
  9.8 0.2 broadcast.22
  10.0 0.0 copy-start.3
  10.0 0.1 pad_add_fusion.pos_ref
  10.1 0.8 %copy-done.3 = bf16[3,8,128,128]{3,2,1,0:T(8,128)(2,1)} copy-done((bf16[3,8,128,128]{3,2,1,0:T(8,128)(2,1)}, bf16[3,8,128,128]{3,2,1,0:T(8,128)(2,1)S(1)}, u32[]{:S(2)}) %copy-start.3) | copy-done | bytes 786456
  10.9 0.0 copy-done
  10.9 0.0 copy-done.2
  10.9 8.6 %first_sweep.1 = (bf16[64,128,128]{2,1,0:T(8,128)(2,1)S(1)}, bf16[64,128,128]{2,1,0:T(8,128)(2,1)S(1)}, bf16[32,8,128,128]{3,2,1,0:T(8,128)(2,1)S(1)}, f32[64,12...) custom-call(s32[3]{0:T(128)S(1)} %pad_add_fusion.pos_ref, ...), custom_call_target="tpu_custom_call" | custom-call | flops 68719476736 | bytes 16777216 | tf_op jit(solution)/shard_map/first_sweep/pallas_call | solution.py:199
  19.5 1.3 %collective-permute-start.8 = (bf16[8,128,128]{2,1,0:T(8,128)(2,1)S(1)}, bf16[8,128,128]{2,1,0:T(8,128)(2,1)S(1)}, u32[]{:S(2)}, u32[]{:S(2)}) collective-permute-start(bf16[8,128,128]{2,1,0:T(8,128)(2,1)S(1)} %copy-done.4), channel_id=1, source_target_pairs={{1,0},{2,1},{3,2},{5,4},{6,5},{7,6},{9,8},{10,9},{11,10},{13,12},{... | collective-permute-start | bytes 786440 | tf_op jit(solution)/shard_map/ppermute | solution.py:562
  20.8 5.2 %collective-permute-start.7 = (bf16[8,128,128]{2,1,0:T(8,128)(2,1)S(1)}, bf16[8,128,128]{2,1,0:T(8,128)(2,1)S(1)}, u32[]{:S(2)}, u32[]{:S(2)}) collective-permute-start(bf16[8,128,128]{2,1,0:T(8,128)(2,1)S(1)} %copy-done.4), channel_id=1, source_target_pairs={{0,1},{1,2},{2,3},{4,5},{5,6},{6,7},{8,9},{9,10},{10,11},{12,13},{... | collective-permute-start | bytes 786440 | tf_op jit(solution)/shard_map/ppermute | solution.py:562
  26.0 0.0 collective-permute-done.3.bef
  26.0 7.1 %collective-permute-done.4.aft = bf16[16,128,128]{2,1,0:T(8,128)(2,1)S(1)} collective-permute-done((bf16[16,128,128]{2,1,0:T(8,128)(2,1)S(1)}, bf16[16,128,128]{2,1,0:T(8,128)(2,1)S(1)}, u32[]{:S(2)}, u32[]{:S(2)}) %collective-permute-start.4) | collective-permute-done | bytes 524320 | tf_op jit(solution)/shard_map/ppermute | solution.py:562
  33.1 3.9 %edge_second.1 = (f32[64,128,128]{2,1,0:T(8,128)S(1)}, bf16[65,128,128]{2,1,0:T(8,128)(2,1)S(1)}, f32[32,128,128]{2,1,0:T(8,128)S(1)}, bf16[16,128,128]{2,1,0:T(8,128)(2,1)S(1)}, bf16[16,128,128]{2,1,0:T(8,128)(2,1)S(1)}) custom-call(s32[8,64]{1,0:T(8,128)S(1)} %get-tuple-element.45.hs, ...), custom_call_target="tpu_custom_call", output_to_operand_aliasing={{0}: (8, {}), {2}: (5, {})} | custom-call | flops 8589934592 | bytes 8388608 | tf_op jit(solution)/shard_map/edge_second/pallas_call | solution.py:280
  37.1 2.8 %collective-permute-start.5 = (bf16[16,128,128]{2,1,0:T(8,128)(2,1)S(1)}, bf16[16,128,128]{2,1,0:T(8,128)(2,1)S(1)}, u32[]{:S(2)}, u32[]{:S(2)}) collective-permute-start(bf16[16,128,128]{2,1,0:T(8,128)(2,1)S(1)} %get-tuple-element.54), channel_id=1, source_target_pairs={{0,1},{1,2},{2,3},{3,4},{4,5},{5,6},{6,7},{7,8},{8,9},{9,10},{10,1... | collective-permute-start | bytes 1572872 | tf_op jit(solution)/shard_map/ppermute | solution.py:562
  39.9 1.3 %collective-permute-start.6 = (bf16[16,128,128]{2,1,0:T(8,128)(2,1)S(1)}, bf16[16,128,128]{2,1,0:T(8,128)(2,1)S(1)}, u32[]{:S(2)}, u32[]{:S(2)}) collective-permute-start(bf16[16,128,128]{2,1,0:T(8,128)(2,1)S(1)} %get-tuple-element.55), channel_id=1, source_target_pairs={{1,0},{2,1},{3,2},{4,3},{5,4},{6,5},{7,6},{8,7},{9,8},{10,9},{11,1... | collective-permute-start | bytes 1572872 | tf_op jit(solution)/shard_map/ppermute | solution.py:562
  41.2 0.0 collective-permute-done.8.rest_2_
  41.2 0.0 collective-permute-done.7.rest_1_
  41.2 16.3 %inner_rows.1 = (bf16[64,128,128]{2,1,0:T(8,128)(2,1)S(1)}, f32[32,128,128]{2,1,0:T(8,128)S(1)}, bf16[32,128,128]{2,1,0:T(8,128)(2,1)S(1)}, bf16[65,128,128]{2,1...) custom-call(s32[3]{0:T(128)S(1)} %pad_add_fusion.pos_ref, ...), custom_call_target="tpu_custom_call", output_to_operand_aliasing={{3}: (7, {}), {4}: (8, {})} | custom-call | flops 68719476736 | bytes 16777216 | tf_op jit(solution)/shard_map/inner_rows/pallas_call | solution.py:415
  57.6 0.0 collective-permute-done.5.bef
  57.6 8.7 %collective-permute-done.6.aft = bf16[16,128,128]{2,1,0:T(8,128)(2,1)S(1)} collective-permute-done((bf16[16,128,128]{2,1,0:T(8,128)(2,1)S(1)}, bf16[16,128,128]{2,1,0:T(8,128)(2,1)S(1)}, u32[]{:S(2)}, u32[]{:S(2)}) %collective-permute-start.6) | collective-permute-done | bytes 524320 | tf_op jit(solution)/shard_map/ppermute | solution.py:562
  66.3 3.2 %edge_final.1 = (bf16[64,128,128]{2,1,0:T(8,128)(2,1)S(1)}, f32[32,128,128]{2,1,0:T(8,128)S(1)}, bf16[128,128]{1,0:T(8,128)(2,1)S(1)}, bf16[128,128]{1,0:T(8,128)(2,1)S(1)}) custom-call(s32[8,64]{1,0:T(8,128)S(1)} %get-tuple-element.45.hs, s32[8,64]{1,0:T(8,128)S(1)} %get-tuple-element.46.hc, ...), custom_call_target="tpu_custom_call", output_to_operand_aliasing={{0}: (8, {}), {1}: (6, {})} | custom-call | flops 4294967296 | bytes 8388608 | tf_op jit(solution)/shard_map/edge_final/pallas_call | solution.py:458
  69.6 1.3 %collective-permute-start.10 = (bf16[128,128]{1,0:T(8,128)(2,1)S(1)}, bf16[128,128]{1,0:T(8,128)(2,1)S(1)}, u32[]{:S(2)}, u32[]{:S(2)}) collective-permute-start(bf16[128,128]{1,0:T(8,128)(2,1)S(1)} %get-tuple-element.64.first_ref), channel_id=1, source_target_pairs={{1,0},{2,1},{3,2},{5,4},{6,5},{7,6},{9,8},{10,9},{11,10},{13,12},{... | collective-permute-start | bytes 98312 | tf_op jit(solution)/shard_map/ppermute | solution.py:562
  70.9 4.5 %collective-permute-start.9 = (bf16[128,128]{1,0:T(8,128)(2,1)S(1)}, bf16[128,128]{1,0:T(8,128)(2,1)S(1)}, u32[]{:S(2)}, u32[]{:S(2)}) collective-permute-start(bf16[128,128]{1,0:T(8,128)(2,1)S(1)} %get-tuple-element.65.last_ref), channel_id=1, source_target_pairs={{0,1},{1,2},{2,3},{4,5},{5,6},{6,7},{8,9},{9,10},{10,11},{12,13},{... | collective-permute-start | bytes 98312 | tf_op jit(solution)/shard_map/ppermute | solution.py:562
  75.4 2.3 %coarse_own.1.s2_in = f32[64,128,128]{2,1,0:T(8,128)S(1)} custom-call(s32[33]{0:T(128)S(1)} %get-tuple-element.43.bd, s32[6]{0:T(128)S(1)} %get-tuple-element.44.trim, bf16[64,128,128]{2,1,0:T(8,128)(2,1)S(1)} %get-tuple-element.66.r2_ref, f32[64,128,128]{2,1,0:T(8,128)S(1)} %get-tuple-element.67.s2_in, ...), custom_call_target="tpu_custom_call", output_to_operand_aliasing={{}: (3, {})} | custom-call | flops 2147483648 | bytes 5242880 | tf_op jit(solution)/shard_map/coarse_own/pallas_call | solution.py:494
  77.8 0.0 collective-permute-done.10.aft
  77.8 0.0 collective-permute-done.9.bef
  77.8 3.0 %coarse_split.1 = (f32[64,128,128]{2,1,0:T(8,128)S(1)}, f32[64,128,128]{2,1,0:T(8,128)}) custom-call(s32[33]{0:T(128)S(1)} %get-tuple-element.43.bd, s32[6]{0:T(128)S(1)} %get-tuple-element.44.trim, bf16[128,128]{1,0:T(8,128)(2,1)S(1)} %get-tuple-element.64.first_ref, ...), custom_call_target="tpu_custom_call", output_to_operand_aliasing={{0}: (6, {}), {1}: (8, {})} | custom-call | flops 268435456 | bytes 1048576 | tf_op jit(solution)/shard_map/coarse_split/pallas_call | solution.py:541
Async XLA Ops:
  0.0 9.8 %copy-start.4 = (bf16[8,128,128]{2,1,0:T(8,128)(2,1)S(1)}, bf16[8,128,128]{2,1,0:T(8,128)(2,1)}, u32[]{:S(2)}) copy-start(bf16[8,128,128]{2,1,0:T(8,128)(2,1)} %rest_0_.1) | copy-start | bytes 786436
  0.0 8.4 %copy-start.1 = (s32[1,32]{1,0:T(1,128)S(1)}, s32[1,32]{1,0:T(1,128)}, u32[]{:S(2)}) copy-start(s32[1,32]{1,0:T(1,128)} %size_ref.1) | copy-start | bytes 388
  2.1 8.8 %copy-start = (s32[64,8]{0,1:T(8,128)S(1)}, s32[64,8]{0,1:T(8,128)}, u32[]{:S(2)}) copy-start(s32[64,8]{0,1:T(8,128)} %param.11) | copy-start | bytes 6148
  2.1 8.8 %copy-start.2 = (s32[64]{0:T(128)S(1)}, s32[64]{0:T(128)}, u32[]{:S(2)}) copy-start(s32[64]{0:T(128)} %param.12) | copy-start | bytes 772
  2.1 23.9 %collective-permute-start.3 = (bf16[16,128,128]{2,1,0:T(8,128)(2,1)S(1)}, bf16[16,128,128]{2,1,0:T(8,128)(2,1)S(1)}, u32[]{:S(2)}, u32[]{:S(2)}) collective-permute-start(bf16[16,128,128]{2,1,0:T(8,128)(2,1)S(1)} %get-tuple-element.49), channel_id=1, source_target_pairs={{0,1},{1,2},{2,3},{3,4},{4,5},{5,6},{6,7},{7,8},{8,9},{9,10},{10,1... | collective-permute-start | bytes 1572872 | tf_op jit(solution)/shard_map/ppermute | solution.py:562
  7.1 26.1 %collective-permute-start.4 = (bf16[16,128,128]{2,1,0:T(8,128)(2,1)S(1)}, bf16[16,128,128]{2,1,0:T(8,128)(2,1)S(1)}, u32[]{:S(2)}, u32[]{:S(2)}) collective-permute-start(bf16[16,128,128]{2,1,0:T(8,128)(2,1)S(1)} %get-tuple-element.40), channel_id=1, source_target_pairs={{1,0},{2,1},{3,2},{4,3},{5,4},{6,5},{7,6},{8,7},{9,8},{10,9},{11,1... | collective-permute-start | bytes 1572872 | tf_op jit(solution)/shard_map/ppermute | solution.py:562
  10.0 0.9 %copy-start.3 = (bf16[3,8,128,128]{3,2,1,0:T(8,128)(2,1)}, bf16[3,8,128,128]{3,2,1,0:T(8,128)(2,1)S(1)}, u32[]{:S(2)}) copy-start(bf16[3,8,128,128]{3,2,1,0:T(8,128)(2,1)S(1)} %get-tuple-element.71._.rest_3_) | copy-start | bytes 2359300
  19.5 21.7 %collective-permute-start.8 = (bf16[8,128,128]{2,1,0:T(8,128)(2,1)S(1)}, bf16[8,128,128]{2,1,0:T(8,128)(2,1)S(1)}, u32[]{:S(2)}, u32[]{:S(2)}) collective-permute-start(bf16[8,128,128]{2,1,0:T(8,128)(2,1)S(1)} %copy-done.4), channel_id=1, source_target_pairs={{1,0},{2,1},{3,2},{5,4},{6,5},{7,6},{9,8},{10,9},{11,10},{13,12},{... | collective-permute-start | bytes 786440 | tf_op jit(solution)/shard_map/ppermute | solution.py:562
  20.8 20.4 %collective-permute-start.7 = (bf16[8,128,128]{2,1,0:T(8,128)(2,1)S(1)}, bf16[8,128,128]{2,1,0:T(8,128)(2,1)S(1)}, u32[]{:S(2)}, u32[]{:S(2)}) collective-permute-start(bf16[8,128,128]{2,1,0:T(8,128)(2,1)S(1)} %copy-done.4), channel_id=1, source_target_pairs={{0,1},{1,2},{2,3},{4,5},{5,6},{6,7},{8,9},{9,10},{10,11},{12,13},{... | collective-permute-start | bytes 786440 | tf_op jit(solution)/shard_map/ppermute | solution.py:562
  37.1 20.5 %collective-permute-start.5 = (bf16[16,128,128]{2,1,0:T(8,128)(2,1)S(1)}, bf16[16,128,128]{2,1,0:T(8,128)(2,1)S(1)}, u32[]{:S(2)}, u32[]{:S(2)}) collective-permute-start(bf16[16,128,128]{2,1,0:T(8,128)(2,1)S(1)} %get-tuple-element.54), channel_id=1, source_target_pairs={{0,1},{1,2},{2,3},{3,4},{4,5},{5,6},{6,7},{7,8},{8,9},{9,10},{10,1... | collective-permute-start | bytes 1572872 | tf_op jit(solution)/shard_map/ppermute | solution.py:562
  39.9 26.4 %collective-permute-start.6 = (bf16[16,128,128]{2,1,0:T(8,128)(2,1)S(1)}, bf16[16,128,128]{2,1,0:T(8,128)(2,1)S(1)}, u32[]{:S(2)}, u32[]{:S(2)}) collective-permute-start(bf16[16,128,128]{2,1,0:T(8,128)(2,1)S(1)} %get-tuple-element.55), channel_id=1, source_target_pairs={{1,0},{2,1},{3,2},{4,3},{5,4},{6,5},{7,6},{8,7},{9,8},{10,9},{11,1... | collective-permute-start | bytes 1572872 | tf_op jit(solution)/shard_map/ppermute | solution.py:562
  69.6 8.2 %collective-permute-start.10 = (bf16[128,128]{1,0:T(8,128)(2,1)S(1)}, bf16[128,128]{1,0:T(8,128)(2,1)S(1)}, u32[]{:S(2)}, u32[]{:S(2)}) collective-permute-start(bf16[128,128]{1,0:T(8,128)(2,1)S(1)} %get-tuple-element.64.first_ref), channel_id=1, source_target_pairs={{1,0},{2,1},{3,2},{5,4},{6,5},{7,6},{9,8},{10,9},{11,10},{13,12},{... | collective-permute-start | bytes 98312 | tf_op jit(solution)/shard_map/ppermute | solution.py:562
  70.9 6.9 %collective-permute-start.9 = (bf16[128,128]{1,0:T(8,128)(2,1)S(1)}, bf16[128,128]{1,0:T(8,128)(2,1)S(1)}, u32[]{:S(2)}, u32[]{:S(2)}) collective-permute-start(bf16[128,128]{1,0:T(8,128)(2,1)S(1)} %get-tuple-element.65.last_ref), channel_id=1, source_target_pairs={{0,1},{1,2},{2,3},{4,5},{5,6},{6,7},{8,9},{9,10},{10,11},{12,13},{... | collective-permute-start | bytes 98312 | tf_op jit(solution)/shard_map/ppermute | solution.py:562

commit v2 on v1

--- a/solution.py
+++ b/solution.py
@@ -49,30 +49,43 @@
         self.H = HALO
 
 
-def edge_smooth(p, rhs, smoother):
-    step = 8
-    starts = [0, step, p.R - p.H, p.R - p.H + step]
-
-    def kernel(b_hbm, s_hbm, lo_ref, hi_ref, b, s, sems):
+def edge_smooth(p, pos, sizes, rhs, smoother):
+    step = p.H // 2
+    share = p.A // p.G
+
+    def kernel(pos_ref, size_ref, b_hbm, s_hbm, apart, *rest):
+        outs, (b, s, sems) = rest[:4], rest[4:]
+        odd = pos_ref[2]
+        starts = []
+        for first, last in ((0, p.R - step), (step, p.R - 2 * step)):
+            starts += [jnp.where(odd > 0, last, first), jnp.where(odd > 0, first, last)]
         copies = []
         for c, at in enumerate(starts):
             copies.append(pltpu.make_async_copy(b_hbm.at[pl.ds(at, step)], b.at[c], sems.at[0, c]))
             copies.append(pltpu.make_async_copy(s_hbm.at[pl.ds(at, step)], s.at[c], sems.at[1, c]))
         for c in copies:
             c.start()
-        for c in range(len(starts)):
+
+        def reach(a, t):
+            begin, most = t
+            end = begin + size_ref[0, a]
+            owner = a // share
+            here = jnp.maximum(lax.div(end - 1, p.R) - owner, owner - lax.div(begin, p.R))
+            return end, jnp.maximum(most, here)
+
+        apart[0] = lax.fori_loop(0, p.A, reach, (jnp.int32(0), jnp.int32(0)))[1]
+        for c in range(4):
             copies[2 * c].wait()
             copies[2 * c + 1].wait()
-            out = lo_ref if c < 2 else hi_ref
             for r in range(step):
-                out[(c % 2) * step + r] = (relax_fine * mm(s[c, r], b[c, r])).astype(BF16)
-
-    out = jax.ShapeDtypeStruct((p.H, p.BS, p.N), BF16)
-    return pl.pallas_call(
-        kernel,
-        in_specs=[HBM, HBM],
-        out_specs=[VM, VM],
-        out_shape=[out, out],
+                outs[c][r] = (relax_fine * mm(s[c, r], b[c, r])).astype(BF16)
+
+    out = jax.ShapeDtypeStruct((step, p.BS, p.N), BF16)
+    return pl.pallas_call(
+        kernel,
+        in_specs=[SMEM, SMEM, HBM, HBM],
+        out_specs=[SMEM] + [VM] * 4,
+        out_shape=[jax.ShapeDtypeStruct((1,), I32)] + [out] * 4,
         scratch_shapes=[
             pltpu.VMEM((4, step, p.BS, p.N), BF16),
             pltpu.VMEM((4, step, p.BS, p.BS), BF16),
@@ -81,7 +94,7 @@
         compiler_params=params(8),
         cost_estimate=cost(4 * p.H * p.BS * p.BS * p.N, 6 * p.H * p.BS * p.N),
         name="edge_smooth",
-    )(far(rhs), far(smoother))
+    )(pos, sizes, far(rhs), far(smoother))
 
 
 def end_row(p, r):
@@ -94,14 +107,15 @@
     return mm(lhs, rhs)
 
 
-def first_sweep(p, pos, cols, counts, sizes, rhs, smoother, blocks, distant):
+def first_sweep(p, pos, cols, counts, sizes, rhs, smoother, blocks, apart, inverses):
     piece = 8
+    share = p.A // p.G
     pieces = p.R // piece
     end_pieces = 2 * p.H // piece
 
     def kernel(
-        pos_ref, col_ref, cnt_ref, size_ref, b_hbm, sm_hbm, blk_hbm, _,
-        b, sm, blk, s2, ext, acc, lcol, hslot, hcol, hn, bounds, trims, lists, sems, list_sems,
+        pos_ref, col_ref, cnt_ref, size_ref, b_hbm, sm_hbm, blk_hbm, apart_ref, own, by_odd, by_even, distant,
+        b, sm, blk, inv, s2, ext, acc, lcol, hslot, hcol, hn, bounds, trims, lists, sems, list_sems, inv_sems,
     ):
         start, here = pos_ref[0], pos_ref[1]
         small = [
@@ -118,6 +132,26 @@
             c.start()
         for c in range(end_pieces):
             block_copy(c).start()
+        back = jnp.where((pos_ref[1] & 1) > 0, p.G - 1, 1)
+
+        def inverse_copy(src, distance, t):
+            at = pl.ds(lax.rem(pos_ref[1] - distance + p.G, p.G) * share, share)
+            return pltpu.make_async_copy(src, inv.at[at], inv_sems.at[t])
+
+        def place_all(act):
+            act(inverse_copy(own, 0, 0))
+
+            @pl.when(apart_ref[0] <= 1)
+            def _():
+                act(inverse_copy(by_odd, back, 1))
+                act(inverse_copy(by_even, p.G - back, 2))
+
+            @pl.when(apart_ref[0] > 1)
+            def _():
+                for t in range(1, p.G):
+                    act(inverse_copy(distant.at[t - 1], t, t))
+
+        place_all(lambda c: c.start())
         ext[p.R] = jnp.zeros((p.BS, p.N), BF16)
 
         cols = col_ref[...] - start
@@ -169,6 +203,8 @@
             block_copy(c).wait()
             lax.fori_loop(c * piece, (c + 1) * piece, edge_row, 0, unroll=4)
 
+        place_all(lambda c: c.wait())
+
         bounds[0] = 0
 
         def agg(a, t):
@@ -198,12 +234,13 @@
     ints = lambda n: jax.ShapeDtypeStruct((n,), I32)
     return pl.pallas_call(
         kernel,
-        in_specs=[SMEM, VM, VM, SMEM] + [HBM] * 4,
-        out_specs=[VM] * 6 + [SMEM] * 6,
+        in_specs=[SMEM, VM, VM, SMEM] + [HBM] * 3 + [SMEM] + [ANY] * 4,
+        out_specs=[VM] * 7 + [SMEM] * 6,
         out_shape=[
             pltpu.VMEM(rhs.shape, BF16),
             pltpu.VMEM(smoother.shape, BF16),
             pltpu.VMEM((2 * p.H,) + blocks.shape[1:], BF16),
+            pltpu.VMEM((p.A, p.BS, p.BS), BF16),
             pltpu.VMEM((p.R, p.BS, p.N), F32),
             pltpu.VMEM((p.R + 1, p.BS, p.N), BF16),
             pltpu.VMEM((2 * p.H, p.BS, p.N), F32),
@@ -215,11 +252,12 @@
             pltpu.VMEM((4, p.K, p.R), I32),
             pltpu.SemaphoreType.DMA((3, pieces)),
             pltpu.SemaphoreType.DMA((4,)),
+            pltpu.SemaphoreType.DMA((p.G,)),
         ],
         compiler_params=params(8),
         cost_estimate=cost(2 * p.R * p.K * p.BS * p.BS * p.N, 2 * p.R * p.K * p.BS * p.BS),
         name="first_sweep",
-    )(pos, cols, counts, sizes, far(rhs), far(smoother), far(blocks), far(distant))
+    )(pos, cols, counts, sizes, far(rhs), far(smoother), far(blocks), apart, *inverses)
 
 
 GROUP = 4
@@ -232,7 +270,7 @@
     return mm(lhs, rhs)
 
 
-def take_rest(p, hslot, hcol, hn, blk, halo, acc):
+def take_rest(p, hslot, hcol, hn, blk, halo, acc, rows):
     def row(r, c):
         i = end_row(p, r)
 
@@ -242,61 +280,75 @@
 
         return c
 
-    lax.fori_loop(0, 2 * p.H, row, 0)
-
-
-def fill_halo(p, before, after, halo):
-    halo[:p.H] = before[...]
-    halo[p.H:2 * p.H] = after[...]
-    halo[2 * p.H] = jnp.zeros((p.BS, p.N), BF16)
-
-
-def edge_second(p, hslot, hcol, hn, before, after, acc, smoother, blocks, s2):
-    def kernel(hs, hc, hn_ref, bef, aft, acc_in, sm, blk, s2_in, s2_out, ext_out, acc_ref, lo, hi, halo, res):
-        fill_halo(p, bef, aft, halo)
-        take_rest(p, hs, hc, hn_ref, blk, halo, acc_ref)
-
-        def residual(r, c):
-            i = end_row(p, r)
-            res[r] = (acc_ref[r] - halo_product(hs, hc, blk, r, i, range(WIDE), halo)).astype(BF16)
-            return c
-
-        lax.fori_loop(0, 2 * p.H, residual, 0, unroll=8)
-
-        def sweep(out, r0, i0):
-            for g in range(0, p.H, GROUP):
+    for first, last in rows:
+        lax.fori_loop(first, last, row, 0)
+
+
+def put_halo(p, odd, halo, from_odd, from_even, before, after):
+    step = p.H // 2
+    halo[pl.ds(jnp.where(odd > 0, after, before), step)] = from_odd[...]
+    halo[pl.ds(jnp.where(odd > 0, before, after), step)] = from_even[...]
+
+
+def edge_second(p, outer, pos, hslot, hcol, hn, parts, acc, smoother, blocks, s2, ext2=None, halo=None):
+    step = p.H // 2
+    halves = ((0, step), (2 * p.H - step, 2 * p.H)) if outer else ((step, p.H), (p.H, p.H + step))
+    before, after = (0, 2 * p.H - step) if outer else (step, p.H)
+
+    def kernel(pos_ref, hs, hc, hn_ref, acc_in, s2_in, *rest):
+        from_odd, from_even, sm, blk = rest[-12:-8]
+        acc_ref, s2_out, ext_out, halo_ref, to_odd, to_even, res, sent = rest[-8:]
+        odd = pos_ref[2]
+        put_halo(p, odd, halo_ref, from_odd, from_even, before, after)
+        if not outer:
+            halo_ref[2 * p.H] = jnp.zeros((p.BS, p.N), BF16)
+            ext_out[p.R] = jnp.zeros((p.BS, p.N), BF16)
+        take_rest(p, hs, hc, hn_ref, blk, halo_ref, acc_ref, halves)
+        for first, last in halves:
+
+            def residual(r, c):
+                i = end_row(p, r)
+                res[r] = (acc_ref[r] - halo_product(hs, hc, blk, r, i, range(WIDE), halo_ref)).astype(BF16)
+                return c
+
+            lax.fori_loop(first, last, residual, 0, unroll=8)
+        for h, (first, last) in enumerate(halves):
+            shift_by = 0 if first < p.H else p.R - 2 * p.H
+            for g in range(first, last, GROUP):
                 rows = range(g, g + GROUP)
-                new = [s2_in[i0 + r] + relax_fine * mm(sm[i0 + r], res[r0 + r]) for r in rows]
+                new = [s2_in[shift_by + r] + relax_fine * mm(sm[shift_by + r], res[r]) for r in rows]
                 for r, v in zip(rows, new):
-                    s2_out[i0 + r] = v
-                    out[r] = v.astype(BF16)
-                    ext_out[i0 + r] = v.astype(BF16)
-
-        sweep(lo, 0, 0)
-        sweep(hi, p.H, p.R - p.H)
-        ext_out[p.R] = jnp.zeros((p.BS, p.N), BF16)
-
-    out = jax.ShapeDtypeStruct((p.H, p.BS, p.N), BF16)
-    return pl.pallas_call(
-        kernel,
-        in_specs=[SMEM] * 3 + [VM] * 6,
-        out_specs=[VM] * 5,
+                    s2_out[shift_by + r] = v
+                    sent[h, r - first] = v.astype(BF16)
+                    ext_out[shift_by + r] = v.astype(BF16)
+        to_odd[...] = sent[odd]
+        to_even[...] = sent[1 - odd]
+
+    out = jax.ShapeDtypeStruct((step, p.BS, p.N), BF16)
+    kept = [] if not outer else [near(ext2), near(halo)]
+    return pl.pallas_call(
+        kernel,
+        in_specs=[SMEM] * 4 + [VM] * (6 + len(kept)),
+        out_specs=[VM] * 6,
         out_shape=[
+            pltpu.VMEM((2 * p.H, p.BS, p.N), F32),
             pltpu.VMEM((p.R, p.BS, p.N), F32),
             pltpu.VMEM((p.R + 1, p.BS, p.N), BF16),
-            pltpu.VMEM((2 * p.H, p.BS, p.N), F32),
+            pltpu.VMEM((2 * p.H + 1, p.BS, p.N), BF16),
             out,
             out,
         ],
-        input_output_aliases={8: 0, 5: 2},
+        input_output_aliases={4: 0, 5: 1, **({6: 2, 7: 3} if outer else {})},
         scratch_shapes=[
-            pltpu.VMEM((2 * p.H + 1, p.BS, p.N), BF16),
             pltpu.VMEM((2 * p.H, p.BS, p.N), BF16),
+            pltpu.VMEM((2, step, p.BS, p.N), BF16),
         ],
         compiler_params=params(8),
         cost_estimate=cost(8 * p.H * p.BS * p.BS * p.N, 4 * p.H * p.K * p.BS * p.BS),
-        name="edge_second",
-    )(hslot, hcol, hn, near(before), near(after), near(acc), near(smoother), near(blocks), near(s2))
+        name="edge_second_outer" if outer else "edge_second_inner",
+    )(
+        pos, hslot, hcol, hn, near(acc), near(s2), *kept, near(parts[0]), near(parts[1]), near(smoother), near(blocks)
+    )
 
 
 def aggregate_sum(p, resid, first, last):
@@ -319,42 +371,17 @@
     return jnp.logical_and(first >= p.H, last <= p.R - p.H)
 
 
-def inner_rows(p, pos, lcol, bounds, rhs, smoother, end_blocks, blocks, ext1, ext2, s2, inverses):
+def inner_second(p, lcol, rhs, smoother, ext1, ext2, s2, blocks):
     piece = 4
     inner = p.R - 2 * p.H
-    share = p.A // p.G
-
-    def kernel(pos_ref, lcol_ref, bd, b, sm, end_blk, ext1_ref, ext_in, s2_ref, blk_hbm, *rest):
-        inv_refs, (r2, acc, inv, ext, s2_out, out, blk, row_sems, sems, blk_sems) = rest[:4], rest[4:]
-
+
+    def kernel(lcol_ref, b, sm, ext1_ref, ext_in, s2_ref, blk_hbm, ext, s2_out, blk, blk_sems):
         def block_copy(c):
             src = blk_hbm.at[pl.ds(p.H + c * piece, piece)]
             return pltpu.make_async_copy(src, blk.at[pl.ds(c * piece, piece)], blk_sems.at[c])
 
         for c in range(inner // piece):
             block_copy(c).start()
-
-        own, before, after, distant = inv_refs
-
-        def place(src, t):
-            at = pl.ds(lax.rem(pos_ref[1] - t + p.G, p.G) * share, share)
-            return pltpu.make_async_copy(src, inv.at[at], sems.at[t])
-
-        def place_all(act):
-            act(place(own, 0))
-
-            @pl.when(pos_ref[2] == 0)
-            def _():
-                act(place(before, 1))
-                act(place(after, p.G - 1))
-
-            @pl.when(pos_ref[2] > 0)
-            def _():
-                for t in range(1, p.G):
-                    act(place(distant.at[t - 1], t))
-
-        place_all(lambda c: c.start())
-
         for c in range(inner // piece):
             block_copy(c).wait()
             rows = range(c * piece, (c + 1) * piece)
@@ -366,13 +393,38 @@
                 s2_out[p.H + r] = v
                 ext[p.H + r] = v.astype(BF16)
 
+    return pl.pallas_call(
+        kernel,
+        in_specs=[SMEM] + [VM] * 5 + [HBM],
+        out_specs=[VM] * 3,
+        out_shape=[
+            pltpu.VMEM((p.R + 1, p.BS, p.N), BF16),
+            pltpu.VMEM((p.R, p.BS, p.N), F32),
+            pltpu.VMEM((inner,) + blocks.shape[1:], BF16),
+        ],
+        input_output_aliases={4: 0, 5: 1},
+        scratch_shapes=[pltpu.SemaphoreType.DMA((inner // piece,))],
+        compiler_params=params(8),
+        cost_estimate=cost(0, 0),
+        name="inner_second",
+    )(lcol, near(rhs), near(smoother), near(ext1), near(ext2), near(s2), far(blocks))
+
+
+def inner_rows(p, pos, lcol, bounds, rhs, end_blocks, blocks, ext, s2, parts, inv):
+    inner = p.R - 2 * p.H
+
+    def kernel(
+        pos_ref, lcol_ref, bd, b, end_blk, blk, ext, inv, s2_ref, from_odd, from_even,
+        r2, acc, s2_out, halo, out, row_sems,
+    ):
+        put_halo(p, pos_ref[2], halo, from_odd, from_even, 0, 2 * p.H - p.H // 2)
+
         def inner_row(r, c):
             i = p.H + r
             r2[i] = (b[i].astype(F32) - row_product(p, blk, r, i, ext, lcol_ref)).astype(BF16)
             return c
 
         lax.fori_loop(0, inner, inner_row, 0, unroll=4)
-        place_all(lambda c: c.wait())
 
         def copy(r):
             return pltpu.make_async_copy(s2_out.at[r], out.at[r], row_sems.at[r])
@@ -414,36 +466,33 @@
 
     return pl.pallas_call(
         kernel,
-        in_specs=[SMEM] * 3 + [VM] * 6 + [HBM] + [ANY] * 3 + [HBM],
-        out_specs=[VM] * 5 + [HBM],
+        in_specs=[SMEM] * 3 + [VM] * 8,
+        out_specs=[VM] * 4 + [HBM],
         out_shape=[
             pltpu.VMEM((p.R, p.BS, p.N), BF16),
             pltpu.VMEM((2 * p.H, p.BS, p.N), F32),
-            pltpu.VMEM((p.A, p.BS, p.BS), BF16),
-            pltpu.VMEM((p.R + 1, p.BS, p.N), BF16),
             pltpu.VMEM((p.R, p.BS, p.N), F32),
+            pltpu.VMEM((2 * p.H + 1, p.BS, p.N), BF16),
             jax.ShapeDtypeStruct((p.R, p.BS, p.N), F32),
         ],
-        input_output_aliases={7: 3, 8: 4},
-        scratch_shapes=[
-            pltpu.VMEM((inner,) + blocks.shape[1:], BF16),
-            pltpu.SemaphoreType.DMA((p.R,)),
-            pltpu.SemaphoreType.DMA((p.G,)),
-            pltpu.SemaphoreType.DMA((inner // piece,)),
-        ],
-        compiler_params=params(16),
-        cost_estimate=cost(2 * p.R * p.K * p.BS * p.BS * p.N, 2 * p.R * p.K * p.BS * p.BS),
+        input_output_aliases={8: 2},
+        scratch_shapes=[pltpu.SemaphoreType.DMA((p.R,))],
+        compiler_params=params(8),
+        cost_estimate=cost(4 * p.R * p.K * p.BS * p.BS * p.N, p.R * p.K * p.BS * p.BS),
         name="inner_rows",
     )(
-        pos, lcol, bounds, near(rhs), near(smoother), near(end_blocks), near(ext1), near(ext2), near(s2), far(blocks),
-        *inverses[:3], far(inverses[3]),
-    )
-
-
-def edge_final(p, hslot, hcol, hn, trims, before, after, acc, blocks, r2):
-    def kernel(hs, hc, hn_ref, trim, bef, aft, acc_in, blk, r2_in, r2_out, acc_ref, part_first, part_last, halo):
-        fill_halo(p, bef, aft, halo)
-        take_rest(p, hs, hc, hn_ref, blk, halo, acc_ref)
+        pos, lcol, bounds, near(rhs), near(end_blocks), near(blocks), near(ext), near(inv), near(s2), *map(near, parts)
+    )
+
+
+def edge_final(p, pos, hslot, hcol, hn, trims, parts, halo, acc, blocks, r2):
+    step = p.H // 2
+
+    def kernel(pos_ref, hs, hc, hn_ref, trim, from_odd, from_even, halo_in, acc_in, blk, r2_in, *rest):
+        r2_out, acc_ref, halo, part_first, part_last, to_odd, to_even, both = rest
+        put_halo(p, pos_ref[2], halo, from_odd, from_even, step, p.H)
+        halo[2 * p.H] = jnp.zeros((p.BS, p.N), BF16)
+        take_rest(p, hs, hc, hn_ref, blk, halo, acc_ref, ((0, 2 * p.H),))
 
         def row(r, c):
             i = end_row(p, r)
@@ -451,26 +500,31 @@
             return c
 
         lax.fori_loop(0, 2 * p.H, row, 0, unroll=8)
-        part_first[...] = aggregate_sum(p, r2_out, 0, trim[0]).astype(BF16)
-        part_last[...] = aggregate_sum(p, r2_out, trim[1], p.R).astype(BF16)
+        both[0] = aggregate_sum(p, r2_out, 0, trim[0]).astype(BF16)
+        both[1] = aggregate_sum(p, r2_out, trim[1], p.R).astype(BF16)
+        part_first[...] = both[0]
+        part_last[...] = both[1]
+        odd = pos_ref[1] & 1
+        to_odd[...] = both[odd]
+        to_even[...] = both[1 - odd]
 
     one = jax.ShapeDtypeStruct((p.BS, p.N), BF16)
     return pl.pallas_call(
         kernel,
-        in_specs=[SMEM] * 4 + [VM] * 5,
-        out_specs=[VM] * 4,
+        in_specs=[SMEM] * 5 + [VM] * 6,
+        out_specs=[VM] * 7,
         out_shape=[
             pltpu.VMEM((p.R, p.BS, p.N), BF16),
             pltpu.VMEM((2 * p.H, p.BS, p.N), F32),
-            one,
-            one,
-        ],
-        input_output_aliases={8: 0, 6: 1},
-        scratch_shapes=[pltpu.VMEM((2 * p.H + 1, p.BS, p.N), BF16)],
+            pltpu.VMEM((2 * p.H + 1, p.BS, p.N), BF16),
+            *[one] * 4,
+        ],
+        input_output_aliases={10: 0, 8: 1, 7: 2},
+        scratch_shapes=[pltpu.VMEM((2, p.BS, p.N), BF16)],
         compiler_params=params(8),
         cost_estimate=cost(4 * p.H * p.BS * p.BS * p.N, 4 * p.H * p.K * p.BS * p.BS),
         name="edge_final",
-    )(hslot, hcol, hn, trims, near(before), near(after), near(acc), near(blocks), near(r2))
+    )(pos, hslot, hcol, hn, trims, *map(near, parts), near(halo), near(acc), near(blocks), near(r2))
 
 
 def coarse_own(p, bounds, trims, r2, s2, inv):
@@ -503,16 +557,22 @@
     )(bounds, trims, near(r2), near(s2), near(inv))
 
 
-def coarse_split(p, bounds, trims, part_first, part_last, from_before, from_after, s2, inv, out):
-    def kernel(bd, trim, first_ref, last_ref, bef, aft, s2_in, inv_ref, out_in, s2_ref, out_ref, row_sems):
+def coarse_split(p, pos, bounds, trims, part_first, part_last, parts, s2, inv, out):
+    def kernel(
+        pos_ref, bd, trim, first_ref, last_ref, by_odd, by_even, s2_in, inv_ref, out_in, s2_ref, out_ref, row_sems
+    ):
+        odd = (pos_ref[1] & 1) > 0
+        bef = jnp.where(odd, by_even[...].astype(F32), by_odd[...].astype(F32))
+        aft = jnp.where(odd, by_odd[...].astype(F32), by_even[...].astype(F32))
+
         @pl.when(trim[2] > 0)
         def _():
-            res = (bef[...].astype(F32) + first_ref[...].astype(F32)).astype(BF16)
+            res = (bef + first_ref[...].astype(F32)).astype(BF16)
             add_fix(inv_ref[trim[4]], res, s2_ref, 0, trim[0])
 
         @pl.when(trim[3] > 0)
         def _():
-            res = (last_ref[...].astype(F32) + aft[...].astype(F32)).astype(BF16)
+            res = (last_ref[...].astype(F32) + aft).astype(BF16)
             add_fix(inv_ref[trim[5]], res, s2_ref, trim[1], p.R)
 
         def inner(a, t):
@@ -540,26 +600,26 @@
 
     return pl.pallas_call(
         kernel,
-        in_specs=[SMEM] * 2 + [VM] * 6 + [HBM],
+        in_specs=[SMEM] * 3 + [VM] * 6 + [HBM],
         out_specs=[VM, HBM],
         out_shape=[
             pltpu.VMEM((p.R, p.BS, p.N), F32),
             jax.ShapeDtypeStruct((p.R, p.BS, p.N), F32),
         ],
-        input_output_aliases={6: 0, 8: 1},
+        input_output_aliases={7: 0, 9: 1},
         scratch_shapes=[pltpu.SemaphoreType.DMA((p.R,))],
         compiler_params=params(8),
         cost_estimate=cost(4 * p.BS * p.BS * p.N, p.R * p.BS * p.N),
         name="coarse_split",
     )(
-        bounds, trims, near(part_first), near(part_last), near(from_before), near(from_after), near(s2), near(inv), out
+        pos, bounds, trims, near(part_first), near(part_last), *map(near, parts), near(s2), near(inv), out
     )[1]
 
 
-def shift(value, axis, up):
+def swaps(axis, odd):
     size = lax.axis_size(axis)
-    pairs = [(i, i + 1) for i in range(size - 1)]
-    return lax.ppermute(value, axis, pairs if up else [(j, i) for i, j in pairs])
+    pairs = [(i, i + 1) for i in range(odd, size - 1, 2)]
+    return lambda value: lax.ppermute(value, axis, pairs + [(j, i) for i, j in pairs])
 
 
 def body(load_rhs, blocks, columns, counts, smoother, agg_sizes, coarse_inv):
@@ -567,16 +627,14 @@
     group = lax.axis_size("agg")
     p = Sizes(rows, blocks.shape[1], bs, n, agg_sizes.shape[1], group)
     here = lax.axis_index("agg")
-
-    lo1, hi1 = edge_smooth(p, load_rhs, smoother)
-    before1, after1 = shift(hi1, AXES, True), shift(lo1, AXES, False)
-
-    sizes, own_inv, lo1 = lax.optimization_barrier((agg_sizes, coarse_inv, lo1))
-    ids = jnp.arange(p.A, dtype=I32)
-    ends = jnp.sum(jnp.where(ids[None, :] <= ids[:, None], sizes, 0), axis=1)
-    owner = ids // (p.A // group)
-    reach = jnp.maximum((ends - 1) // rows - owner, owner - (ends - sizes[0]) // rows)
-    apart = jnp.max(reach) > 1
+    index = lax.axis_index(AXES)
+    pos = jnp.stack([index * rows, here, index & 1]).astype(I32)
+
+    swap_odd, swap_even = swaps(AXES, 1), swaps(AXES, 0)
+
+    apart, *out1 = edge_smooth(p, pos, agg_sizes, load_rhs, smoother)
+    inner1 = swap_odd(out1[0]), swap_even(out1[1])
+    outer1 = swap_odd(out1[2]), swap_even(out1[3])
 
     def every(own):
         turn = lambda t: lax.ppermute(own, "agg", [(i, (i + t) % group) for i in range(group)])
@@ -585,23 +643,29 @@
     def none(own):
         return jnp.zeros((group - 1,) + own.shape, own.dtype)
 
-    distant = lax.cond(apart, every, none, own_inv)
-    pos = jnp.stack([lax.axis_index(AXES) * rows, here, apart.astype(I32)]).astype(I32)
-    rhs, smoother, end_blocks, s2, ext1, acc1, lcol, hslot, hcol, hn, bounds, trims = first_sweep(
-        p, pos, columns.T, counts[None, :], agg_sizes, load_rhs, smoother, blocks, distant
-    )
-    late, hn = lax.optimization_barrier((coarse_inv, hn))
-    inverses = coarse_inv, shift(late, "agg", True), shift(late, "agg", False), distant
-
-    s2, ext2, _, lo2, hi2 = edge_second(p, hslot, hcol, hn, before1, after1, acc1, smoother, end_blocks, s2)
-    before2, after2 = shift(hi2, AXES, True), shift(lo2, AXES, False)
-    r2, acc2, inv, _, s2, out = inner_rows(
-        p, pos, lcol, bounds, rhs, smoother, end_blocks, blocks, ext1, ext2, s2, inverses
-    )
-    r2, _, part_first, part_last = edge_final(p, hslot, hcol, hn, trims, before2, after2, acc2, end_blocks, r2)
-    from_before, from_after = shift(part_last, "agg", True), shift(part_first, "agg", False)
+    distant = lax.cond(apart[0] > 1, every, none, coarse_inv)
+    inverses = coarse_inv, swaps("agg", 1)(coarse_inv), swaps("agg", 0)(coarse_inv), distant
+    rhs, smoother, end_blocks, inv, s2, ext1, acc1, lcol, hslot, hcol, hn, bounds, trims = first_sweep(
+        p, pos, columns.T, counts[None, :], agg_sizes, load_rhs, smoother, blocks, apart, inverses
+    )
+    acc1, s2, ext2, halo, *out2 = edge_second(
+        p, False, pos, hslot, hcol, hn, inner1, acc1, smoother, end_blocks, s2
+    )
+    inner2 = swap_odd(out2[0]), swap_even(out2[1])
+    _, s2, ext2, _, *out2 = edge_second(
+        p, True, pos, hslot, hcol, hn, outer1, acc1, smoother, end_blocks, s2, ext2, halo
+    )
+    outer2 = swap_odd(out2[0]), swap_even(out2[1])
+    ext2, s2, inner_blocks = inner_second(p, lcol, rhs, smoother, ext1, ext2, s2, blocks)
+    r2, acc2, s2, halo, out = inner_rows(
+        p, pos, lcol, bounds, rhs, end_blocks, inner_blocks, ext2, s2, inner2, inv
+    )
+    r2, _, _, part_first, part_last, to_odd, to_even = edge_final(
+        p, pos, hslot, hcol, hn, trims, outer2, halo, acc2, end_blocks, r2
+    )
+    parts = swaps("agg", 1)(to_odd), swaps("agg", 0)(to_even)
     s2 = coarse_own(p, bounds, trims, r2, s2, inv)
-    return coarse_split(p, bounds, trims, part_first, part_last, from_before, from_after, s2, inv, out)
+    return coarse_split(p, pos, bounds, trims, part_first, part_last, parts, s2, inv, out)
 
 
 def solution(mesh):

time: 81.7 us -> 76.1 us (0.931)
  waiting for transfers between devices: 15.8 us -> 3.32 us
  starting transfers between devices: 22.7 us -> 27.4 us
  Pallas kernels: 39.5 us -> 42.7 us
    ppermute x8 -> x12, waiting for transfers between devices: 15.8 us -> 3.32 us  [swaps(): lax.ppermute(value, axis, pairs + [(j, i) for i, j in pairs])]
    ppermute x8 -> x12, starting transfers between devices: 22.7 us -> 27.4 us  [swaps(): lax.ppermute(value, axis, pairs + [(j, i) for i, j in pairs])]
    pallas_call x6 -> x8, Pallas kernels: 37.2 us -> 40.5 us  [the longest x1 10.1 us: inner_rows(): pl.pallas_call(kernel, in_specs=[SMEM] * 3 + [VM] * 8, out_specs=[VM] * 4...]
  transfers between devices with their start and end apart: 8 -> 12, of which waited for: 2 -> 2; matrix products, arithmetic and copies ran while one was open for 1% -> 0% of each run, Pallas kernels for 39% -> 48%
where the time goes in v2:
time: 76.1 us; the launch traced here: 75.3 us
  Pallas kernels  42.7 us (56%)
  starting transfers between devices  27.4 us (36%)
  waiting for transfers between devices  3.32 us (4%)
  between operations  1.05 us (1%)
  local copies, waits for them, and re-layouts  0.84 us (1%)
    ppermute x12, starting transfers between devices, swaps(): lax.ppermute(value, axis, pairs + [(j, i) for i, j in pairs])  27.4 us
    pallas_call x1, Pallas kernels, inner_rows(): pl.pallas_call(kernel, in_specs=[SMEM] * 3 + [VM] * 8, out_specs=[VM] * 4...  10.1 us
    pallas_call x1, Pallas kernels, first_sweep(): pl.pallas_call(kernel, in_specs=[SMEM, VM, VM, SMEM] + [HBM] * 3 + [SMEM]...  9.27 us
    pallas_call x1, Pallas kernels, inner_second(): pl.pallas_call(kernel, in_specs=[SMEM] + [VM] * 5 + [HBM], out_specs=[VM]...  6.54 us
    pallas_call x2, Pallas kernels, edge_second(): pl.pallas_call(kernel, in_specs=[SMEM] * 4 + [VM] * (6 + len(kept)), out_...  5.02 us
    pallas_call x1, Pallas kernels, edge_final(): pl.pallas_call(kernel, in_specs=[SMEM] * 5 + [VM] * 6, out_specs=[VM] * 7...  3.69 us
    ppermute x12, waiting for transfers between devices, swaps(): lax.ppermute(value, axis, pairs + [(j, i) for i, j in pairs])  3.32 us
    pallas_call x1, Pallas kernels, coarse_split(): pl.pallas_call(kernel, in_specs=[SMEM] * 3 + [VM] * 6 + [HBM], out_specs=...  3.08 us
  transfers between devices with their start and end apart: 12, of which 2 were waited for; matrix products, arithmetic and copies ran while one was open for 0% of the time, Pallas kernels for 48%

profile of v2, /device:TPU:0, one launch (start us, length us, event | category | flops | bytes accessed | tf_op | source)
XLA Modules:
  0.0 75.3 jit_solution(15161579649559339301)
XLA Ops:
  0.0 3.0 %collective-permute-start.4 = (bf16[8,128,128]{2,1,0:T(8,128)(2,1)}, bf16[8,128,128]{2,1,0:T(8,128)(2,1)S(1)}, u32[]{:S(2)}, u32[]{:S(2)}) collective-permute-start(bf16[8,128,128]{2,1,0:T(8,128)(2,1)} %own.1), channel_id=1, source_target_pairs={{0,1},{2,3},{1,0},{3,2},{4,5},{6,7},{5,4},{7,6},{8,9},{10,11},{9,8... | collective-permute-start | bytes 786440 | tf_op jit(solution)/shard_map/ppermute | solution.py:622
  3.0 0.7 collective-permute-start.3
  3.7 0.1 pad_add_fusion.pos_ref
  3.8 0.0 copy-start.2
  3.8 0.7 copy-done.2
  4.4 0.0 copy-start.4
  4.4 2.8 %edge_smooth.1 = (s32[1]{0:T(128)}, bf16[8,128,128]{2,1,0:T(8,128)(2,1)S(1)}, bf16[8,128,128]{2,1,0:T(8,128)(2,1)S(1)}, bf16[8,128,128]{2,1,0:T(8,128)(2,1)S(1)}, bf16[8,128,128]{2,1,0:T(8,128)(2,1)S(1)}) custom-call(s32[3]{0:T(128)S(1)} %pad_add_fusion.pos_ref, s32[1,32]{1,0:T(1,128)S(1)} %copy-done.2, bf16[64,128,128]{2,1,0:T(8,128)(2,1)} %b_hbm.3, ...), custom_call_target="tpu_custom_call" | custom-call | flops 4294967296 | bytes 1572864 | tf_op jit(solution)/shard_map/edge_smooth/pallas_call | solution.py:84
  7.3 0.0 copy-start
  7.3 0.0 copy-start.1
  7.3 0.0 copy-start.3
  8.0 0.0 copy-done.4
  8.0 0.2 conditional.1
  8.0 0.2 broadcast.2
  8.2 0.7 collective-permute-start.5
  8.9 5.7 %collective-permute-start.6 = (bf16[8,128,128]{2,1,0:T(8,128)(2,1)S(1)}, bf16[8,128,128]{2,1,0:T(8,128)(2,1)S(1)}, u32[]{:S(2)}, u32[]{:S(2)}) collective-permute-start(bf16[8,128,128]{2,1,0:T(8,128)(2,1)S(1)} %get-tuple-element.60), channel_id=1, source_target_pairs={{0,1},{2,3},{4,5},{6,7},{8,9},{10,11},{12,13},{14,15},{16,17},{18,... | collective-permute-start | bytes 786440 | tf_op jit(solution)/shard_map/ppermute | solution.py:622
  14.6 0.7 collective-permute-start.7
  15.2 0.0 collective-permute-done.4.by_even
  15.2 3.3 %collective-permute-start.8 = (bf16[8,128,128]{2,1,0:T(8,128)(2,1)S(1)}, bf16[8,128,128]{2,1,0:T(8,128)(2,1)S(1)}, u32[]{:S(2)}, u32[]{:S(2)}) collective-permute-start(bf16[8,128,128]{2,1,0:T(8,128)(2,1)S(1)} %get-tuple-element.68), channel_id=1, source_target_pairs={{0,1},{2,3},{4,5},{6,7},{8,9},{10,11},{12,13},{14,15},{16,17},{18,... | collective-permute-start | bytes 786440 | tf_op jit(solution)/shard_map/ppermute | solution.py:622
  18.6 0.0 collective-permute-done.3.by_odd
  18.6 0.0 copy-done
  18.6 0.0 copy-done.1
  18.6 0.0 copy-done.3
  18.6 9.3 %first_sweep.1 = (bf16[64,128,128]{2,1,0:T(8,128)(2,1)S(1)}, bf16[64,128,128]{2,1,0:T(8,128)(2,1)S(1)}, bf16[32,8,128,128]{3,2,1,0:T(8,128)(2,1)S(1)}, bf16[32,1...) custom-call(s32[3]{0:T(128)S(1)} %pad_add_fusion.pos_ref, ...), custom_call_target="tpu_custom_call" | custom-call | flops 68719476736 | bytes 16777216 | tf_op jit(solution)/shard_map/first_sweep/pallas_call | solution.py:235
  27.9 0.0 collective-permute-done.5.rest_0_
  27.9 0.0 collective-permute-done.6.rest_1_
  27.9 2.1 %edge_second_inner.1 = (f32[32,128,128]{2,1,0:T(8,128)S(1)}, f32[64,128,128]{2,1,0:T(8,128)S(1)}, bf16[65,128,128]{2,1,0:T(8,128)(2,1)S(1)}, bf16[33,128,128]{2,...) custom-call(s32[3]{0:T(128)S(1)} %pad_add_fusion.pos_ref, ...), custom_call_target="tpu_custom_call", output_to_operand_aliasing={{0}: (4, {}), {1}: (5, {})} | custom-call | flops 8589934592 | bytes 8388608 | tf_op jit(solution)/shard_map/edge_second_inner/pallas_call | solution.py:329
  30.0 0.7 collective-permute-start.11
  30.7 3.3 %collective-permute-start.12 = (bf16[8,128,128]{2,1,0:T(8,128)(2,1)S(1)}, bf16[8,128,128]{2,1,0:T(8,128)(2,1)S(1)}, u32[]{:S(2)}, u32[]{:S(2)}) collective-permute-start(bf16[8,128,128]{2,1,0:T(8,128)(2,1)S(1)} %get-tuple-element.81), channel_id=1, source_target_pairs={{0,1},{2,3},{4,5},{6,7},{8,9},{10,11},{12,13},{14,15},{16,17},{18,... | collective-permute-start | bytes 786440 | tf_op jit(solution)/shard_map/ppermute | solution.py:622
  34.0 0.0 collective-permute-done.7.rest_2_
  34.0 3.1 %collective-permute-done.8.rest_3_ = bf16[8,128,128]{2,1,0:T(8,128)(2,1)S(1)} collective-permute-done((bf16[8,128,128]{2,1,0:T(8,128)(2,1)S(1)}, bf16[8,128,128]{2,1,0:T(8,128)(2,1)S(1)}, u32[]{:S(2)}, u32[]{:S(2)}) %collective-permute-start.8) | collective-permute-done | bytes 262176 | tf_op jit(solution)/shard_map/ppermute | solution.py:622
  37.1 2.9 %edge_second_outer.1 = (f32[32,128,128]{2,1,0:T(8,128)S(1)}, f32[64,128,128]{2,1,0:T(8,128)S(1)}, bf16[65,128,128]{2,1,0:T(8,128)(2,1)S(1)}, bf16[33,128,128]{2,...) custom-call(s32[3]{0:T(128)S(1)} %pad_add_fusion.pos_ref, ...), custom_call_target="tpu_custom_call", output_to_operand_aliasing={{0}: (4, {}), {1}: (5, {}), {2}: (6, {}), {3}: (7, {})} | custom-call | flops 8589934592 | bytes 8388608 | tf_op jit(solution)/shard_map/edge_second_outer/pallas_call | solution.py:329
  40.0 1.4 %collective-permute-start.9 = (bf16[8,128,128]{2,1,0:T(8,128)(2,1)}, bf16[8,128,128]{2,1,0:T(8,128)(2,1)}, u32[]{:S(2)}, u32[]{:S(2)}) collective-permute-start(bf16[8,128,128]{2,1,0:T(8,128)(2,1)} %get-tuple-element.69), channel_id=1, source_target_pairs={{1,2},{3,4},{5,6},{7,8},{9,10},{11,12},{13,14},{15,16},{17,18},{19... | collective-permute-start | bytes 786440 | tf_op jit(solution)/shard_map/ppermute | solution.py:622
  41.4 1.4 %collective-permute-start.10 = (bf16[8,128,128]{2,1,0:T(8,128)(2,1)}, bf16[8,128,128]{2,1,0:T(8,128)(2,1)}, u32[]{:S(2)}, u32[]{:S(2)}) collective-permute-start(bf16[8,128,128]{2,1,0:T(8,128)(2,1)} %get-tuple-element.70), channel_id=1, source_target_pairs={{0,1},{2,3},{4,5},{6,7},{8,9},{10,11},{12,13},{14,15},{16,17},{18,... | collective-permute-start | bytes 786440 | tf_op jit(solution)/shard_map/ppermute | solution.py:622
  42.8 6.5 %inner_second.1 = (bf16[65,128,128]{2,1,0:T(8,128)(2,1)S(1)}, f32[64,128,128]{2,1,0:T(8,128)S(1)}, bf16[32,8,128,128]{3,2,1,0:T(8,128)(2,1)S(1)}) custom-call(s32[8,64]{1,0:T(8,128)S(1)} %get-tuple-element.71.lcol_ref, bf16[64,128,128]{2,1,0:T(8,128)(2,1)S(1)} %get-tuple-element.72.b, ...), custom_call_target="tpu_custom_call", output_to_operand_aliasing={{0}: (4, {}), {1}: (5, {})} | custom-call | tf_op jit(solution)/shard_map/inner_second/pallas_call | solution.py:396
  49.4 0.0 collective-permute-done.11.from_odd
  49.4 0.0 collective-permute-done.12.from_even
  49.4 10.1 %inner_rows.1 = (bf16[64,128,128]{2,1,0:T(8,128)(2,1)S(1)}, f32[32,128,128]{2,1,0:T(8,128)S(1)}, f32[64,128,128]{2,1,0:T(8,128)S(1)}, bf16[33,128,128]{2,1,0:T(8,128)(2,1)S(1)}, f32[64,128,128]{2,1,0:T(8,128)}) custom-call(s32[3]{0:T(128)S(1)} %pad_add_fusion.pos_ref, s32[8,64]{1,0:T(8,128)S(1)} %get-tuple-element.71.lcol_ref, ...), custom_call_target="tpu_custom_call", output_to_operand_aliasing={{2}: (8, {})} | custom-call | flops 137438953472 | bytes 8388608 | tf_op jit(solution)/shard_map/inner_rows/pallas_call | solution.py:467
  59.5 0.0 collective-permute-done.9.from_odd
  59.5 0.2 collective-permute-done.10.from_even
  59.6 3.7 %edge_final.1 = (bf16[64,128,128]{2,1,0:T(8,128)(2,1)S(1)}, f32[32,128,128]{2,1,0:T(8,128)S(1)}, bf16[33,128,128]{2,1,0:T(8,128)(2,1)S(1)}, bf16[128,128]{1,0:T(...) custom-call(s32[3]{0:T(128)S(1)} %pad_add_fusion.pos_ref, ...), custom_call_target="tpu_custom_call", output_to_operand_aliasing={{0}: (10, {}), {1}: (8, {}), {2}: (7, {})} | custom-call | flops 4294967296 | bytes 8388608 | tf_op jit(solution)/shard_map/edge_final/pallas_call | solution.py:512
  63.3 0.7 collective-permute-start.13
  64.0 5.9 %collective-permute-start.14 = (bf16[128,128]{1,0:T(8,128)(2,1)S(1)}, bf16[128,128]{1,0:T(8,128)(2,1)S(1)}, u32[]{:S(2)}, u32[]{:S(2)}) collective-permute-start(bf16[128,128]{1,0:T(8,128)(2,1)S(1)} %get-tuple-element.88), channel_id=1, source_target_pairs={{0,1},{2,3},{1,0},{3,2},{4,5},{6,7},{5,4},{7,6},{8,9},{10,11},{9,8... | collective-permute-start | bytes 98312 | tf_op jit(solution)/shard_map/ppermute | solution.py:622
  69.9 2.2 %coarse_own.1.s2_in = f32[64,128,128]{2,1,0:T(8,128)S(1)} custom-call(s32[33]{0:T(128)S(1)} %get-tuple-element.52.bd, s32[6]{0:T(128)S(1)} %get-tuple-element.53.trim, bf16[64,128,128]{2,1,0:T(8,128)(2,1)S(1)} %get-tuple-element.89.r2_ref, f32[64,128,128]{2,1,0:T(8,128)S(1)} %get-tuple-element.90.s2_in, ...), custom_call_target="tpu_custom_call", output_to_operand_aliasing={{}: (3, {})} | custom-call | flops 2147483648 | bytes 5242880 | tf_op jit(solution)/shard_map/coarse_own/pallas_call | solution.py:548
  72.1 0.0 collective-permute-done.13.by_odd
  72.1 0.0 collective-permute-done.14.by_even
  72.1 3.1 %coarse_split.1 = (f32[64,128,128]{2,1,0:T(8,128)S(1)}, f32[64,128,128]{2,1,0:T(8,128)}) custom-call(s32[3]{0:T(128)S(1)} %pad_add_fusion.pos_ref, s32[33]{0:T(128)S(1)} %get-tuple-element.52.bd, s32[6]{0:T(128)S(1)} %get-tuple-element.53.trim, bf16[128,128]{1,0:T(8,128)(2,1)S(1)} %get-tuple-element.85.first_ref, ...), custom_call_target="tpu_custom_call", output_to_operand_aliasing={{0}: (7, {}), {1}: (9, {})} | custom-call | flops 268435456 | bytes 1048576 | tf_op jit(solution)/shard_map/coarse_split/pallas_call | solution.py:601
Async XLA Ops:
  0.0 15.2 %collective-permute-start.4 = (bf16[8,128,128]{2,1,0:T(8,128)(2,1)}, bf16[8,128,128]{2,1,0:T(8,128)(2,1)S(1)}, u32[]{:S(2)}, u32[]{:S(2)}) collective-permute-start(bf16[8,128,128]{2,1,0:T(8,128)(2,1)} %own.1), channel_id=1, source_target_pairs={{0,1},{2,3},{1,0},{3,2},{4,5},{6,7},{5,4},{7,6},{8,9},{10,11},{9,8... | collective-permute-start | bytes 786440 | tf_op jit(solution)/shard_map/ppermute | solution.py:622
  3.0 15.6 %collective-permute-start.3 = (bf16[8,128,128]{2,1,0:T(8,128)(2,1)}, bf16[8,128,128]{2,1,0:T(8,128)(2,1)S(1)}, u32[]{:S(2)}, u32[]{:S(2)}) collective-permute-start(bf16[8,128,128]{2,1,0:T(8,128)(2,1)} %own.1), channel_id=1, source_target_pairs={{1,2},{2,1},{5,6},{6,5},{9,10},{10,9},{13,14},{14,13},{17,18},{18,... | collective-permute-start | bytes 786440 | tf_op jit(solution)/shard_map/ppermute | solution.py:622
  3.8 0.7 copy-start.2
  4.4 3.5 %copy-start.4 = (bf16[8,128,128]{2,1,0:T(8,128)(2,1)S(1)}, bf16[8,128,128]{2,1,0:T(8,128)(2,1)}, u32[]{:S(2)}) copy-start(bf16[8,128,128]{2,1,0:T(8,128)(2,1)} %own.1) | copy-start | bytes 786436
  7.3 11.3 %copy-start = (s32[64,8]{0,1:T(8,128)S(1)}, s32[64,8]{0,1:T(8,128)}, u32[]{:S(2)}) copy-start(s32[64,8]{0,1:T(8,128)} %param.11) | copy-start | bytes 6148
  7.3 11.3 %copy-start.1 = (s32[64]{0:T(128)S(1)}, s32[64]{0:T(128)}, u32[]{:S(2)}) copy-start(s32[64]{0:T(128)} %param.12) | copy-start | bytes 772
  7.3 11.3 %copy-start.3 = (s32[1,32]{1,0:T(1,128)S(1)}, s32[1,32]{1,0:T(1,128)}, u32[]{:S(2)}) copy-start(s32[1,32]{1,0:T(1,128)} %size_ref.3) | copy-start | bytes 388
  8.2 19.7 %collective-permute-start.5 = (bf16[8,128,128]{2,1,0:T(8,128)(2,1)S(1)}, bf16[8,128,128]{2,1,0:T(8,128)(2,1)S(1)}, u32[]{:S(2)}, u32[]{:S(2)}) collective-permute-start(bf16[8,128,128]{2,1,0:T(8,128)(2,1)S(1)} %get-tuple-element.59), channel_id=1, source_target_pairs={{1,2},{3,4},{5,6},{7,8},{9,10},{11,12},{13,14},{15,16},{17,18},{19... | collective-permute-start | bytes 786440 | tf_op jit(solution)/shard_map/ppermute | solution.py:622
  8.9 19.0 %collective-permute-start.6 = (bf16[8,128,128]{2,1,0:T(8,128)(2,1)S(1)}, bf16[8,128,128]{2,1,0:T(8,128)(2,1)S(1)}, u32[]{:S(2)}, u32[]{:S(2)}) collective-permute-start(bf16[8,128,128]{2,1,0:T(8,128)(2,1)S(1)} %get-tuple-element.60), channel_id=1, source_target_pairs={{0,1},{2,3},{4,5},{6,7},{8,9},{10,11},{12,13},{14,15},{16,17},{18,... | collective-permute-start | bytes 786440 | tf_op jit(solution)/shard_map/ppermute | solution.py:622
  14.6 19.5 %collective-permute-start.7 = (bf16[8,128,128]{2,1,0:T(8,128)(2,1)S(1)}, bf16[8,128,128]{2,1,0:T(8,128)(2,1)S(1)}, u32[]{:S(2)}, u32[]{:S(2)}) collective-permute-start(bf16[8,128,128]{2,1,0:T(8,128)(2,1)S(1)} %get-tuple-element.67), channel_id=1, source_target_pairs={{1,2},{3,4},{5,6},{7,8},{9,10},{11,12},{13,14},{15,16},{17,18},{19... | collective-permute-start | bytes 786440 | tf_op jit(solution)/shard_map/ppermute | solution.py:622
  15.2 21.9 %collective-permute-start.8 = (bf16[8,128,128]{2,1,0:T(8,128)(2,1)S(1)}, bf16[8,128,128]{2,1,0:T(8,128)(2,1)S(1)}, u32[]{:S(2)}, u32[]{:S(2)}) collective-permute-start(bf16[8,128,128]{2,1,0:T(8,128)(2,1)S(1)} %get-tuple-element.68), channel_id=1, source_target_pairs={{0,1},{2,3},{4,5},{6,7},{8,9},{10,11},{12,13},{14,15},{16,17},{18,... | collective-permute-start | bytes 786440 | tf_op jit(solution)/shard_map/ppermute | solution.py:622
  30.0 19.3 %collective-permute-start.11 = (bf16[8,128,128]{2,1,0:T(8,128)(2,1)S(1)}, bf16[8,128,128]{2,1,0:T(8,128)(2,1)S(1)}, u32[]{:S(2)}, u32[]{:S(2)}) collective-permute-start(bf16[8,128,128]{2,1,0:T(8,128)(2,1)S(1)} %get-tuple-element.80), channel_id=1, source_target_pairs={{1,2},{3,4},{5,6},{7,8},{9,10},{11,12},{13,14},{15,16},{17,18},{19... | collective-permute-start | bytes 786440 | tf_op jit(solution)/shard_map/ppermute | solution.py:622
  30.7 18.7 %collective-permute-start.12 = (bf16[8,128,128]{2,1,0:T(8,128)(2,1)S(1)}, bf16[8,128,128]{2,1,0:T(8,128)(2,1)S(1)}, u32[]{:S(2)}, u32[]{:S(2)}) collective-permute-start(bf16[8,128,128]{2,1,0:T(8,128)(2,1)S(1)} %get-tuple-element.81), channel_id=1, source_target_pairs={{0,1},{2,3},{4,5},{6,7},{8,9},{10,11},{12,13},{14,15},{16,17},{18,... | collective-permute-start | bytes 786440 | tf_op jit(solution)/shard_map/ppermute | solution.py:622
  40.0 19.4 %collective-permute-start.9 = (bf16[8,128,128]{2,1,0:T(8,128)(2,1)}, bf16[8,128,128]{2,1,0:T(8,128)(2,1)}, u32[]{:S(2)}, u32[]{:S(2)}) collective-permute-start(bf16[8,128,128]{2,1,0:T(8,128)(2,1)} %get-tuple-element.69), channel_id=1, source_target_pairs={{1,2},{3,4},{5,6},{7,8},{9,10},{11,12},{13,14},{15,16},{17,18},{19... | collective-permute-start | bytes 786440 | tf_op jit(solution)/shard_map/ppermute | solution.py:622
  41.4 18.2 %collective-permute-start.10 = (bf16[8,128,128]{2,1,0:T(8,128)(2,1)}, bf16[8,128,128]{2,1,0:T(8,128)(2,1)}, u32[]{:S(2)}, u32[]{:S(2)}) collective-permute-start(bf16[8,128,128]{2,1,0:T(8,128)(2,1)} %get-tuple-element.70), channel_id=1, source_target_pairs={{0,1},{2,3},{4,5},{6,7},{8,9},{10,11},{12,13},{14,15},{16,17},{18,... | collective-permute-start | bytes 786440 | tf_op jit(solution)/shard_map/ppermute | solution.py:622
  63.3 8.7 %collective-permute-start.13 = (bf16[128,128]{1,0:T(8,128)(2,1)S(1)}, bf16[128,128]{1,0:T(8,128)(2,1)S(1)}, u32[]{:S(2)}, u32[]{:S(2)}) collective-permute-start(bf16[128,128]{1,0:T(8,128)(2,1)S(1)} %get-tuple-element.87), channel_id=1, source_target_pairs={{1,2},{2,1},{5,6},{6,5},{9,10},{10,9},{13,14},{14,13},{17,18},{18,... | collective-permute-start | bytes 98312 | tf_op jit(solution)/shard_map/ppermute | solution.py:622
  64.0 8.1 %collective-permute-start.14 = (bf16[128,128]{1,0:T(8,128)(2,1)S(1)}, bf16[128,128]{1,0:T(8,128)(2,1)S(1)}, u32[]{:S(2)}, u32[]{:S(2)}) collective-permute-start(bf16[128,128]{1,0:T(8,128)(2,1)S(1)} %get-tuple-element.88), channel_id=1, source_target_pairs={{0,1},{2,3},{1,0},{3,2},{4,5},{6,7},{5,4},{7,6},{8,9},{10,11},{9,8... | collective-permute-start | bytes 98312 | tf_op jit(solution)/shard_map/ppermute | solution.py:622

commit v3 on v2

--- a/solution.py
+++ b/solution.py
@@ -49,11 +49,10 @@
         self.H = HALO
 
 
-def edge_smooth(p, pos, sizes, rhs, smoother):
+def edge_smooth(p, pos, rhs, smoother):
     step = p.H // 2
-    share = p.A // p.G
-
-    def kernel(pos_ref, size_ref, b_hbm, s_hbm, apart, *rest):
+
+    def kernel(pos_ref, b_hbm, s_hbm, *rest):
         outs, (b, s, sems) = rest[:4], rest[4:]
         odd = pos_ref[2]
         starts = []
@@ -66,14 +65,6 @@
         for c in copies:
             c.start()
 
-        def reach(a, t):
-            begin, most = t
-            end = begin + size_ref[0, a]
-            owner = a // share
-            here = jnp.maximum(lax.div(end - 1, p.R) - owner, owner - lax.div(begin, p.R))
-            return end, jnp.maximum(most, here)
-
-        apart[0] = lax.fori_loop(0, p.A, reach, (jnp.int32(0), jnp.int32(0)))[1]
         for c in range(4):
             copies[2 * c].wait()
             copies[2 * c + 1].wait()
@@ -83,9 +74,9 @@
     out = jax.ShapeDtypeStruct((step, p.BS, p.N), BF16)
     return pl.pallas_call(
         kernel,
-        in_specs=[SMEM, SMEM, HBM, HBM],
-        out_specs=[SMEM] + [VM] * 4,
-        out_shape=[jax.ShapeDtypeStruct((1,), I32)] + [out] * 4,
+        in_specs=[SMEM, HBM, HBM],
+        out_specs=[VM] * 4,
+        out_shape=[out] * 4,
         scratch_shapes=[
             pltpu.VMEM((4, step, p.BS, p.N), BF16),
             pltpu.VMEM((4, step, p.BS, p.BS), BF16),
@@ -94,7 +85,7 @@
         compiler_params=params(8),
         cost_estimate=cost(4 * p.H * p.BS * p.BS * p.N, 6 * p.H * p.BS * p.N),
         name="edge_smooth",
-    )(pos, sizes, far(rhs), far(smoother))
+    )(pos, far(rhs), far(smoother))
 
 
 def end_row(p, r):
@@ -108,7 +99,7 @@
 
 
 def first_sweep(p, pos, cols, counts, sizes, rhs, smoother, blocks, apart, inverses):
-    piece = 8
+    piece = p.H // 2
     share = p.A // p.G
     pieces = p.R // piece
     end_pieces = 2 * p.H // piece
@@ -201,7 +192,8 @@
 
         for c in range(end_pieces):
             block_copy(c).wait()
-            lax.fori_loop(c * piece, (c + 1) * piece, edge_row, 0, unroll=4)
+            if c not in (0, end_pieces - 1):
+                lax.fori_loop(c * piece, (c + 1) * piece, edge_row, 0, unroll=8)
 
         place_all(lambda c: c.wait())
 
@@ -261,7 +253,31 @@
 
 
 GROUP = 4
-WIDE = 4
+NARROW, WIDE = 4, 6
+
+
+def outer_local(p, lcol, rhs, blocks, ext, acc):
+    step = p.H // 2
+
+    def kernel(lcol_ref, b, blk, ext_ref, acc_in, acc_ref):
+        def edge_row(r, c):
+            i = end_row(p, r)
+            acc_ref[r] = b[i].astype(F32) - row_product(p, blk, r, i, ext_ref, lcol_ref)
+            return c
+
+        lax.fori_loop(0, step, edge_row, 0, unroll=8)
+        lax.fori_loop(2 * p.H - step, 2 * p.H, edge_row, 0, unroll=8)
+
+    return pl.pallas_call(
+        kernel,
+        in_specs=[SMEM] + [VM] * 4,
+        out_specs=VM,
+        out_shape=pltpu.VMEM((2 * p.H, p.BS, p.N), F32),
+        input_output_aliases={4: 0},
+        compiler_params=params(8),
+        cost_estimate=cost(0, 0),
+        name="outer_local",
+    )(lcol, near(rhs), near(blocks), near(ext), near(acc))
 
 
 def halo_product(hslot, hcol, blk, r, i, slots, halo):
@@ -270,13 +286,13 @@
     return mm(lhs, rhs)
 
 
-def take_rest(p, hslot, hcol, hn, blk, halo, acc, rows):
+def take_rest(p, hslot, hcol, hn, blk, halo, acc, rows, taken):
     def row(r, c):
         i = end_row(p, r)
 
-        @pl.when(hn[0, i] > WIDE)
+        @pl.when(hn[0, i] > taken)
         def _():
-            acc[r] = acc[r] - halo_product(hslot, hcol, blk, r, i, range(WIDE, p.K), halo)
+            acc[r] = acc[r] - halo_product(hslot, hcol, blk, r, i, range(taken, p.K), halo)
 
         return c
 
@@ -294,6 +310,7 @@
     step = p.H // 2
     halves = ((0, step), (2 * p.H - step, 2 * p.H)) if outer else ((step, p.H), (p.H, p.H + step))
     before, after = (0, 2 * p.H - step) if outer else (step, p.H)
+    taken = min(p.K, WIDE if outer else NARROW)
 
     def kernel(pos_ref, hs, hc, hn_ref, acc_in, s2_in, *rest):
         from_odd, from_even, sm, blk = rest[-12:-8]
@@ -303,12 +320,12 @@
         if not outer:
             halo_ref[2 * p.H] = jnp.zeros((p.BS, p.N), BF16)
             ext_out[p.R] = jnp.zeros((p.BS, p.N), BF16)
-        take_rest(p, hs, hc, hn_ref, blk, halo_ref, acc_ref, halves)
+        take_rest(p, hs, hc, hn_ref, blk, halo_ref, acc_ref, halves, taken)
         for first, last in halves:
 
             def residual(r, c):
                 i = end_row(p, r)
-                res[r] = (acc_ref[r] - halo_product(hs, hc, blk, r, i, range(WIDE), halo_ref)).astype(BF16)
+                res[r] = (acc_ref[r] - halo_product(hs, hc, blk, r, i, range(taken), halo_ref)).astype(BF16)
                 return c
 
             lax.fori_loop(first, last, residual, 0, unroll=8)
@@ -372,7 +389,7 @@
 
 
 def inner_second(p, lcol, rhs, smoother, ext1, ext2, s2, blocks):
-    piece = 4
+    piece = 8
     inner = p.R - 2 * p.H
 
     def kernel(lcol_ref, b, sm, ext1_ref, ext_in, s2_ref, blk_hbm, ext, s2_out, blk, blk_sems):
@@ -424,7 +441,7 @@
             r2[i] = (b[i].astype(F32) - row_product(p, blk, r, i, ext, lcol_ref)).astype(BF16)
             return c
 
-        lax.fori_loop(0, inner, inner_row, 0, unroll=4)
+        lax.fori_loop(0, inner, inner_row, 0, unroll=8)
 
         def copy(r):
             return pltpu.make_async_copy(s2_out.at[r], out.at[r], row_sems.at[r])
@@ -457,7 +474,7 @@
             acc[r] = b[i].astype(F32) - row_product(p, end_blk, r, i, ext, lcol_ref)
             return c
 
-        lax.fori_loop(0, 2 * p.H, edge_row, 0, unroll=4)
+        lax.fori_loop(0, 2 * p.H, edge_row, 0, unroll=8)
 
         def settle(a, first, last):
             lax.fori_loop(first, last, wait, 0)
@@ -492,14 +509,18 @@
         r2_out, acc_ref, halo, part_first, part_last, to_odd, to_even, both = rest
         put_halo(p, pos_ref[2], halo, from_odd, from_even, step, p.H)
         halo[2 * p.H] = jnp.zeros((p.BS, p.N), BF16)
-        take_rest(p, hs, hc, hn_ref, blk, halo, acc_ref, ((0, 2 * p.H),))
-
-        def row(r, c):
-            i = end_row(p, r)
-            r2_out[i] = (acc_ref[r] - halo_product(hs, hc, blk, r, i, range(WIDE), halo)).astype(BF16)
-            return c
-
-        lax.fori_loop(0, 2 * p.H, row, 0, unroll=8)
+        inner = ((step, 2 * p.H - step),)
+        outer = ((0, step), (2 * p.H - step, 2 * p.H))
+        for rows, taken in ((inner, min(p.K, NARROW)), (outer, min(p.K, WIDE))):
+            take_rest(p, hs, hc, hn_ref, blk, halo, acc_ref, rows, taken)
+            for first, last in rows:
+
+                def row(r, c):
+                    i = end_row(p, r)
+                    r2_out[i] = (acc_ref[r] - halo_product(hs, hc, blk, r, i, range(taken), halo)).astype(BF16)
+                    return c
+
+                lax.fori_loop(first, last, row, 0, unroll=8)
         both[0] = aggregate_sum(p, r2_out, 0, trim[0]).astype(BF16)
         both[1] = aggregate_sum(p, r2_out, trim[1], p.R).astype(BF16)
         part_first[...] = both[0]
@@ -565,16 +586,6 @@
         bef = jnp.where(odd, by_even[...].astype(F32), by_odd[...].astype(F32))
         aft = jnp.where(odd, by_odd[...].astype(F32), by_even[...].astype(F32))
 
-        @pl.when(trim[2] > 0)
-        def _():
-            res = (bef + first_ref[...].astype(F32)).astype(BF16)
-            add_fix(inv_ref[trim[4]], res, s2_ref, 0, trim[0])
-
-        @pl.when(trim[3] > 0)
-        def _():
-            res = (last_ref[...].astype(F32) + aft).astype(BF16)
-            add_fix(inv_ref[trim[5]], res, s2_ref, trim[1], p.R)
-
         def inner(a, t):
             begin, end = t
             first, last = bd[a], bd[a + 1]
@@ -582,6 +593,8 @@
             return jnp.where(sent, jnp.minimum(begin, first), begin), jnp.where(sent, last, end)
 
         begin, end = lax.fori_loop(0, p.A, inner, (jnp.int32(p.R), jnp.int32(p.R)))
+        head = jnp.where(trim[2] > 0, trim[0], 0)
+        tail = jnp.where(trim[3] > 0, trim[1], p.R)
 
         def copy(r):
             return pltpu.make_async_copy(s2_ref.at[r], out_ref.at[r], row_sems.at[r])
@@ -594,9 +607,23 @@
             copy(r).wait()
             return c
 
-        for step in (send, wait):
-            lax.fori_loop(0, begin, step, 0)
-            lax.fori_loop(end, p.R, step, 0)
+        lax.fori_loop(head, jnp.minimum(begin, tail), send, 0)
+        lax.fori_loop(end, tail, send, 0)
+
+        @pl.when(trim[2] > 0)
+        def _():
+            res = (bef + first_ref[...].astype(F32)).astype(BF16)
+            add_fix(inv_ref[trim[4]], res, s2_ref, 0, head)
+            lax.fori_loop(0, head, send, 0)
+
+        @pl.when(trim[3] > 0)
+        def _():
+            res = (last_ref[...].astype(F32) + aft).astype(BF16)
+            add_fix(inv_ref[trim[5]], res, s2_ref, tail, p.R)
+            lax.fori_loop(tail, p.R, send, 0)
+
+        lax.fori_loop(0, begin, wait, 0)
+        lax.fori_loop(end, p.R, wait, 0)
 
     return pl.pallas_call(
         kernel,
@@ -632,7 +659,7 @@
 
     swap_odd, swap_even = swaps(AXES, 1), swaps(AXES, 0)
 
-    apart, *out1 = edge_smooth(p, pos, agg_sizes, load_rhs, smoother)
+    out1 = edge_smooth(p, pos, load_rhs, smoother)
     inner1 = swap_odd(out1[0]), swap_even(out1[1])
     outer1 = swap_odd(out1[2]), swap_even(out1[3])
 
@@ -643,6 +670,12 @@
     def none(own):
         return jnp.zeros((group - 1,) + own.shape, own.dtype)
 
+    sizes, _ = lax.optimization_barrier((agg_sizes, out1[0]))
+    ids = jnp.arange(p.A, dtype=I32)
+    ends = jnp.sum(jnp.where(ids[None, :] <= ids[:, None], sizes, 0), axis=1)
+    owner = ids // (p.A // group)
+    reach = jnp.maximum((ends - 1) // rows - owner, owner - (ends - sizes[0]) // rows)
+    apart = jnp.max(reach)[None]
     distant = lax.cond(apart[0] > 1, every, none, coarse_inv)
     inverses = coarse_inv, swaps("agg", 1)(coarse_inv), swaps("agg", 0)(coarse_inv), distant
     rhs, smoother, end_blocks, inv, s2, ext1, acc1, lcol, hslot, hcol, hn, bounds, trims = first_sweep(
@@ -652,6 +685,7 @@
         p, False, pos, hslot, hcol, hn, inner1, acc1, smoother, end_blocks, s2
     )
     inner2 = swap_odd(out2[0]), swap_even(out2[1])
+    acc1 = outer_local(p, lcol, rhs, end_blocks, ext1, acc1)
     _, s2, ext2, _, *out2 = edge_second(
         p, True, pos, hslot, hcol, hn, outer1, acc1, smoother, end_blocks, s2, ext2, halo
     )

time: 76.1 us -> 74.5 us (0.979)
  starting transfers between devices: 27.4 us -> 25.1 us
  waiting for transfers between devices: 3.32 us -> 5.09 us
  Pallas kernels: 42.7 us -> 41.7 us
    ppermute x12, starting transfers between devices: 27.4 us -> 25.1 us  [swaps(): lax.ppermute(value, axis, pairs + [(j, i) for i, j in pairs])]
    ppermute x12, waiting for transfers between devices: 3.32 us -> 5.09 us  [swaps(): lax.ppermute(value, axis, pairs + [(j, i) for i, j in pairs])]
    pallas_call x1 -> x2, Pallas kernels: 2.83 us -> 4.4 us  [the longest x1 2.54 us: edge_smooth(): pl.pallas_call(kernel, in_specs=[SMEM, HBM, HBM], out_specs=[VM] * 4, out...]
    pallas_call x1, Pallas kernels: 9.27 us -> 7.79 us  [first_sweep(): pl.pallas_call(kernel, in_specs=[SMEM, VM, VM, SMEM] + [HBM] * 3 + [SMEM]...]
    pallas_call x1, Pallas kernels: 10.1 us -> 8.94 us  [inner_rows(): pl.pallas_call(kernel, in_specs=[SMEM] * 3 + [VM] * 8, out_specs=[VM] * 4...]
  transfers between devices with their start and end apart: 12 -> 12, of which waited for: 2 -> 3; matrix products, arithmetic and copies ran while one was open for 0% -> 1% of each run, Pallas kernels for 48% -> 47%
where the time goes in v3:
time: 74.5 us; the launch traced here: 74 us
  Pallas kernels  41.7 us (56%)
  starting transfers between devices  25.1 us (34%)
  waiting for transfers between devices  5.09 us (7%)
  between operations  1.05 us (1%)
  other arithmetic  0.84 us (1%)
    ppermute x12, starting transfers between devices, swaps(): lax.ppermute(value, axis, pairs + [(j, i) for i, j in pairs])  25.1 us
    pallas_call x1, Pallas kernels, inner_rows(): pl.pallas_call(kernel, in_specs=[SMEM] * 3 + [VM] * 8, out_specs=[VM] * 4...  8.94 us
    pallas_call x1, Pallas kernels, first_sweep(): pl.pallas_call(kernel, in_specs=[SMEM, VM, VM, SMEM] + [HBM] * 3 + [SMEM]...  7.79 us
    pallas_call x1, Pallas kernels, inner_second(): pl.pallas_call(kernel, in_specs=[SMEM] + [VM] * 5 + [HBM], out_specs=[VM]...  5.81 us
    pallas_call x2, Pallas kernels, edge_second(): pl.pallas_call(kernel, in_specs=[SMEM] * 4 + [VM] * (6 + len(kept)), out_...  5.37 us
    ppermute x12, waiting for transfers between devices, swaps(): lax.ppermute(value, axis, pairs + [(j, i) for i, j in pairs])  5.09 us
    pallas_call x1, Pallas kernels, edge_final(): pl.pallas_call(kernel, in_specs=[SMEM] * 5 + [VM] * 6, out_specs=[VM] * 7...  3.72 us
    pallas_call x1, Pallas kernels, coarse_split(): pl.pallas_call(kernel, in_specs=[SMEM] * 3 + [VM] * 6 + [HBM], out_specs=...  3 us
  transfers between devices with their start and end apart: 12, of which 3 were waited for; matrix products, arithmetic and copies ran while one was open for 1% of the time, Pallas kernels for 47%

profile of v3, /device:TPU:0, one launch (start us, length us, event | category | flops | bytes accessed | tf_op | source)
XLA Modules:
  0.0 74.0 jit_solution(18301746057424933794)
XLA Ops:
  0.0 3.0 %collective-permute-start.4 = (bf16[8,128,128]{2,1,0:T(8,128)(2,1)}, bf16[8,128,128]{2,1,0:T(8,128)(2,1)S(1)}, u32[]{:S(2)}, u32[]{:S(2)}) collective-permute-start(bf16[8,128,128]{2,1,0:T(8,128)(2,1)} %own.1), channel_id=1, source_target_pairs={{0,1},{2,3},{1,0},{3,2},{4,5},{6,7},{5,4},{7,6},{8,9},{10,11},{9,8... | collective-permute-start | bytes 786440 | tf_op jit(solution)/shard_map/ppermute | solution.py:649
  3.0 0.7 collective-permute-start.3
  3.7 0.1 pad_add_fusion.pos_ref
  3.8 0.0 copy-start.2
  3.8 0.0 copy-start.5
  3.8 2.5 %edge_smooth.1 = (bf16[8,128,128]{2,1,0:T(8,128)(2,1)S(1)}, bf16[8,128,128]{2,1,0:T(8,128)(2,1)S(1)}, bf16[8,128,128]{2,1,0:T(8,128)(2,1)S(1)}, bf16[8,128,128]{2,1,0:T(8,128)(2,1)S(1)}) custom-call(s32[3]{0:T(128)S(1)} %pad_add_fusion.pos_ref, bf16[64,128,128]{2,1,0:T(8,128)(2,1)} %b_hbm.3, bf16[64,128,128]{2,1,0:T(8,128)(2,1)} %sm_hbm.1), custom_call_target="tpu_custom_call" | custom-call | flops 4294967296 | bytes 1572864 | tf_op jit(solution)/shard_map/edge_smooth/pallas_call | solution.py:75
  6.3 0.0 copy-start
  6.3 0.0 copy-start.1
  6.4 0.0 copy-done.2
  6.4 0.1 select_reduce_fusion
  6.5 0.7 maximum_reduce_fusion
  7.8 0.0 copy-done.5
  7.8 0.2 conditional.1
  7.8 0.2 broadcast.22
  8.0 0.7 collective-permute-start.5
  8.7 5.7 %collective-permute-start.6 = (bf16[8,128,128]{2,1,0:T(8,128)(2,1)S(1)}, bf16[8,128,128]{2,1,0:T(8,128)(2,1)S(1)}, u32[]{:S(2)}, u32[]{:S(2)}) collective-permute-start(bf16[8,128,128]{2,1,0:T(8,128)(2,1)S(1)} %get-tuple-element.64), channel_id=1, source_target_pairs={{0,1},{2,3},{4,5},{6,7},{8,9},{10,11},{12,13},{14,15},{16,17},{18,... | collective-permute-start | bytes 786440 | tf_op jit(solution)/shard_map/ppermute | solution.py:649
  14.4 0.7 collective-permute-start.7
  15.0 0.0 collective-permute-done.4.by_even
  15.0 3.3 %collective-permute-start.8 = (bf16[8,128,128]{2,1,0:T(8,128)(2,1)S(1)}, bf16[8,128,128]{2,1,0:T(8,128)(2,1)S(1)}, u32[]{:S(2)}, u32[]{:S(2)}) collective-permute-start(bf16[8,128,128]{2,1,0:T(8,128)(2,1)S(1)} %get-tuple-element.71), channel_id=1, source_target_pairs={{0,1},{2,3},{4,5},{6,7},{8,9},{10,11},{12,13},{14,15},{16,17},{18,... | collective-permute-start | bytes 786440 | tf_op jit(solution)/shard_map/ppermute | solution.py:649
  18.4 0.0 collective-permute-done.3.by_odd
  18.4 0.0 copy-done
  18.4 0.0 copy-done.1
  18.4 7.8 %first_sweep.1 = (bf16[64,128,128]{2,1,0:T(8,128)(2,1)S(1)}, bf16[64,128,128]{2,1,0:T(8,128)(2,1)S(1)}, bf16[32,8,128,128]{3,2,1,0:T(8,128)(2,1)S(1)}, bf16[32,1...) custom-call(s32[3]{0:T(128)S(1)} %pad_add_fusion.pos_ref, ...), custom_call_target="tpu_custom_call" | custom-call | flops 68719476736 | bytes 16777216 | tf_op jit(solution)/shard_map/first_sweep/pallas_call | solution.py:227
  26.2 0.0 copy-start.3
  26.2 0.7 collective-permute-done.6.rest_1_
  26.9 0.0 collective-permute-done.5.rest_0_
  26.9 2.1 %edge_second_inner.1 = (f32[32,128,128]{2,1,0:T(8,128)S(1)}, f32[64,128,128]{2,1,0:T(8,128)S(1)}, bf16[65,128,128]{2,1,0:T(8,128)(2,1)S(1)}, bf16[33,128,128]{2,...) custom-call(s32[3]{0:T(128)S(1)} %pad_add_fusion.pos_ref, ...), custom_call_target="tpu_custom_call", output_to_operand_aliasing={{0}: (4, {}), {1}: (5, {})} | custom-call | flops 8589934592 | bytes 8388608 | tf_op jit(solution)/shard_map/edge_second_inner/pallas_call | solution.py:346
  29.1 0.7 collective-permute-start.11
  29.8 2.6 %collective-permute-start.12 = (bf16[8,128,128]{2,1,0:T(8,128)(2,1)S(1)}, bf16[8,128,128]{2,1,0:T(8,128)(2,1)S(1)}, u32[]{:S(2)}, u32[]{:S(2)}) collective-permute-start(bf16[8,128,128]{2,1,0:T(8,128)(2,1)S(1)} %get-tuple-element.81), channel_id=1, source_target_pairs={{0,1},{2,3},{4,5},{6,7},{8,9},{10,11},{12,13},{14,15},{16,17},{18,... | collective-permute-start | bytes 786440 | tf_op jit(solution)/shard_map/ppermute | solution.py:649
  32.4 1.9 %outer_local.1.acc_in = f32[32,128,128]{2,1,0:T(8,128)S(1)} custom-call(s32[8,64]{1,0:T(8,128)S(1)} %get-tuple-element.58.lcol_ref, bf16[64,128,128]{2,1,0:T(8,128)(2,1)S(1)} %get-tuple-element.59.b, bf16[32,8,128,128]{3,2,1,0:T(8,128)(2,1)S(1)} %get-tuple-element.60.rest_3_.blk.rest_5_.end_blk, ...), custom_call_target="tpu_custom_call", output_to_operand_aliasing={{}: (4, {})} | custom-call | tf_op jit(solution)/shard_map/outer_local/pallas_call | solution.py:271
  34.2 0.0 collective-permute-done.7.rest_2_
  34.2 3.3 %collective-permute-done.8.rest_3_ = bf16[8,128,128]{2,1,0:T(8,128)(2,1)S(1)} collective-permute-done((bf16[8,128,128]{2,1,0:T(8,128)(2,1)S(1)}, bf16[8,128,128]{2,1,0:T(8,128)(2,1)S(1)}, u32[]{:S(2)}, u32[]{:S(2)}) %collective-permute-start.8) | collective-permute-done | bytes 262176 | tf_op jit(solution)/shard_map/ppermute | solution.py:649
  37.5 0.0 copy-done.3
  37.5 3.2 %edge_second_outer.1 = (f32[32,128,128]{2,1,0:T(8,128)S(1)}, f32[64,128,128]{2,1,0:T(8,128)S(1)}, bf16[65,128,128]{2,1,0:T(8,128)(2,1)S(1)}, bf16[33,128,128]{2,...) custom-call(s32[3]{0:T(128)S(1)} %pad_add_fusion.pos_ref, ...), custom_call_target="tpu_custom_call", output_to_operand_aliasing={{0}: (4, {}), {1}: (5, {}), {2}: (6, {}), {3}: (7, {})} | custom-call | flops 8589934592 | bytes 8388608 | tf_op jit(solution)/shard_map/edge_second_outer/pallas_call | solution.py:346
  40.8 1.4 %collective-permute-start.9 = (bf16[8,128,128]{2,1,0:T(8,128)(2,1)}, bf16[8,128,128]{2,1,0:T(8,128)(2,1)}, u32[]{:S(2)}, u32[]{:S(2)}) collective-permute-start(bf16[8,128,128]{2,1,0:T(8,128)(2,1)} %get-tuple-element.72), channel_id=1, source_target_pairs={{1,2},{3,4},{5,6},{7,8},{9,10},{11,12},{13,14},{15,16},{17,18},{19... | collective-permute-start | bytes 786440 | tf_op jit(solution)/shard_map/ppermute | solution.py:649
  42.2 1.4 %collective-permute-start.10 = (bf16[8,128,128]{2,1,0:T(8,128)(2,1)}, bf16[8,128,128]{2,1,0:T(8,128)(2,1)}, u32[]{:S(2)}, u32[]{:S(2)}) collective-permute-start(bf16[8,128,128]{2,1,0:T(8,128)(2,1)} %get-tuple-element.73), channel_id=1, source_target_pairs={{0,1},{2,3},{4,5},{6,7},{8,9},{10,11},{12,13},{14,15},{16,17},{18,... | collective-permute-start | bytes 786440 | tf_op jit(solution)/shard_map/ppermute | solution.py:649
  43.6 5.8 %inner_second.1 = (bf16[65,128,128]{2,1,0:T(8,128)(2,1)S(1)}, f32[64,128,128]{2,1,0:T(8,128)S(1)}, bf16[32,8,128,128]{3,2,1,0:T(8,128)(2,1)S(1)}) custom-call(s32[8,64]{1,0:T(8,128)S(1)} %get-tuple-element.58.lcol_ref, bf16[64,128,128]{2,1,0:T(8,128)(2,1)S(1)} %get-tuple-element.59.b, ...), custom_call_target="tpu_custom_call", output_to_operand_aliasing={{0}: (4, {}), {1}: (5, {})} | custom-call | tf_op jit(solution)/shard_map/inner_second/pallas_call | solution.py:413
  49.4 0.0 collective-permute-done.11.from_odd
  49.4 0.0 collective-permute-done.12.from_even
  49.4 0.0 copy-start.4
  49.4 8.9 %inner_rows.1 = (bf16[64,128,128]{2,1,0:T(8,128)(2,1)S(1)}, f32[32,128,128]{2,1,0:T(8,128)S(1)}, f32[64,128,128]{2,1,0:T(8,128)S(1)}, bf16[33,128,128]{2,1,0:T(8,128)(2,1)S(1)}, f32[64,128,128]{2,1,0:T(8,128)}) custom-call(s32[3]{0:T(128)S(1)} %pad_add_fusion.pos_ref, s32[8,64]{1,0:T(8,128)S(1)} %get-tuple-element.58.lcol_ref, ...), custom_call_target="tpu_custom_call", output_to_operand_aliasing={{2}: (8, {})} | custom-call | flops 137438953472 | bytes 8388608 | tf_op jit(solution)/shard_map/inner_rows/pallas_call | solution.py:484
  58.4 0.0 collective-permute-done.9.from_odd
  58.4 1.0 %collective-permute-done.10.from_even = bf16[8,128,128]{2,1,0:T(8,128)(2,1)} collective-permute-done((bf16[8,128,128]{2,1,0:T(8,128)(2,1)}, bf16[8,128,128]{2,1,0:T(8,128)(2,1)}, u32[]{:S(2)}, u32[]{:S(2)}) %collective-permute-start.10) | collective-permute-done | bytes 262176 | tf_op jit(solution)/shard_map/ppermute | solution.py:649
  59.4 0.0 copy-done.4
  59.4 3.7 %edge_final.1 = (bf16[64,128,128]{2,1,0:T(8,128)(2,1)S(1)}, f32[32,128,128]{2,1,0:T(8,128)S(1)}, bf16[33,128,128]{2,1,0:T(8,128)(2,1)S(1)}, bf16[128,128]{1,0:T(...) custom-call(s32[3]{0:T(128)S(1)} %pad_add_fusion.pos_ref, ...), custom_call_target="tpu_custom_call", output_to_operand_aliasing={{0}: (10, {}), {1}: (8, {}), {2}: (7, {})} | custom-call | flops 4294967296 | bytes 8388608 | tf_op jit(solution)/shard_map/edge_final/pallas_call | solution.py:533
  63.2 0.7 collective-permute-start.13
  63.8 4.3 %collective-permute-start.14 = (bf16[128,128]{1,0:T(8,128)(2,1)S(1)}, bf16[128,128]{1,0:T(8,128)(2,1)S(1)}, u32[]{:S(2)}, u32[]{:S(2)}) collective-permute-start(bf16[128,128]{1,0:T(8,128)(2,1)S(1)} %get-tuple-element.88), channel_id=1, source_target_pairs={{0,1},{2,3},{1,0},{3,2},{4,5},{6,7},{5,4},{7,6},{8,9},{10,11},{9,8... | collective-permute-start | bytes 98312 | tf_op jit(solution)/shard_map/ppermute | solution.py:649
  68.1 2.7 %coarse_own.1.s2_in = f32[64,128,128]{2,1,0:T(8,128)S(1)} custom-call(s32[33]{0:T(128)S(1)} %get-tuple-element.53.bd, s32[6]{0:T(128)S(1)} %get-tuple-element.54.trim, bf16[64,128,128]{2,1,0:T(8,128)(2,1)S(1)} %get-tuple-element.89.r2_ref, f32[64,128,128]{2,1,0:T(8,128)S(1)} %get-tuple-element.90.s2_in, ...), custom_call_target="tpu_custom_call", output_to_operand_aliasing={{}: (3, {})} | custom-call | flops 2147483648 | bytes 5242880 | tf_op jit(solution)/shard_map/coarse_own/pallas_call | solution.py:569
  70.8 0.0 collective-permute-done.13.by_odd
  70.8 0.0 collective-permute-done.14.by_even
  70.8 3.0 %coarse_split.1 = (f32[64,128,128]{2,1,0:T(8,128)S(1)}, f32[64,128,128]{2,1,0:T(8,128)}) custom-call(s32[3]{0:T(128)S(1)} %pad_add_fusion.pos_ref, s32[33]{0:T(128)S(1)} %get-tuple-element.53.bd, s32[6]{0:T(128)S(1)} %get-tuple-element.54.trim, bf16[128,128]{1,0:T(8,128)(2,1)S(1)} %get-tuple-element.85.first_ref, ...), custom_call_target="tpu_custom_call", output_to_operand_aliasing={{0}: (7, {}), {1}: (9, {})} | custom-call | flops 268435456 | bytes 1048576 | tf_op jit(solution)/shard_map/coarse_split/pallas_call | solution.py:628
Async XLA Ops:
  0.0 15.0 %collective-permute-start.4 = (bf16[8,128,128]{2,1,0:T(8,128)(2,1)}, bf16[8,128,128]{2,1,0:T(8,128)(2,1)S(1)}, u32[]{:S(2)}, u32[]{:S(2)}) collective-permute-start(bf16[8,128,128]{2,1,0:T(8,128)(2,1)} %own.1), channel_id=1, source_target_pairs={{0,1},{2,3},{1,0},{3,2},{4,5},{6,7},{5,4},{7,6},{8,9},{10,11},{9,8... | collective-permute-start | bytes 786440 | tf_op jit(solution)/shard_map/ppermute | solution.py:649
  3.0 15.4 %collective-permute-start.3 = (bf16[8,128,128]{2,1,0:T(8,128)(2,1)}, bf16[8,128,128]{2,1,0:T(8,128)(2,1)S(1)}, u32[]{:S(2)}, u32[]{:S(2)}) collective-permute-start(bf16[8,128,128]{2,1,0:T(8,128)(2,1)} %own.1), channel_id=1, source_target_pairs={{1,2},{2,1},{5,6},{6,5},{9,10},{10,9},{13,14},{14,13},{17,18},{18,... | collective-permute-start | bytes 786440 | tf_op jit(solution)/shard_map/ppermute | solution.py:649
  3.8 2.6 %copy-start.2 = (s32[1,32]{1,0:T(1,128)S(1)}, s32[1,32]{1,0:T(1,128)}, u32[]{:S(2)}) copy-start(s32[1,32]{1,0:T(1,128)} %size_ref.1) | copy-start | bytes 388
  3.8 4.0 %copy-start.5 = (bf16[8,128,128]{2,1,0:T(8,128)(2,1)S(1)}, bf16[8,128,128]{2,1,0:T(8,128)(2,1)}, u32[]{:S(2)}) copy-start(bf16[8,128,128]{2,1,0:T(8,128)(2,1)} %own.1) | copy-start | bytes 786436
  6.3 12.1 %copy-start = (s32[64,8]{0,1:T(8,128)S(1)}, s32[64,8]{0,1:T(8,128)}, u32[]{:S(2)}) copy-start(s32[64,8]{0,1:T(8,128)} %param.11) | copy-start | bytes 6148
  6.3 12.0 %copy-start.1 = (s32[64]{0:T(128)S(1)}, s32[64]{0:T(128)}, u32[]{:S(2)}) copy-start(s32[64]{0:T(128)} %param.12) | copy-start | bytes 772
  8.0 18.9 %collective-permute-start.5 = (bf16[8,128,128]{2,1,0:T(8,128)(2,1)S(1)}, bf16[8,128,128]{2,1,0:T(8,128)(2,1)S(1)}, u32[]{:S(2)}, u32[]{:S(2)}) collective-permute-start(bf16[8,128,128]{2,1,0:T(8,128)(2,1)S(1)} %get-tuple-element.51), channel_id=1, source_target_pairs={{1,2},{3,4},{5,6},{7,8},{9,10},{11,12},{13,14},{15,16},{17,18},{19... | collective-permute-start | bytes 786440 | tf_op jit(solution)/shard_map/ppermute | solution.py:649
  8.7 18.3 %collective-permute-start.6 = (bf16[8,128,128]{2,1,0:T(8,128)(2,1)S(1)}, bf16[8,128,128]{2,1,0:T(8,128)(2,1)S(1)}, u32[]{:S(2)}, u32[]{:S(2)}) collective-permute-start(bf16[8,128,128]{2,1,0:T(8,128)(2,1)S(1)} %get-tuple-element.64), channel_id=1, source_target_pairs={{0,1},{2,3},{4,5},{6,7},{8,9},{10,11},{12,13},{14,15},{16,17},{18,... | collective-permute-start | bytes 786440 | tf_op jit(solution)/shard_map/ppermute | solution.py:649
  14.4 19.9 %collective-permute-start.7 = (bf16[8,128,128]{2,1,0:T(8,128)(2,1)S(1)}, bf16[8,128,128]{2,1,0:T(8,128)(2,1)S(1)}, u32[]{:S(2)}, u32[]{:S(2)}) collective-permute-start(bf16[8,128,128]{2,1,0:T(8,128)(2,1)S(1)} %get-tuple-element.70), channel_id=1, source_target_pairs={{1,2},{3,4},{5,6},{7,8},{9,10},{11,12},{13,14},{15,16},{17,18},{19... | collective-permute-start | bytes 786440 | tf_op jit(solution)/shard_map/ppermute | solution.py:649
  15.0 22.5 %collective-permute-start.8 = (bf16[8,128,128]{2,1,0:T(8,128)(2,1)S(1)}, bf16[8,128,128]{2,1,0:T(8,128)(2,1)S(1)}, u32[]{:S(2)}, u32[]{:S(2)}) collective-permute-start(bf16[8,128,128]{2,1,0:T(8,128)(2,1)S(1)} %get-tuple-element.71), channel_id=1, source_target_pairs={{0,1},{2,3},{4,5},{6,7},{8,9},{10,11},{12,13},{14,15},{16,17},{18,... | collective-permute-start | bytes 786440 | tf_op jit(solution)/shard_map/ppermute | solution.py:649
  26.2 11.4 %copy-start.3 = (s32[8,64]{1,0:T(8,128)}, s32[8,64]{1,0:T(8,128)S(1)}, u32[]{:S(2)}) copy-start(s32[8,64]{1,0:T(8,128)S(1)} %get-tuple-element.57.hn_ref) | copy-start | bytes 6148
  29.1 20.3 %collective-permute-start.11 = (bf16[8,128,128]{2,1,0:T(8,128)(2,1)S(1)}, bf16[8,128,128]{2,1,0:T(8,128)(2,1)S(1)}, u32[]{:S(2)}, u32[]{:S(2)}) collective-permute-start(bf16[8,128,128]{2,1,0:T(8,128)(2,1)S(1)} %get-tuple-element.80), channel_id=1, source_target_pairs={{1,2},{3,4},{5,6},{7,8},{9,10},{11,12},{13,14},{15,16},{17,18},{19... | collective-permute-start | bytes 786440 | tf_op jit(solution)/shard_map/ppermute | solution.py:649
  29.8 19.7 %collective-permute-start.12 = (bf16[8,128,128]{2,1,0:T(8,128)(2,1)S(1)}, bf16[8,128,128]{2,1,0:T(8,128)(2,1)S(1)}, u32[]{:S(2)}, u32[]{:S(2)}) collective-permute-start(bf16[8,128,128]{2,1,0:T(8,128)(2,1)S(1)} %get-tuple-element.81), channel_id=1, source_target_pairs={{0,1},{2,3},{4,5},{6,7},{8,9},{10,11},{12,13},{14,15},{16,17},{18,... | collective-permute-start | bytes 786440 | tf_op jit(solution)/shard_map/ppermute | solution.py:649
  40.8 17.6 %collective-permute-start.9 = (bf16[8,128,128]{2,1,0:T(8,128)(2,1)}, bf16[8,128,128]{2,1,0:T(8,128)(2,1)}, u32[]{:S(2)}, u32[]{:S(2)}) collective-permute-start(bf16[8,128,128]{2,1,0:T(8,128)(2,1)} %get-tuple-element.72), channel_id=1, source_target_pairs={{1,2},{3,4},{5,6},{7,8},{9,10},{11,12},{13,14},{15,16},{17,18},{19... | collective-permute-start | bytes 786440 | tf_op jit(solution)/shard_map/ppermute | solution.py:649
  42.2 17.3 %collective-permute-start.10 = (bf16[8,128,128]{2,1,0:T(8,128)(2,1)}, bf16[8,128,128]{2,1,0:T(8,128)(2,1)}, u32[]{:S(2)}, u32[]{:S(2)}) collective-permute-start(bf16[8,128,128]{2,1,0:T(8,128)(2,1)} %get-tuple-element.73), channel_id=1, source_target_pairs={{0,1},{2,3},{4,5},{6,7},{8,9},{10,11},{12,13},{14,15},{16,17},{18,... | collective-permute-start | bytes 786440 | tf_op jit(solution)/shard_map/ppermute | solution.py:649
  49.4 10.0 %copy-start.4 = (s32[8,64]{1,0:T(8,128)S(1)}, s32[8,64]{1,0:T(8,128)}, u32[]{:S(2)}) copy-start(s32[8,64]{1,0:T(8,128)} %copy-done.3) | copy-start | bytes 6148
  63.2 7.6 %collective-permute-start.13 = (bf16[128,128]{1,0:T(8,128)(2,1)S(1)}, bf16[128,128]{1,0:T(8,128)(2,1)S(1)}, u32[]{:S(2)}, u32[]{:S(2)}) collective-permute-start(bf16[128,128]{1,0:T(8,128)(2,1)S(1)} %get-tuple-element.87), channel_id=1, source_target_pairs={{1,2},{2,1},{5,6},{6,5},{9,10},{10,9},{13,14},{14,13},{17,18},{18,... | collective-permute-start | bytes 98312 | tf_op jit(solution)/shard_map/ppermute | solution.py:649
  63.8 7.0 %collective-permute-start.14 = (bf16[128,128]{1,0:T(8,128)(2,1)S(1)}, bf16[128,128]{1,0:T(8,128)(2,1)S(1)}, u32[]{:S(2)}, u32[]{:S(2)}) collective-permute-start(bf16[128,128]{1,0:T(8,128)(2,1)S(1)} %get-tuple-element.88), channel_id=1, source_target_pairs={{0,1},{2,3},{1,0},{3,2},{4,5},{6,7},{5,4},{7,6},{8,9},{10,11},{9,8... | collective-permute-start | bytes 98312 | tf_op jit(solution)/shard_map/ppermute | solution.py:649

commit v4 on v3

--- a/solution.py
+++ b/solution.py
@@ -441,7 +441,7 @@
             r2[i] = (b[i].astype(F32) - row_product(p, blk, r, i, ext, lcol_ref)).astype(BF16)
             return c
 
-        lax.fori_loop(0, inner, inner_row, 0, unroll=8)
+        lax.fori_loop(0, inner, inner_row, 0, unroll=16)
 
         def copy(r):
             return pltpu.make_async_copy(s2_out.at[r], out.at[r], row_sems.at[r])
@@ -474,7 +474,7 @@
             acc[r] = b[i].astype(F32) - row_product(p, end_blk, r, i, ext, lcol_ref)
             return c
 
-        lax.fori_loop(0, 2 * p.H, edge_row, 0, unroll=8)
+        lax.fori_loop(0, 2 * p.H, edge_row, 0, unroll=16)
 
         def settle(a, first, last):
             lax.fori_loop(first, last, wait, 0)

time: 74.5 us -> 74.1 us (level)
  the two profiles are of different devices: /device:TPU:0 before, /device:TPU:1 now
where the time goes in v4:
time: 74.1 us; the launch traced here: 74 us
  Pallas kernels  41 us (55%)
  starting transfers between devices  26.8 us (36%)
  waiting for transfers between devices  4.01 us (5%)
  between operations  1.1 us (1%)
  other arithmetic  0.84 us (1%)
    ppermute x12, starting transfers between devices, swaps(): lax.ppermute(value, axis, pairs + [(j, i) for i, j in pairs])  26.8 us
    pallas_call x1, Pallas kernels, inner_rows(): pl.pallas_call(kernel, in_specs=[SMEM] * 3 + [VM] * 8, out_specs=[VM] * 4...  8 us
    pallas_call x1, Pallas kernels, first_sweep(): pl.pallas_call(kernel, in_specs=[SMEM, VM, VM, SMEM] + [HBM] * 3 + [SMEM]...  7.79 us
    pallas_call x1, Pallas kernels, inner_second(): pl.pallas_call(kernel, in_specs=[SMEM] + [VM] * 5 + [HBM], out_specs=[VM]...  5.81 us
    pallas_call x2, Pallas kernels, edge_second(): pl.pallas_call(kernel, in_specs=[SMEM] * 4 + [VM] * (6 + len(kept)), out_...  5.38 us
    ppermute x12, waiting for transfers between devices, swaps(): lax.ppermute(value, axis, pairs + [(j, i) for i, j in pairs])  4.01 us
    pallas_call x1, Pallas kernels, edge_final(): pl.pallas_call(kernel, in_specs=[SMEM] * 5 + [VM] * 6, out_specs=[VM] * 7...  3.57 us
    pallas_call x1, Pallas kernels, coarse_split(): pl.pallas_call(kernel, in_specs=[SMEM] * 3 + [VM] * 6 + [HBM], out_specs=...  3.23 us
  transfers between devices with their start and end apart: 12, of which 2 were waited for; matrix products, arithmetic and copies ran while one was open for 1% of the time, Pallas kernels for 46%

profile of v4, /device:TPU:1, one launch (start us, length us, event | category | flops | bytes accessed | tf_op | source)
XLA Modules:
  0.0 74.0 jit_solution(1959123406830340782)
XLA Ops:
  0.0 2.1 %collective-permute-start.4 = (bf16[8,128,128]{2,1,0:T(8,128)(2,1)}, bf16[8,128,128]{2,1,0:T(8,128)(2,1)S(1)}, u32[]{:S(2)}, u32[]{:S(2)}) collective-permute-start(bf16[8,128,128]{2,1,0:T(8,128)(2,1)} %own.1), channel_id=1, source_target_pairs={{0,1},{2,3},{1,0},{3,2},{4,5},{6,7},{5,4},{7,6},{8,9},{10,11},{9,8... | collective-permute-start | bytes 786440 | tf_op jit(solution)/shard_map/ppermute | solution.py:649
  2.1 0.7 collective-permute-start.3
  2.8 0.1 pad_add_fusion.pos_ref
  2.9 0.0 copy-start.2
  2.9 0.0 copy-start.5
  2.9 2.5 %edge_smooth.1 = (bf16[8,128,128]{2,1,0:T(8,128)(2,1)S(1)}, bf16[8,128,128]{2,1,0:T(8,128)(2,1)S(1)}, bf16[8,128,128]{2,1,0:T(8,128)(2,1)S(1)}, bf16[8,128,128]{2,1,0:T(8,128)(2,1)S(1)}) custom-call(s32[3]{0:T(128)S(1)} %pad_add_fusion.pos_ref, bf16[64,128,128]{2,1,0:T(8,128)(2,1)} %b_hbm.3, bf16[64,128,128]{2,1,0:T(8,128)(2,1)} %sm_hbm.1), custom_call_target="tpu_custom_call" | custom-call | flops 4294967296 | bytes 1572864 | tf_op jit(solution)/shard_map/edge_smooth/pallas_call | solution.py:75
  5.4 0.0 copy-start
  5.4 0.0 copy-start.1
  5.5 0.0 copy-done.2
  5.5 0.1 select_reduce_fusion
  5.6 0.7 maximum_reduce_fusion
  6.9 0.0 copy-done.5
  6.9 0.2 conditional.1
  6.9 0.2 broadcast.22
  7.1 4.9 %collective-permute-start.5 = (bf16[8,128,128]{2,1,0:T(8,128)(2,1)S(1)}, bf16[8,128,128]{2,1,0:T(8,128)(2,1)S(1)}, u32[]{:S(2)}, u32[]{:S(2)}) collective-permute-start(bf16[8,128,128]{2,1,0:T(8,128)(2,1)S(1)} %get-tuple-element.51), channel_id=1, source_target_pairs={{1,2},{3,4},{5,6},{7,8},{9,10},{11,12},{13,14},{15,16},{17,18},{19... | collective-permute-start | bytes 786440 | tf_op jit(solution)/shard_map/ppermute | solution.py:649
  12.0 0.9 %collective-permute-start.6 = (bf16[8,128,128]{2,1,0:T(8,128)(2,1)S(1)}, bf16[8,128,128]{2,1,0:T(8,128)(2,1)S(1)}, u32[]{:S(2)}, u32[]{:S(2)}) collective-permute-start(bf16[8,128,128]{2,1,0:T(8,128)(2,1)S(1)} %get-tuple-element.64), channel_id=1, source_target_pairs={{0,1},{2,3},{4,5},{6,7},{8,9},{10,11},{12,13},{14,15},{16,17},{18,... | collective-permute-start | bytes 786440 | tf_op jit(solution)/shard_map/ppermute | solution.py:649
  12.9 5.9 %collective-permute-start.7 = (bf16[8,128,128]{2,1,0:T(8,128)(2,1)S(1)}, bf16[8,128,128]{2,1,0:T(8,128)(2,1)S(1)}, u32[]{:S(2)}, u32[]{:S(2)}) collective-permute-start(bf16[8,128,128]{2,1,0:T(8,128)(2,1)S(1)} %get-tuple-element.70), channel_id=1, source_target_pairs={{1,2},{3,4},{5,6},{7,8},{9,10},{11,12},{13,14},{15,16},{17,18},{19... | collective-permute-start | bytes 786440 | tf_op jit(solution)/shard_map/ppermute | solution.py:649
  18.8 0.0 collective-permute-done.4.by_even
  18.8 0.1 collective-permute-start.8
  18.9 0.0 collective-permute-done.3.by_odd
  18.9 0.0 copy-done
  18.9 0.0 copy-done.1
  19.0 7.8 %first_sweep.1 = (bf16[64,128,128]{2,1,0:T(8,128)(2,1)S(1)}, bf16[64,128,128]{2,1,0:T(8,128)(2,1)S(1)}, bf16[32,8,128,128]{3,2,1,0:T(8,128)(2,1)S(1)}, bf16[32,1...) custom-call(s32[3]{0:T(128)S(1)} %pad_add_fusion.pos_ref, ...), custom_call_target="tpu_custom_call" | custom-call | flops 68719476736 | bytes 16777216 | tf_op jit(solution)/shard_map/first_sweep/pallas_call | solution.py:227
  26.8 0.0 copy-start.3
  26.8 0.0 collective-permute-done.6.rest_1_
  26.8 0.0 collective-permute-done.5.rest_0_
  26.8 2.1 %edge_second_inner.1 = (f32[32,128,128]{2,1,0:T(8,128)S(1)}, f32[64,128,128]{2,1,0:T(8,128)S(1)}, bf16[65,128,128]{2,1,0:T(8,128)(2,1)S(1)}, bf16[33,128,128]{2,...) custom-call(s32[3]{0:T(128)S(1)} %pad_add_fusion.pos_ref, ...), custom_call_target="tpu_custom_call", output_to_operand_aliasing={{0}: (4, {}), {1}: (5, {})} | custom-call | flops 8589934592 | bytes 8388608 | tf_op jit(solution)/shard_map/edge_second_inner/pallas_call | solution.py:346
  28.9 1.9 %collective-permute-start.11 = (bf16[8,128,128]{2,1,0:T(8,128)(2,1)S(1)}, bf16[8,128,128]{2,1,0:T(8,128)(2,1)S(1)}, u32[]{:S(2)}, u32[]{:S(2)}) collective-permute-start(bf16[8,128,128]{2,1,0:T(8,128)(2,1)S(1)} %get-tuple-element.80), channel_id=1, source_target_pairs={{1,2},{3,4},{5,6},{7,8},{9,10},{11,12},{13,14},{15,16},{17,18},{19... | collective-permute-start | bytes 786440 | tf_op jit(solution)/shard_map/ppermute | solution.py:649
  30.9 2.1 %collective-permute-start.12 = (bf16[8,128,128]{2,1,0:T(8,128)(2,1)S(1)}, bf16[8,128,128]{2,1,0:T(8,128)(2,1)S(1)}, u32[]{:S(2)}, u32[]{:S(2)}) collective-permute-start(bf16[8,128,128]{2,1,0:T(8,128)(2,1)S(1)} %get-tuple-element.81), channel_id=1, source_target_pairs={{0,1},{2,3},{4,5},{6,7},{8,9},{10,11},{12,13},{14,15},{16,17},{18,... | collective-permute-start | bytes 786440 | tf_op jit(solution)/shard_map/ppermute | solution.py:649
  33.0 1.9 %outer_local.1.acc_in = f32[32,128,128]{2,1,0:T(8,128)S(1)} custom-call(s32[8,64]{1,0:T(8,128)S(1)} %get-tuple-element.58.lcol_ref, bf16[64,128,128]{2,1,0:T(8,128)(2,1)S(1)} %get-tuple-element.59.b, bf16[32,8,128,128]{3,2,1,0:T(8,128)(2,1)S(1)} %get-tuple-element.60.rest_3_.blk.rest_5_.end_blk, ...), custom_call_target="tpu_custom_call", output_to_operand_aliasing={{}: (4, {})} | custom-call | tf_op jit(solution)/shard_map/outer_local/pallas_call | solution.py:271
  34.9 0.0 collective-permute-done.7.rest_2_
  34.9 2.0 %collective-permute-done.8.rest_3_ = bf16[8,128,128]{2,1,0:T(8,128)(2,1)S(1)} collective-permute-done((bf16[8,128,128]{2,1,0:T(8,128)(2,1)S(1)}, bf16[8,128,128]{2,1,0:T(8,128)(2,1)S(1)}, u32[]{:S(2)}, u32[]{:S(2)}) %collective-permute-start.8) | collective-permute-done | bytes 262176 | tf_op jit(solution)/shard_map/ppermute | solution.py:649
  36.9 0.0 copy-done.3
  36.9 3.2 %edge_second_outer.1 = (f32[32,128,128]{2,1,0:T(8,128)S(1)}, f32[64,128,128]{2,1,0:T(8,128)S(1)}, bf16[65,128,128]{2,1,0:T(8,128)(2,1)S(1)}, bf16[33,128,128]{2,...) custom-call(s32[3]{0:T(128)S(1)} %pad_add_fusion.pos_ref, ...), custom_call_target="tpu_custom_call", output_to_operand_aliasing={{0}: (4, {}), {1}: (5, {}), {2}: (6, {}), {3}: (7, {})} | custom-call | flops 8589934592 | bytes 8388608 | tf_op jit(solution)/shard_map/edge_second_outer/pallas_call | solution.py:346
  40.2 2.1 %collective-permute-start.9 = (bf16[8,128,128]{2,1,0:T(8,128)(2,1)}, bf16[8,128,128]{2,1,0:T(8,128)(2,1)}, u32[]{:S(2)}, u32[]{:S(2)}) collective-permute-start(bf16[8,128,128]{2,1,0:T(8,128)(2,1)} %get-tuple-element.72), channel_id=1, source_target_pairs={{1,2},{3,4},{5,6},{7,8},{9,10},{11,12},{13,14},{15,16},{17,18},{19... | collective-permute-start | bytes 786440 | tf_op jit(solution)/shard_map/ppermute | solution.py:649
  42.3 1.0 %collective-permute-start.10 = (bf16[8,128,128]{2,1,0:T(8,128)(2,1)}, bf16[8,128,128]{2,1,0:T(8,128)(2,1)}, u32[]{:S(2)}, u32[]{:S(2)}) collective-permute-start(bf16[8,128,128]{2,1,0:T(8,128)(2,1)} %get-tuple-element.73), channel_id=1, source_target_pairs={{0,1},{2,3},{4,5},{6,7},{8,9},{10,11},{12,13},{14,15},{16,17},{18,... | collective-permute-start | bytes 786440 | tf_op jit(solution)/shard_map/ppermute | solution.py:649
  43.2 5.8 %inner_second.1 = (bf16[65,128,128]{2,1,0:T(8,128)(2,1)S(1)}, f32[64,128,128]{2,1,0:T(8,128)S(1)}, bf16[32,8,128,128]{3,2,1,0:T(8,128)(2,1)S(1)}) custom-call(s32[8,64]{1,0:T(8,128)S(1)} %get-tuple-element.58.lcol_ref, bf16[64,128,128]{2,1,0:T(8,128)(2,1)S(1)} %get-tuple-element.59.b, ...), custom_call_target="tpu_custom_call", output_to_operand_aliasing={{0}: (4, {}), {1}: (5, {})} | custom-call | tf_op jit(solution)/shard_map/inner_second/pallas_call | solution.py:413
  49.0 0.0 collective-permute-done.11.from_odd
  49.1 0.0 collective-permute-done.12.from_even
  49.1 0.0 copy-start.4
  49.1 8.0 %inner_rows.1 = (bf16[64,128,128]{2,1,0:T(8,128)(2,1)S(1)}, f32[32,128,128]{2,1,0:T(8,128)S(1)}, f32[64,128,128]{2,1,0:T(8,128)S(1)}, bf16[33,128,128]{2,1,0:T(8,128)(2,1)S(1)}, f32[64,128,128]{2,1,0:T(8,128)}) custom-call(s32[3]{0:T(128)S(1)} %pad_add_fusion.pos_ref, s32[8,64]{1,0:T(8,128)S(1)} %get-tuple-element.58.lcol_ref, ...), custom_call_target="tpu_custom_call", output_to_operand_aliasing={{2}: (8, {})} | custom-call | flops 137438953472 | bytes 8388608 | tf_op jit(solution)/shard_map/inner_rows/pallas_call | solution.py:484
  57.1 0.0 collective-permute-done.9.from_odd
  57.1 1.9 %collective-permute-done.10.from_even = bf16[8,128,128]{2,1,0:T(8,128)(2,1)} collective-permute-done((bf16[8,128,128]{2,1,0:T(8,128)(2,1)}, bf16[8,128,128]{2,1,0:T(8,128)(2,1)}, u32[]{:S(2)}, u32[]{:S(2)}) %collective-permute-start.10) | collective-permute-done | bytes 262176 | tf_op jit(solution)/shard_map/ppermute | solution.py:649
  59.0 0.0 copy-done.4
  59.0 3.6 %edge_final.1 = (bf16[64,128,128]{2,1,0:T(8,128)(2,1)S(1)}, f32[32,128,128]{2,1,0:T(8,128)S(1)}, bf16[33,128,128]{2,1,0:T(8,128)(2,1)S(1)}, bf16[128,128]{1,0:T(...) custom-call(s32[3]{0:T(128)S(1)} %pad_add_fusion.pos_ref, ...), custom_call_target="tpu_custom_call", output_to_operand_aliasing={{0}: (10, {}), {1}: (8, {}), {2}: (7, {})} | custom-call | flops 4294967296 | bytes 8388608 | tf_op jit(solution)/shard_map/edge_final/pallas_call | solution.py:533
  62.6 0.7 collective-permute-start.13
  63.3 4.4 %collective-permute-start.14 = (bf16[128,128]{1,0:T(8,128)(2,1)S(1)}, bf16[128,128]{1,0:T(8,128)(2,1)S(1)}, u32[]{:S(2)}, u32[]{:S(2)}) collective-permute-start(bf16[128,128]{1,0:T(8,128)(2,1)S(1)} %get-tuple-element.88), channel_id=1, source_target_pairs={{0,1},{2,3},{1,0},{3,2},{4,5},{6,7},{5,4},{7,6},{8,9},{10,11},{9,8... | collective-permute-start | bytes 98312 | tf_op jit(solution)/shard_map/ppermute | solution.py:649
  67.7 2.8 %coarse_own.1.s2_in = f32[64,128,128]{2,1,0:T(8,128)S(1)} custom-call(s32[33]{0:T(128)S(1)} %get-tuple-element.53.bd, s32[6]{0:T(128)S(1)} %get-tuple-element.54.trim, bf16[64,128,128]{2,1,0:T(8,128)(2,1)S(1)} %get-tuple-element.89.r2_ref, f32[64,128,128]{2,1,0:T(8,128)S(1)} %get-tuple-element.90.s2_in, ...), custom_call_target="tpu_custom_call", output_to_operand_aliasing={{}: (3, {})} | custom-call | flops 2147483648 | bytes 5242880 | tf_op jit(solution)/shard_map/coarse_own/pallas_call | solution.py:569
  70.5 0.0 collective-permute-done.13.by_odd
  70.6 0.0 collective-permute-done.14.by_even
  70.6 3.2 %coarse_split.1 = (f32[64,128,128]{2,1,0:T(8,128)S(1)}, f32[64,128,128]{2,1,0:T(8,128)}) custom-call(s32[3]{0:T(128)S(1)} %pad_add_fusion.pos_ref, s32[33]{0:T(128)S(1)} %get-tuple-element.53.bd, s32[6]{0:T(128)S(1)} %get-tuple-element.54.trim, bf16[128,128]{1,0:T(8,128)(2,1)S(1)} %get-tuple-element.85.first_ref, ...), custom_call_target="tpu_custom_call", output_to_operand_aliasing={{0}: (7, {}), {1}: (9, {})} | custom-call | flops 268435456 | bytes 1048576 | tf_op jit(solution)/shard_map/coarse_split/pallas_call | solution.py:628
Async XLA Ops:
  0.0 18.8 %collective-permute-start.4 = (bf16[8,128,128]{2,1,0:T(8,128)(2,1)}, bf16[8,128,128]{2,1,0:T(8,128)(2,1)S(1)}, u32[]{:S(2)}, u32[]{:S(2)}) collective-permute-start(bf16[8,128,128]{2,1,0:T(8,128)(2,1)} %own.1), channel_id=1, source_target_pairs={{0,1},{2,3},{1,0},{3,2},{4,5},{6,7},{5,4},{7,6},{8,9},{10,11},{9,8... | collective-permute-start | bytes 786440 | tf_op jit(solution)/shard_map/ppermute | solution.py:649
  2.1 16.8 %collective-permute-start.3 = (bf16[8,128,128]{2,1,0:T(8,128)(2,1)}, bf16[8,128,128]{2,1,0:T(8,128)(2,1)S(1)}, u32[]{:S(2)}, u32[]{:S(2)}) collective-permute-start(bf16[8,128,128]{2,1,0:T(8,128)(2,1)} %own.1), channel_id=1, source_target_pairs={{1,2},{2,1},{5,6},{6,5},{9,10},{10,9},{13,14},{14,13},{17,18},{18,... | collective-permute-start | bytes 786440 | tf_op jit(solution)/shard_map/ppermute | solution.py:649
  2.9 2.6 %copy-start.2 = (s32[1,32]{1,0:T(1,128)S(1)}, s32[1,32]{1,0:T(1,128)}, u32[]{:S(2)}) copy-start(s32[1,32]{1,0:T(1,128)} %size_ref.1) | copy-start | bytes 388
  2.9 4.0 %copy-start.5 = (bf16[8,128,128]{2,1,0:T(8,128)(2,1)S(1)}, bf16[8,128,128]{2,1,0:T(8,128)(2,1)}, u32[]{:S(2)}) copy-start(bf16[8,128,128]{2,1,0:T(8,128)(2,1)} %own.1) | copy-start | bytes 786436
  5.4 13.5 %copy-start = (s32[64,8]{0,1:T(8,128)S(1)}, s32[64,8]{0,1:T(8,128)}, u32[]{:S(2)}) copy-start(s32[64,8]{0,1:T(8,128)} %param.11) | copy-start | bytes 6148
  5.4 13.5 %copy-start.1 = (s32[64]{0:T(128)S(1)}, s32[64]{0:T(128)}, u32[]{:S(2)}) copy-start(s32[64]{0:T(128)} %param.12) | copy-start | bytes 772
  7.1 19.7 %collective-permute-start.5 = (bf16[8,128,128]{2,1,0:T(8,128)(2,1)S(1)}, bf16[8,128,128]{2,1,0:T(8,128)(2,1)S(1)}, u32[]{:S(2)}, u32[]{:S(2)}) collective-permute-start(bf16[8,128,128]{2,1,0:T(8,128)(2,1)S(1)} %get-tuple-element.51), channel_id=1, source_target_pairs={{1,2},{3,4},{5,6},{7,8},{9,10},{11,12},{13,14},{15,16},{17,18},{19... | collective-permute-start | bytes 786440 | tf_op jit(solution)/shard_map/ppermute | solution.py:649
  12.0 14.7 %collective-permute-start.6 = (bf16[8,128,128]{2,1,0:T(8,128)(2,1)S(1)}, bf16[8,128,128]{2,1,0:T(8,128)(2,1)S(1)}, u32[]{:S(2)}, u32[]{:S(2)}) collective-permute-start(bf16[8,128,128]{2,1,0:T(8,128)(2,1)S(1)} %get-tuple-element.64), channel_id=1, source_target_pairs={{0,1},{2,3},{4,5},{6,7},{8,9},{10,11},{12,13},{14,15},{16,17},{18,... | collective-permute-start | bytes 786440 | tf_op jit(solution)/shard_map/ppermute | solution.py:649
  12.9 22.0 %collective-permute-start.7 = (bf16[8,128,128]{2,1,0:T(8,128)(2,1)S(1)}, bf16[8,128,128]{2,1,0:T(8,128)(2,1)S(1)}, u32[]{:S(2)}, u32[]{:S(2)}) collective-permute-start(bf16[8,128,128]{2,1,0:T(8,128)(2,1)S(1)} %get-tuple-element.70), channel_id=1, source_target_pairs={{1,2},{3,4},{5,6},{7,8},{9,10},{11,12},{13,14},{15,16},{17,18},{19... | collective-permute-start | bytes 786440 | tf_op jit(solution)/shard_map/ppermute | solution.py:649
  18.8 18.1 %collective-permute-start.8 = (bf16[8,128,128]{2,1,0:T(8,128)(2,1)S(1)}, bf16[8,128,128]{2,1,0:T(8,128)(2,1)S(1)}, u32[]{:S(2)}, u32[]{:S(2)}) collective-permute-start(bf16[8,128,128]{2,1,0:T(8,128)(2,1)S(1)} %get-tuple-element.71), channel_id=1, source_target_pairs={{0,1},{2,3},{4,5},{6,7},{8,9},{10,11},{12,13},{14,15},{16,17},{18,... | collective-permute-start | bytes 786440 | tf_op jit(solution)/shard_map/ppermute | solution.py:649
  26.8 10.2 %copy-start.3 = (s32[8,64]{1,0:T(8,128)}, s32[8,64]{1,0:T(8,128)S(1)}, u32[]{:S(2)}) copy-start(s32[8,64]{1,0:T(8,128)S(1)} %get-tuple-element.57.hn_ref) | copy-start | bytes 6148
  28.9 20.1 %collective-permute-start.11 = (bf16[8,128,128]{2,1,0:T(8,128)(2,1)S(1)}, bf16[8,128,128]{2,1,0:T(8,128)(2,1)S(1)}, u32[]{:S(2)}, u32[]{:S(2)}) collective-permute-start(bf16[8,128,128]{2,1,0:T(8,128)(2,1)S(1)} %get-tuple-element.80), channel_id=1, source_target_pairs={{1,2},{3,4},{5,6},{7,8},{9,10},{11,12},{13,14},{15,16},{17,18},{19... | collective-permute-start | bytes 786440 | tf_op jit(solution)/shard_map/ppermute | solution.py:649
  30.9 18.2 %collective-permute-start.12 = (bf16[8,128,128]{2,1,0:T(8,128)(2,1)S(1)}, bf16[8,128,128]{2,1,0:T(8,128)(2,1)S(1)}, u32[]{:S(2)}, u32[]{:S(2)}) collective-permute-start(bf16[8,128,128]{2,1,0:T(8,128)(2,1)S(1)} %get-tuple-element.81), channel_id=1, source_target_pairs={{0,1},{2,3},{4,5},{6,7},{8,9},{10,11},{12,13},{14,15},{16,17},{18,... | collective-permute-start | bytes 786440 | tf_op jit(solution)/shard_map/ppermute | solution.py:649
  40.2 16.9 %collective-permute-start.9 = (bf16[8,128,128]{2,1,0:T(8,128)(2,1)}, bf16[8,128,128]{2,1,0:T(8,128)(2,1)}, u32[]{:S(2)}, u32[]{:S(2)}) collective-permute-start(bf16[8,128,128]{2,1,0:T(8,128)(2,1)} %get-tuple-element.72), channel_id=1, source_target_pairs={{1,2},{3,4},{5,6},{7,8},{9,10},{11,12},{13,14},{15,16},{17,18},{19... | collective-permute-start | bytes 786440 | tf_op jit(solution)/shard_map/ppermute | solution.py:649
  42.3 16.8 %collective-permute-start.10 = (bf16[8,128,128]{2,1,0:T(8,128)(2,1)}, bf16[8,128,128]{2,1,0:T(8,128)(2,1)}, u32[]{:S(2)}, u32[]{:S(2)}) collective-permute-start(bf16[8,128,128]{2,1,0:T(8,128)(2,1)} %get-tuple-element.73), channel_id=1, source_target_pairs={{0,1},{2,3},{4,5},{6,7},{8,9},{10,11},{12,13},{14,15},{16,17},{18,... | collective-permute-start | bytes 786440 | tf_op jit(solution)/shard_map/ppermute | solution.py:649
  49.1 10.0 %copy-start.4 = (s32[8,64]{1,0:T(8,128)S(1)}, s32[8,64]{1,0:T(8,128)}, u32[]{:S(2)}) copy-start(s32[8,64]{1,0:T(8,128)} %copy-done.3) | copy-start | bytes 6148
  62.6 7.9 %collective-permute-start.13 = (bf16[128,128]{1,0:T(8,128)(2,1)S(1)}, bf16[128,128]{1,0:T(8,128)(2,1)S(1)}, u32[]{:S(2)}, u32[]{:S(2)}) collective-permute-start(bf16[128,128]{1,0:T(8,128)(2,1)S(1)} %get-tuple-element.87), channel_id=1, source_target_pairs={{1,2},{2,1},{5,6},{6,5},{9,10},{10,9},{13,14},{14,13},{17,18},{18,... | collective-permute-start | bytes 98312 | tf_op jit(solution)/shard_map/ppermute | solution.py:649
  63.3 7.3 %collective-permute-start.14 = (bf16[128,128]{1,0:T(8,128)(2,1)S(1)}, bf16[128,128]{1,0:T(8,128)(2,1)S(1)}, u32[]{:S(2)}, u32[]{:S(2)}) collective-permute-start(bf16[128,128]{1,0:T(8,128)(2,1)S(1)} %get-tuple-element.88), channel_id=1, source_target_pairs={{0,1},{2,3},{1,0},{3,2},{4,5},{6,7},{5,4},{7,6},{8,9},{10,11},{9,8... | collective-permute-start | bytes 98312 | tf_op jit(solution)/shard_map/ppermute | solution.py:649
